TPU v7x, 32 devices: a whole 2x2x4 slice. The times are simulated.
32 devices in a mesh: exp: 4 (over z), row: 2 (over core), basis: 4 (over y, x).
Axes of the slice: x: 2, y: 2, z: 4, core: 2. Of those that a mesh axis runs over, the one named last changes fastest.
Arguments:
- scene_patches: bfloat16 [256, 4096], P(('exp', 'row')), may hold values from -6 to 6
- visit_dest: int32 [256, 4], P(('exp', 'row')), may hold values from 0 to 7, all different within a row; in each aligned block of 32 rows (0 to 31, 32 to 63, ...) at most 32 rows name the same one
- visit_block: int32 [256, 4], P(('exp', 'row')), may hold values from 0 to 127
- row_maps: bfloat16 [16, 96, 64], P('basis'), may hold values from -0.75 to 0.75
- col_maps: bfloat16 [16, 96, 64], P('basis'), may hold values from -0.75 to 0.75
- psf_weights: bfloat16 [32, 16, 4, 8], P('exp', 'basis', 'row'), may hold values from -1.796875 to 1.796875
- inv_variance: float32 [32], P(('exp', 'basis')), may hold values from 0.25 to 1
- observed: bfloat16 [32, 256, 512], P(('exp', 'basis'), 'row'), may hold values from -12 to 12
Outputs:
- residual: float32 [32, 256, 512], P(('exp', 'basis'), 'row')
Inputs may be any that keep to these rules, and one draw needn't show every extreme that they name: `visit_dest`: the 4 entries of a patch name different row bands. Among the 32 patches of one device no value is named more than 32 times, a bound that some block reaches.
All inputs are finite; a program needn't handle non-finite values.
Results may differ from a plain program's by a relative error of at most 0.0038.
Values may be sent and summed in bfloat16 or wider, within the bound.
No kernel may reach another device: no remote copies, remote signals or barrier semaphores. Data moves between devices by JAX's collectives and lax.ppermute only.
A program may use at most 64 MiB of HBM per device.

v0:
```python
import jax
import jax.numpy as jnp
from jax import lax
from jax.sharding import PartitionSpec as P


def passed_along(value, axis, by):
    length = lax.axis_size(axis)
    pairs = [(i, i + by) for i in range(length) if 0 <= i + by < length]
    return lax.ppermute(value, axis, pairs)


def pad_last(values, lower, upper):
    widths = [(0, 0)] * (values.ndim - 1) + [(lower, upper)]
    return jnp.pad(values, widths)


def fold_last(values, block_size):
    blocks_along = values.shape[-2]
    edge_width = values.shape[-1] - block_size
    lead = values.shape[:-2]
    head_part = values[..., :block_size].reshape(lead + (blocks_along * block_size,))
    tail_part = pad_last(values[..., block_size:], 0, block_size - edge_width)
    tail_part = tail_part.reshape(lead + (blocks_along * block_size,))
    head_part = pad_last(head_part, 0, edge_width)
    tail_part = pad_last(tail_part, block_size, 0)[..., : blocks_along * block_size + edge_width]
    return head_part + tail_part


def fold_blocks(images, block_size):
    images = jnp.swapaxes(images, -3, -2)
    images = fold_last(images, block_size)
    images = jnp.moveaxis(images, -1, -3)
    images = fold_last(images, block_size)
    return jnp.swapaxes(images, -1, -2)


def band_model(block_rows, weights, row_ops, col_ops, spill_rows, tile_cols):
    count_exp, kind_count, block_grid, col_grid = weights.shape
    block_size = row_ops.shape[2]
    out_width = row_ops.shape[1]
    tile_blocks = block_rows.reshape(-1, block_size, block_size)
    smeared = jnp.einsum(
        "nij,kcj->knic", tile_blocks, col_ops, preferred_element_type=jnp.float32
    ).astype(jnp.bfloat16)
    smeared = lax.optimization_barrier(smeared)
    scales = jnp.swapaxes(weights, 0, 1).reshape(kind_count, -1).astype(jnp.float32)
    scaled = (scales[:, :, None, None] * smeared).astype(jnp.bfloat16)
    images = jnp.einsum("kor,knrc->noc", row_ops, scaled, preferred_element_type=jnp.float32)
    images = images.reshape(count_exp, block_grid, col_grid, out_width, out_width)
    canvas = fold_blocks(images, block_size)
    return canvas[:, :, spill_rows : spill_rows + tile_cols]


def per_device(
    scene_patches, visit_dest, visit_block, row_maps, col_maps, psf_weights, inv_variance, observed
):
    group_size = lax.axis_size("exp") * lax.axis_size("row")
    patch_count, visit_count = visit_dest.shape
    capacity = max(2, 2 * patch_count * visit_count // group_size)
    exp_local, band_rows, tile_cols = observed.shape
    exp_group, kind_count, block_grid, col_grid = psf_weights.shape
    block_size = row_maps.shape[2]
    spill_rows = (row_maps.shape[1] - block_size) // 2
    per_exposure = block_grid * col_grid
    flat_dest = visit_dest.reshape(-1)
    matches = (flat_dest[:, None] == jnp.arange(group_size, dtype=jnp.int32)[None, :]).astype(
        jnp.int32
    )
    slot_rank = jnp.sum(jnp.cumsum(matches, axis=0) * matches, axis=1) - 1
    slot_index = flat_dest * capacity + slot_rank
    select_mat = (
        slot_index[None, :] == jnp.arange(group_size * capacity, dtype=jnp.int32)[:, None]
    ).astype(jnp.int32)
    tagged = jnp.sum(select_mat * (visit_block.reshape(-1) + 1)[None, :], axis=1).astype(
        jnp.bfloat16
    )
    picker = jnp.sum(
        select_mat.reshape(group_size * capacity, patch_count, visit_count), axis=2
    ).astype(jnp.bfloat16)
    outgoing = jnp.dot(picker, scene_patches, preferred_element_type=jnp.float32).astype(
        jnp.bfloat16
    )
    shaped = outgoing.reshape(group_size, capacity, -1)
    labels = tagged.reshape(group_size, capacity)
    arrived, arrived_tags = (
        lax.all_to_all(shaped, ("exp", "row"), split_axis=0, concat_axis=0, tiled=True),
        lax.all_to_all(labels, ("exp", "row"), split_axis=0, concat_axis=0, tiled=True),
    )
    arrived = arrived.reshape(group_size * capacity, -1)
    arrived_tags = arrived_tags.reshape(-1).astype(jnp.int32)
    row_all, col_all, weight_all = (
        lax.all_gather(row_maps, "basis", axis=0, tiled=True),
        lax.all_gather(col_maps, "basis", axis=0, tiled=True),
        lax.all_gather(psf_weights, "basis", axis=1, tiled=True),
    )
    first_exp = lax.axis_index("basis") * exp_local
    wanted = first_exp * per_exposure + 1 + jnp.arange(exp_local * per_exposure, dtype=jnp.int32)
    placing = (arrived_tags[None, :] == wanted[:, None]).astype(jnp.bfloat16)
    own_blocks = jnp.dot(placing, arrived, preferred_element_type=jnp.float32).astype(jnp.bfloat16)
    own_weights = lax.dynamic_slice_in_dim(weight_all, first_exp, exp_local, 0)
    model_band = band_model(own_blocks, own_weights, row_all, col_all, spill_rows, tile_cols)
    upper_spill = model_band[:, :spill_rows]
    lower_spill = model_band[:, spill_rows + band_rows :]
    from_above = passed_along(lower_spill.astype(jnp.bfloat16), "row", 1).astype(lower_spill.dtype)
    from_below = passed_along(upper_spill.astype(jnp.bfloat16), "row", -1).astype(upper_spill.dtype)
    core_rows = model_band[:, spill_rows : spill_rows + band_rows]
    core_rows = core_rows.at[:, :spill_rows].add(from_above)
    core_rows = core_rows.at[:, band_rows - spill_rows :].add(from_below)
    return jnp.sqrt(inv_variance)[:, None, None] * (observed.astype(jnp.float32) - core_rows)


def solution(mesh):
    return jax.shard_map(
        per_device,
        mesh=mesh,
        in_specs=(
            P(("exp", "row"), None),
            P(("exp", "row"), None),
            P(("exp", "row"), None),
            P("basis", None, None),
            P("basis", None, None),
            P("exp", "basis", "row", None),
            P(("exp", "basis")),
            P(("exp", "basis"), "row", None),
        ),
        out_specs=P(("exp", "basis"), "row", None),
        check_vma=False,
    )
```

profile of v0, /device:TPU:0, one launch (start us, length us, event | category | flops | bytes accessed | tf_op | source)
XLA Modules:
  0.0 81.4 jit_solution(5146840714770420215)
XLA Ops:
  0.0 0.8 copy.40
  1.4 0.7 broadcast_add_fusion
  2.4 0.7 convert_element_type.111
  3.1 6.4 %all-to-all-start = ((bf16[8,1,32]{2,1,0:T(2,128)(2,1)}), bf16[8,1,32]{2,1,0:T(2,128)(2,1)S(1)}, u32[]{:S(2)}, u32[]{:S(2)}) async-start(bf16[8,1,32]{2,1,0:T(2,128)(2,1)} %convert_element_type.111), calls=%async_computation | async-start | bytes 8192 | tf_op jit(solution)/shard_map/all_to_all | solution.py:88
  9.6 0.7 multiply_add_fusion
  10.4 2.1 %convolution_convert_fusion = bf16[256,4096]{1,0:T(8,128)(2,1)} fusion(bf16[32,4096]{1,0:T(8,128)(2,1)S(1)} %copy-done, s32[256,32]{0,1:T(8,128)S(1)} %convert_reduce_fusion), kind=kOutput, calls=%fused_computation.4 | convolution fusion | flops 68165632 | bytes 2392064 | tf_op jit(solution)/shard_map/dot_general | solution.py:81
  12.5 2.5 %all-to-all-done = bf16[8,1,32]{2,1,0:T(2,128)(2,1)S(1)} async-done(((bf16[8,1,32]{2,1,0:T(2,128)(2,1)}), bf16[8,1,32]{2,1,0:T(2,128)(2,1)S(1)}, u32[]{:S(2)}, u32[]{:S(2)}) %all-to-all-start) | async-done | bytes 544 | tf_op jit(solution)/shard_map/all_to_all | solution.py:88
  14.9 3.6 %all-to-all-start.1 = ((bf16[8,32,4096]{2,1,0:T(8,128)(2,1)}), bf16[8,32,4096]{2,1,0:T(8,128)(2,1)S(1)}, u32[]{:S(2)}, u32[]{:S(2)}) async-start(bf16[8,32,4096]{2,1,0:T(8,128)(2,1)} %bitcast.2), calls=%async_computation.1 | async-start | bytes 4194304 | tf_op jit(solution)/shard_map/all_to_all | solution.py:87
  18.6 8.4 %all_gather.9 = bf16[8,16,2,8]{3,2,1,0:T(2,128)(2,1)S(1)} all-gather(bf16[8,4,2,8]{3,2,1,0:T(2,128)(2,1)} %param.17), channel_id=1, replica_groups=mesh['exp'=4,'row'=2,'basis'=4] {'basis'}, dimensions={1}, use_global_device_ids=true | all-gather | bytes 5120 | tf_op jit(solution)/shard_map/all_gather | solution.py:95
  27.0 8.8 %all_gather.10 = bf16[16,96,64]{1,2,0:T(8,128)(2,1)S(1)} all-gather(bf16[4,96,64]{1,2,0:T(8,128)(2,1)} %param.16), channel_id=1, replica_groups=mesh['exp'=4,'row'=2,'basis'=4] {'basis'}, dimensions={0}, use_global_device_ids=true | all-gather | bytes 245760 | tf_op jit(solution)/shard_map/all_gather | solution.py:94
  35.8 8.3 %all_gather.11 = bf16[16,96,64]{1,2,0:T(8,128)(2,1)S(1)} all-gather(bf16[4,96,64]{1,2,0:T(8,128)(2,1)} %param.15), channel_id=1, replica_groups=mesh['exp'=4,'row'=2,'basis'=4] {'basis'}, dimensions={0}, use_global_device_ids=true | all-gather | bytes 245760 | tf_op jit(solution)/shard_map/all_gather | solution.py:93
  44.2 23.3 %all-to-all-done.1 = bf16[8,32,4096]{2,1,0:T(8,128)(2,1)S(1)} async-done(((bf16[8,32,4096]{2,1,0:T(8,128)(2,1)}), bf16[8,32,4096]{2,1,0:T(8,128)(2,1)S(1)}, u32[]{:S(2)}, u32[]{:S(2)}) %all-to-all-start.1) | async-done | bytes 2097184 | tf_op jit(solution)/shard_map/all_to_all | solution.py:87
  67.5 0.5 convolution_convert_fusion.1
  68.0 0.6 reshape.165
  68.5 2.3 %convert_bitcast_fusion = bf16[16,32,64,96]{3,2,0,1:T(8,128)(2,1)S(1)} fusion(bf16[32,64,64,1]{2,1,0,3:T(8,128)(2,1)S(1)} %reshape.165, bf16[16,96,64]{1,2,0:T(8,128)(2,1)S(1)} %all_gather.10), kind=kOutput, calls=%fused_computation.2 | convolution fusion | flops 405798912 | bytes 6750208 | tf_op jit(solution)/shard_map/nij,kcj->knic/dot_general | solution.py:43
  70.9 3.2 %fusion = f32[32,96,96,1]{2,1,3,0:T(8,128)S(1)} fusion(bf16[16,32,64,96]{3,2,0,1:T(8,128)(2,1)S(1)} %convert_bitcast_fusion, f32[16,32]{0,1:T(8,128)S(1)} %bitcast.42, bf16[16,96,64]{1,2,0:T(8,128)(2,1)S(1)} %all_gather.11), kind=kOutput, calls=%fused_computation.1 | convolution fusion | flops 613416960 | bytes 7669760 | tf_op jit(solution)/shard_map/kor,knrc->noc/dot_general | solution.py:49
  74.4 0.3 copy.45
  74.7 0.3 copy.44
  75.0 0.3 add_bitcast_fusion
  75.7 1.5 %collective-permute-start = (bf16[2,16,512]{2,1,0:T(8,128)(2,1)S(1)}, bf16[2,16,512]{2,1,0:T(8,128)(2,1)S(1)}, u32[]{:S(2)}, u32[]{:S(2)}) collective-permute-start(bf16[2,16,512]{2,1,0:T(8,128)(2,1)S(1)} %get-tuple-element.32), channel_id=1, source_target_pairs={{0,4},{1,5},{2,6},{3,7},{8,12},{9,13},{10,14},{11,15},{16,20},{17,... | collective-permute-start | bytes 98312 | tf_op jit(solution)/shard_map/ppermute | solution.py:10
  77.1 0.2 slice.97
  77.4 1.3 %collective-permute-start.1 = (bf16[2,16,512]{2,1,0:T(8,128)(2,1)S(1)}, bf16[2,16,512]{2,1,0:T(8,128)(2,1)S(1)}, u32[]{:S(2)}, u32[]{:S(2)}) collective-permute-start(bf16[2,16,512]{2,1,0:T(8,128)(2,1)S(1)} %get-tuple-element.31), channel_id=1, source_target_pairs={{4,0},{5,1},{6,2},{7,3},{12,8},{13,9},{14,10},{15,11},{20,16},{21,... | collective-permute-start | bytes 98312 | tf_op jit(solution)/shard_map/ppermute | solution.py:10
  78.8 1.7 %collective-permute-done.1 = bf16[2,16,512]{2,1,0:T(8,128)(2,1)S(1)} collective-permute-done((bf16[2,16,512]{2,1,0:T(8,128)(2,1)S(1)}, bf16[2,16,512]{2,1,0:T(8,128)(2,1)S(1)}, u32[]{:S(2)}, u32[]{:S(2)}) %collective-permute-start.1) | collective-permute-done | bytes 32800 | tf_op jit(solution)/shard_map/ppermute | solution.py:10
  80.5 0.9 %subtract_multiply_fusion = f32[2,128,512]{2,1,0:T(8,128)} fusion(f32[2,128,512]{2,1,0:T(8,128)S(1)} %fusion.7, bf16[2,128,512]{2,1,0:T(8,128)(2,1)S(1)} %copy-done.1, f32[2]{0:T(128)S(1)} %sqrt.3), kind=kLoop, calls=%fused_computation.11 | loop fusion | flops 393216 | bytes 1310728 | tf_op jit(solution)/shard_map/mul | solution.py:110
  (35 shorter events, 1.9 us)
Async XLA Ops:
  0.0 10.4 %copy-start = (bf16[32,4096]{1,0:T(8,128)(2,1)S(1)}, bf16[32,4096]{1,0:T(8,128)(2,1)}, u32[]{:S(2)}) copy-start(bf16[32,4096]{1,0:T(8,128)(2,1)} %param.12) | copy-start | bytes 786436
  3.1 11.9 %all-to-all-start = ((bf16[8,1,32]{2,1,0:T(2,128)(2,1)}), bf16[8,1,32]{2,1,0:T(2,128)(2,1)S(1)}, u32[]{:S(2)}, u32[]{:S(2)}) async-start(bf16[8,1,32]{2,1,0:T(2,128)(2,1)} %convert_element_type.111), calls=%async_computation | async-start | bytes 8192 | tf_op jit(solution)/shard_map/all_to_all | solution.py:88
  14.9 52.6 %all-to-all-start.1 = ((bf16[8,32,4096]{2,1,0:T(8,128)(2,1)}), bf16[8,32,4096]{2,1,0:T(8,128)(2,1)S(1)}, u32[]{:S(2)}, u32[]{:S(2)}) async-start(bf16[8,32,4096]{2,1,0:T(8,128)(2,1)} %bitcast.2), calls=%async_computation.1 | async-start | bytes 4194304 | tf_op jit(solution)/shard_map/all_to_all | solution.py:87
  74.1 3.1 %copy-start.2 = (f32[2]{0:T(128)S(1)}, f32[2]{0:T(128)}, u32[]{:S(2)}) copy-start(f32[2]{0:T(128)} %param.18) | copy-start | bytes 28
  74.1 6.3 %copy-start.1 = (bf16[2,128,512]{2,1,0:T(8,128)(2,1)S(1)}, bf16[2,128,512]{2,1,0:T(8,128)(2,1)}, u32[]{:S(2)}) copy-start(bf16[2,128,512]{2,1,0:T(8,128)(2,1)} %param.19) | copy-start | bytes 786436
  75.7 3.0 %collective-permute-start = (bf16[2,16,512]{2,1,0:T(8,128)(2,1)S(1)}, bf16[2,16,512]{2,1,0:T(8,128)(2,1)S(1)}, u32[]{:S(2)}, u32[]{:S(2)}) collective-permute-start(bf16[2,16,512]{2,1,0:T(8,128)(2,1)S(1)} %get-tuple-element.32), channel_id=1, source_target_pairs={{0,4},{1,5},{2,6},{3,7},{8,12},{9,13},{10,14},{11,15},{16,20},{17,... | collective-permute-start | bytes 98312 | tf_op jit(solution)/shard_map/ppermute | solution.py:10
  77.4 3.1 %collective-permute-start.1 = (bf16[2,16,512]{2,1,0:T(8,128)(2,1)S(1)}, bf16[2,16,512]{2,1,0:T(8,128)(2,1)S(1)}, u32[]{:S(2)}, u32[]{:S(2)}) collective-permute-start(bf16[2,16,512]{2,1,0:T(8,128)(2,1)S(1)} %get-tuple-element.31), channel_id=1, source_target_pairs={{4,0},{5,1},{6,2},{7,3},{12,8},{13,9},{14,10},{15,11},{20,16},{21,... | collective-permute-start | bytes 98312 | tf_op jit(solution)/shard_map/ppermute | solution.py:10
where the time goes:
time: 81.9 us; the launch traced here: 81.4 us
  waiting for transfers between devices  27.5 us (34%)
  blocking collectives  25.4 us (31%)
  starting transfers between devices  12.7 us (16%)
  matrix products  8.07 us (10%)
  local copies, waits for them, and re-layouts  3.96 us (5%)
  other arithmetic  3.5 us (4%)
    all_to_all x1, waiting for transfers between devices, per_device(): lax.all_to_all(shaped, ('exp', 'row'), split_axis=0, concat_axis=0, tiled...  23.3 us
    all_gather x1, blocking collectives, per_device(): lax.all_gather(col_maps, 'basis', axis=0, tiled=True)  8.79 us
    all_gather x1, blocking collectives, per_device(): lax.all_gather(psf_weights, 'basis', axis=1, tiled=True)  8.36 us
    all_gather x1, blocking collectives, per_device(): lax.all_gather(row_maps, 'basis', axis=0, tiled=True)  8.28 us
    all_to_all x1, starting transfers between devices, per_device(): lax.all_to_all(labels, ('exp', 'row'), split_axis=0, concat_axis=0, tiled...  6.35 us
    all_to_all x1, starting transfers between devices, per_device(): lax.all_to_all(shaped, ('exp', 'row'), split_axis=0, concat_axis=0, tiled...  3.6 us
    dot_general x1, matrix products, band_model(): jnp.einsum('kor,knrc->noc', row_ops, scaled, preferred_element_type=jnp.f...  3.19 us
    ppermute x2, starting transfers between devices, passed_along(): return lax.ppermute(value, axis, pairs)  2.74 us
  transfers between devices with their start and end apart: 4, of which 3 were waited for; matrix products, arithmetic and copies ran while one was open for 4% of the time, Pallas kernels for 0%

commit v1 on v0

--- a/solution.py
+++ b/solution.py
@@ -1,7 +1,269 @@
+import functools
 import jax
 import jax.numpy as jnp
 from jax import lax
+from jax.experimental import pallas as pl
+from jax.experimental.pallas import tpu as pltpu
 from jax.sharding import PartitionSpec as P
+
+LANES = 128
+VMEM_BYTES = 28 * 1024 * 1024
+
+
+def swapped(value, axis, by):
+    length = lax.axis_size(axis)
+    return lax.ppermute(value, axis, [(i, i ^ by) for i in range(length)])
+
+
+def in_vmem(count):
+    return [pl.BlockSpec(memory_space=pltpu.VMEM)] * count
+
+
+def visit_codes(tags, visits, group_blocks):
+    tags = tags.astype(jnp.float32)
+    return tags[:, :visits] * group_blocks + tags[:, visits : 2 * visits]
+
+
+def picks(tags, dims, places):
+    visits, group_blocks, per_exp, col_grid, band_grid, strips, exp_local, rows_axis = dims
+    group, band, basis = places
+    codes = visit_codes(tags, visits, group_blocks)
+    lane = lax.broadcasted_iota(jnp.int32, (1, LANES), 1)
+    exp_at = lane // (strips * col_grid)
+    strip = lane // col_grid % strips
+    block_row = band * (band_grid - 1) + strip
+    dest = group * rows_axis + block_row // band_grid
+    block = (basis * exp_local + exp_at) * per_exp + block_row % band_grid * col_grid + lane % col_grid
+    want = jnp.where(exp_at < exp_local, dest * group_blocks + block, -1).astype(jnp.float32)
+    hit = jnp.zeros((tags.shape[0], LANES), jnp.float32)
+    for v in range(visits):
+        hit = hit + jnp.where(codes[:, v : v + 1] == want, 1.0, 0.0)
+    blocks = exp_local * strips * col_grid
+    return hit.T[:blocks].astype(jnp.bfloat16)
+
+
+def summed_into(out_ref, chunk_refs, before_ref, dims, width, blocks):
+    places = (lax.axis_index("exp"), lax.axis_index("row"), lax.axis_index("basis"))
+    tags = jnp.concatenate([ref[:, width:] for ref in chunk_refs], axis=0)
+    pick = picks(tags, dims, places)
+    step = 4 * LANES
+    for start in range(0, width, step):
+        rows = jnp.concatenate([ref[:, start : start + step] for ref in chunk_refs], axis=0)
+        part = jnp.dot(pick, rows, preferred_element_type=jnp.float32)
+        for t in range(step // LANES):
+            at = (start // LANES + t) * blocks
+            piece = part[:, t * LANES : (t + 1) * LANES]
+            if before_ref is not None:
+                piece = piece + before_ref[at : at + blocks, :]
+            out_ref[at : at + blocks, :] = piece
+
+
+def early_kernel(dims, width, block, kinds_local, *refs):
+    chunk_count = 6
+    chunks = refs[:chunk_count]
+    parcels = refs[chunk_count:-5]
+    sums_ref, rows_ref, main_ref, edge_ref, wide_ref = refs[-5:]
+    visits, group_blocks, per_exp, col_grid, band_grid, strips, exp_local, rows_axis = dims
+    blocks = exp_local * strips * col_grid
+    summed_into(sums_ref, chunks, None, dims, width, blocks)
+    band = lax.axis_index("row")
+    out_rows = 96
+    kinds = kinds_local * len(parcels)
+    src = lax.broadcasted_iota(jnp.int32, (LANES, 2 * LANES), 0)
+    dst = lax.broadcasted_iota(jnp.int32, (LANES, 2 * LANES), 1)
+    half = block // 2
+    inner = dst % block
+    wanted = inner % half * 2 + inner // half
+    perm = jnp.where((src == wanted) & (dst < strips * block), 1.0, 0.0).astype(jnp.bfloat16)
+    lane2 = lax.broadcasted_iota(jnp.int32, (out_rows, 2 * LANES), 1)
+    spill = (out_rows - block) // 2
+    lane_c = lax.broadcasted_iota(jnp.int32, (block, 2 * LANES), 1)
+    lane_e = lax.broadcasted_iota(jnp.int32, (block, LANES), 1)
+    for k in range(kinds):
+        parcel = parcels[k // kinds_local]
+        both = parcel[(k % kinds_local) * out_rows : (k % kinds_local + 1) * out_rows, :]
+        moved = jnp.dot(both, perm, preferred_element_type=jnp.float32)
+        gap = jnp.zeros((block, 2 * LANES), jnp.float32)
+        total = None
+        for s in range(strips):
+            piece = jnp.where(lane2 // block == s, moved, 0.0)
+            parts = [gap] * s + [piece] + [gap] * (strips - 1 - s)
+            piece = jnp.concatenate(parts, axis=0)
+            total = piece if total is None else total + piece
+        first = total[spill : spill + 2 * block, : strips * block]
+        second = total[spill + block : spill + 3 * block, : strips * block]
+        chosen = jnp.where(band == 0, first, second).astype(jnp.bfloat16)
+        rows_ref[k * 2 * block : (k + 1) * 2 * block, :] = chosen
+        cols = both.astype(jnp.float32)
+        cols = jnp.concatenate([cols, jnp.zeros((LANES - out_rows, LANES), jnp.float32)], axis=0)
+        turned = cols.T[block:, :]
+        turned = jnp.concatenate([turned, jnp.zeros_like(turned)], axis=1)
+        for b in range(4):
+            shift = (b * block - spill) % (2 * LANES)
+            placed = pltpu.roll(turned, shift, 1)
+            kept = placed
+            if b == 0:
+                kept = jnp.where(lane_c < 2 * LANES - spill, placed, 0.0)
+                edge = jnp.where(lane_e >= LANES - spill, placed[:, LANES:], 0.0)
+                edge_ref[0, k * LANES : k * LANES + block, :] = edge.astype(jnp.bfloat16)
+                edge_ref[0, k * LANES + block : (k + 1) * LANES, :] = jnp.zeros((block, LANES), jnp.bfloat16)
+            if b == 3:
+                kept = jnp.where(lane_c >= spill, placed, 0.0)
+                edge = jnp.where(lane_e < spill, placed[:, :LANES], 0.0)
+                edge_ref[1, k * LANES + block : (k + 1) * LANES, :] = edge.astype(jnp.bfloat16)
+                edge_ref[1, k * LANES : k * LANES + block, :] = jnp.zeros((block, LANES), jnp.bfloat16)
+            at = k * 4 * block + b * block
+            main_ref[at : at + block, :] = kept.astype(jnp.bfloat16)
+    src = lax.broadcasted_iota(jnp.int32, (LANES, col_grid * block), 0)
+    dst = lax.broadcasted_iota(jnp.int32, (LANES, col_grid * block), 1)
+    spread = jnp.where(src == dst // block, 1.0, 0.0).astype(jnp.bfloat16)
+    for p, parcel in enumerate(parcels):
+        table = parcel[kinds_local * out_rows :, :]
+        lines = jnp.dot(table, spread, preferred_element_type=jnp.float32)
+        for x in range(exp_local):
+            for s in range(strips):
+                for kl in range(kinds_local):
+                    line = (x * (strips + 1) + s) * kinds_local + kl
+                    wide = jnp.broadcast_to(lines[line : line + 1], (16, col_grid * block))
+                    at = ((x * kinds + p * kinds_local + kl) * strips + s) * 16
+                    wide_ref[at : at + 16, :] = wide.astype(jnp.bfloat16)
+
+
+def late_kernel(dims, width, block, kinds, *refs):
+    chunks = refs[:6]
+    (before_ref, rows_ref, main_ref, edge_ref, wide_ref, obs_ref, inv_ref, out_ref) = refs[6:14]
+    sums_ref, image_ref, mid_ref, side_ref = refs[14:]
+    visits, group_blocks, per_exp, col_grid, band_grid, strips, exp_local, rows_axis = dims
+    blocks = exp_local * strips * col_grid
+    summed_into(sums_ref, chunks, before_ref, dims, width, blocks)
+    half = block // 2
+    low = lax.broadcasted_iota(jnp.int32, (half, LANES), 1) < block
+    tall = strips * block
+    wide_cols = col_grid * block
+    band_rows = band_grid * block
+    for x in range(exp_local):
+        for s in range(strips):
+            for m in range(col_grid // 2):
+                n = (x * strips + s) * col_grid + 2 * m
+                a = sums_ref[pl.ds(n, half, stride=blocks), :]
+                b = sums_ref[pl.ds(n + 1, half, stride=blocks), :]
+                even = jnp.where(low, a, pltpu.roll(b, block, 1))
+                odd = jnp.where(low, pltpu.roll(a, block, 1), b)
+                at = s * block
+                cols = slice(m * LANES, (m + 1) * LANES)
+                image_ref[x, at : at + half, cols] = even.astype(jnp.bfloat16)
+                image_ref[x, at + half : at + block, cols] = odd.astype(jnp.bfloat16)
+    window = 4 * block
+    for x in range(exp_local):
+        for k in range(kinds):
+            image = image_ref[x].reshape(strips, block // 16, 16, wide_cols)
+            at = (x * kinds + k) * strips * 16
+            wide = wide_ref[at : at + strips * 16, :].reshape(strips, 1, 16, wide_cols)
+            scaled = (image * wide).reshape(tall, wide_cols)
+            rows = rows_ref[k * band_rows : (k + 1) * band_rows, :]
+            mid = jnp.dot(rows, scaled, preferred_element_type=jnp.float32).astype(jnp.bfloat16)
+            for w in range(2):
+                top = (w * exp_local + x) * band_rows
+                mid_ref[top : top + band_rows, k * window : (k + 1) * window] = mid[:, w * window : (w + 1) * window]
+            at = x * band_rows
+            cols = slice(k * LANES, (k + 1) * LANES)
+            side_ref[0, at : at + band_rows, cols] = mid[:, window : window + LANES]
+            side_ref[1, at : at + band_rows, cols] = mid[:, window - LANES : window]
+    tall2 = exp_local * band_rows
+    for w in range(2):
+        main = jnp.dot(mid_ref[w * tall2 : (w + 1) * tall2, :], main_ref[...], preferred_element_type=jnp.float32)
+        side = jnp.dot(side_ref[w], edge_ref[w], preferred_element_type=jnp.float32)
+        for x in range(exp_local):
+            rows = slice(x * band_rows, (x + 1) * band_rows)
+            noise = jnp.sqrt(jnp.full((1, LANES), inv_ref[x], jnp.float32))
+            for t in range(2):
+                model = main[rows, t * LANES : (t + 1) * LANES]
+                if t == 1 - w:
+                    model = model + side[rows]
+                cols = slice(w * window + t * LANES, w * window + (t + 1) * LANES)
+                out_ref[x, :, cols] = noise * (obs_ref[x, :, cols].astype(jnp.float32) - model)
+
+
+def gathered_device(
+    scene_patches, visit_dest, visit_block, row_maps, col_maps, psf_weights, inv_variance, observed
+):
+    n_exp, n_row, n_basis = (lax.axis_size(a) for a in ("exp", "row", "basis"))
+    patch_count, visits = visit_dest.shape
+    width = scene_patches.shape[1]
+    exp_local, band_rows, tile_cols = observed.shape
+    exp_group, kinds_local, band_grid, col_grid = psf_weights.shape
+    block = row_maps.shape[2]
+    out_width = row_maps.shape[1]
+    strips = band_grid + 1
+    per_exp = band_grid * col_grid
+    group_blocks = exp_group * per_exp
+    kinds = kinds_local * n_basis
+    basis, band = lax.axis_index("basis"), lax.axis_index("row")
+    dims = (visits, group_blocks, per_exp, col_grid, band_grid, strips, exp_local, n_row)
+    blocks = exp_local * strips * col_grid
+
+    tags = jnp.concatenate([visit_dest, visit_block], axis=1).astype(jnp.bfloat16)
+    tags = jnp.pad(tags, ((0, 0), (0, LANES - 2 * visits)))
+    own = jnp.concatenate([scene_patches, tags], axis=1)
+    part = patch_count // n_basis
+    own_part = lax.dynamic_slice_in_dim(own, basis * part, part, 0)
+
+    far = [swapped(own_part, "exp", s) for s in range(n_exp - 1, 1, -1)]
+    near = swapped(own, "exp", 1)
+    own_other = swapped(own, "row", 1)
+
+    weights_other = swapped(psf_weights, "row", 1)
+    weights = jnp.where(
+        band == 0,
+        jnp.concatenate([psf_weights, weights_other[:, :, :1]], axis=2),
+        jnp.concatenate([weights_other[:, :, band_grid - 1 :], psf_weights], axis=2),
+    )
+    weights = jnp.pad(jnp.swapaxes(weights, 1, 2), ((0, 0), (0, 1), (0, 0), (0, LANES - col_grid)))
+    weights = weights.reshape(n_basis, -1, LANES)
+    maps = jnp.concatenate([row_maps, col_maps], axis=2).reshape(-1, LANES)
+    parcels = []
+    for s in range(n_basis):
+        table = lax.dynamic_index_in_dim(weights, basis ^ s, 0, keepdims=False)
+        parcel = jnp.concatenate([maps, table], axis=0)
+        parcels.append(swapped(parcel, "basis", s) if s else parcel)
+
+    far = jnp.concatenate(far, axis=0)
+    spread = [swapped(far, "basis", s) for s in range(n_basis - 1, 0, -1)]
+    near_other = swapped(near, "row", 1)
+    far_other = swapped(far, "row", 1)
+    spread_other = [swapped(v, "row", 1) for v in spread]
+
+    f32, bf16 = jnp.float32, jnp.bfloat16
+    params = pltpu.CompilerParams(vmem_limit_bytes=VMEM_BYTES)
+    early = [own, near, far, own_other, near_other, far_other] + parcels
+    shapes = [
+        jax.ShapeDtypeStruct((width // LANES * blocks, LANES), f32),
+        jax.ShapeDtypeStruct((kinds * band_rows, strips * block), bf16),
+        jax.ShapeDtypeStruct((kinds * 4 * block, 4 * block), bf16),
+        jax.ShapeDtypeStruct((2, kinds * LANES, LANES), bf16),
+        jax.ShapeDtypeStruct((exp_local * kinds * strips * 16, tile_cols), bf16),
+    ]
+    tables = pl.pallas_call(
+        functools.partial(early_kernel, dims, width, block, kinds_local),
+        out_shape=shapes,
+        in_specs=in_vmem(len(early)),
+        out_specs=in_vmem(len(shapes)),
+        compiler_params=params,
+    )(*early)
+    late = spread + spread_other + list(tables) + [observed]
+    return pl.pallas_call(
+        functools.partial(late_kernel, dims, width, block, kinds),
+        out_shape=jax.ShapeDtypeStruct(observed.shape, f32),
+        in_specs=in_vmem(len(late)) + [pl.BlockSpec(memory_space=pltpu.SMEM)],
+        out_specs=pl.BlockSpec(memory_space=pltpu.VMEM),
+        scratch_shapes=[
+            pltpu.VMEM((width // LANES * blocks, LANES), f32),
+            pltpu.VMEM((exp_local, strips * block, tile_cols), bf16),
+            pltpu.VMEM((2 * exp_local * band_rows, kinds * 4 * block), bf16),
+            pltpu.VMEM((2, exp_local * band_rows, kinds * LANES), bf16),
+        ],
+        compiler_params=params,
+    )(*late, inv_variance)
 
 
 def passed_along(value, axis, by):
@@ -52,7 +314,7 @@
     return canvas[:, :, spill_rows : spill_rows + tile_cols]
 
 
-def per_device(
+def exchanged_device(
     scene_patches, visit_dest, visit_block, row_maps, col_maps, psf_weights, inv_variance, observed
 ):
     group_size = lax.axis_size("exp") * lax.axis_size("row")
@@ -110,9 +372,23 @@
     return jnp.sqrt(inv_variance)[:, None, None] * (observed.astype(jnp.float32) - core_rows)
 
 
+def gathers(mesh, patch_count, visits):
+    n_exp, n_row, n_basis = mesh.shape["exp"], mesh.shape["row"], mesh.shape["basis"]
+    capacity = max(2, 2 * patch_count * visits // (n_exp * n_row))
+    powers = all(n & (n - 1) == 0 for n in (n_exp, n_basis)) and n_exp > 2
+    return capacity >= patch_count and powers and n_row == 2 and patch_count % (8 * n_basis) == 0
+
+
+def per_device(mesh, *arrays):
+    patch_count, visits = arrays[1].shape
+    if gathers(mesh, patch_count, visits):
+        return gathered_device(*arrays)
+    return exchanged_device(*arrays)
+
+
 def solution(mesh):
     return jax.shard_map(
-        per_device,
+        functools.partial(per_device, mesh),
         mesh=mesh,
         in_specs=(
             P(("exp", "row"), None),

time: 81.9 us -> 39 us (0.48)
  blocking collectives: 25.4 us -> 0 us
  waiting for transfers between devices: 27.5 us -> 13.8 us
  matrix products: 8.07 us -> 0 us
  Pallas kernels: 0 us -> 6.79 us
  local copies, waits for them, and re-layouts: 3.96 us -> 0.32 us
    all_to_all x2 -> x0, waiting for transfers between devices: 25.8 us -> none  [the longest x1 23.3 us: per_device(): lax.all_to_all(shaped, ('exp', 'row'), split_axis=0, concat_axis=0, tiled...]
    all_gather x3 -> x0, blocking collectives: 25.4 us -> none  [the longest x1 8.79 us: per_device(): lax.all_gather(col_maps, 'basis', axis=0, tiled=True)]
    ppermute x2 -> x16, waiting for transfers between devices: 1.7 us -> 13.8 us  [swapped(): return lax.ppermute(value, axis, [(i, i ^ by) for i in range(length)])]
    ppermute x2 -> x16, starting transfers between devices: 2.74 us -> 13.5 us  [swapped(): return lax.ppermute(value, axis, [(i, i ^ by) for i in range(length)])]
    all_to_all x2 -> x0, starting transfers between devices: 9.96 us -> none  [the longest x1 6.35 us: per_device(): lax.all_to_all(labels, ('exp', 'row'), split_axis=0, concat_axis=0, tiled...]
    dot_general x4 -> x0, matrix products: 8.07 us -> none  [the longest x1 3.19 us: band_model(): jnp.einsum('kor,knrc->noc', row_ops, scaled, preferred_element_type=jnp.f...]
    pallas_call x0 -> x2, Pallas kernels: none -> 6.79 us  [the longest x1 5.33 us: gathered_device(): pl.pallas_call(functools.partial(late_kernel, dims, width, block, kinds),...]
    concatenate x0 -> x4, other arithmetic: none -> 1.94 us  [the longest x1 0.97 us: gathered_device(): own = jnp.concatenate([scene_patches, tags], axis=1)]
  transfers between devices with their start and end apart: 4 -> 16, of which waited for: 3 -> 6; matrix products, arithmetic and copies ran while one was open for 4% -> 5% of each run, Pallas kernels for 0% -> 4%
where the time goes in v1:
time: 39 us; the launch traced here: 38.8 us
  waiting for transfers between devices  13.8 us (35%)
  starting transfers between devices  13.5 us (35%)
  Pallas kernels  6.79 us (17%)
  other arithmetic  4.24 us (11%)
    ppermute x16, waiting for transfers between devices, swapped(): return lax.ppermute(value, axis, [(i, i ^ by) for i in range(length)])  13.8 us
    ppermute x16, starting transfers between devices, swapped(): return lax.ppermute(value, axis, [(i, i ^ by) for i in range(length)])  13.5 us
    pallas_call x1, Pallas kernels, gathered_device(): pl.pallas_call(functools.partial(late_kernel, dims, width, block, kinds),...  5.33 us
    pallas_call x1, Pallas kernels, gathered_device(): pl.pallas_call(functools.partial(early_kernel, dims, width, block, kinds_...  1.46 us
    another operation x2, other arithmetic  1.41 us
    concatenate x1, other arithmetic, gathered_device(): own = jnp.concatenate([scene_patches, tags], axis=1)  0.97 us
    concatenate x1, other arithmetic, gathered_device(): maps = jnp.concatenate([row_maps, col_maps], axis=2).reshape(-1, LANES)  0.9 us
    transpose x1, other arithmetic, gathered_device(): jnp.swapaxes(weights, 1, 2)  0.89 us
  transfers between devices with their start and end apart: 16, of which 6 were waited for; matrix products, arithmetic and copies ran while one was open for 5% of the time, Pallas kernels for 4%

profile of v1, /device:TPU:0, one launch (start us, length us, event | category | flops | bytes accessed | tf_op | source)
XLA Modules:
  0.0 38.8 jit_solution(6238580449254297620)
XLA Ops:
  0.0 0.7 %convert.6 = bf16[32,4]{0,1:T(4,128)(2,1)S(1)} convert(s32[32,4]{0,1:T(4,128)} %param.9) | non-fusion elementwise | flops 128 | bytes 768 | tf_op jit(solution)/shard_map/convert
  0.7 0.7 %convert.7 = bf16[32,4]{0,1:T(4,128)(2,1)S(1)} convert(s32[32,4]{0,1:T(4,128)} %param.10) | non-fusion elementwise | flops 128 | bytes 768 | tf_op jit(solution)/shard_map/convert.1
  1.4 0.1 copy.16
  1.5 1.0 %fusion.1.refs_0_ = bf16[32,4224]{1,0:T(8,128)(2,1)S(1)} fusion(bf16[32,8]{1,0:T(8,128)(2,1)S(1)} %copy.16, bf16[32,4096]{1,0:T(8,128)(2,1)} %param.8), kind=kLoop, calls=%fused_computation.2 | loop fusion | flops 811008 | bytes 532992 | tf_op jit(solution)/shard_map/concatenate | solution.py:207
  2.5 5.1 %collective-permute-start = (bf16[8,4224]{1,0:T(8,128)(2,1)S(1)}, bf16[8,4224]{1,0:T(8,128)(2,1)S(1)}, u32[]{:S(2)}, u32[]{:S(2)}) collective-permute-start(bf16[8,4224]{1,0:T(8,128)(2,1)S(1)} %constant_dynamic-slice_fusion), channel_id=1, source_target_pairs={{0,24},{8,16},{16,8},{24,0},{1,25},{9,17},{17,9},{25,1},{2,26},{10... | collective-permute-start | bytes 202760 | tf_op jit(solution)/shard_map/ppermute | solution.py:15
  7.7 0.6 %collective-permute-start.8 = (bf16[32,4224]{1,0:T(8,128)(2,1)S(1)}, bf16[32,4224]{1,0:T(8,128)(2,1)S(1)}, u32[]{:S(2)}, u32[]{:S(2)}) collective-permute-start(bf16[32,4224]{1,0:T(8,128)(2,1)S(1)} %fusion.1.refs_0_), channel_id=1, source_target_pairs={{0,8},{8,0},{16,24},{24,16},{1,9},{9,1},{17,25},{25,17},{2,10},{10... | collective-permute-start | bytes 811016 | tf_op jit(solution)/shard_map/ppermute | solution.py:15
  8.3 0.9 %pad_maximum_fusion = bf16[4,96,128]{1,2,0:T(8,128)(2,1)S(1)} fusion(bf16[4,96,64]{1,2,0:T(8,128)(2,1)} %param.12, bf16[4,96,64]{1,2,0:T(8,128)(2,1)} %param.11), kind=kLoop, calls=%fused_computation.3 | loop fusion | flops 196608 | bytes 196608 | tf_op jit(solution)/shard_map/concatenate | solution.py:223
  9.2 0.1 copy.17
  9.4 0.3 collective-permute-done.12
  9.7 0.9 %fusion.2 = bf16[8,3,4,8]{3,1,2,0:T(4,128)(2,1)S(1)} fusion(bf16[8,4,1,8]{3,2,1,0:T(2,128)(2,1)S(1)} %get-tuple-element.24, bf16[8,4,2,8]{3,2,1,0:T(2,128)(2,1)} %param.13, bf16[8,4,1,8]{3,2,1,0:T(2,128)(2,1)S(1)} %get-tuple-element.23, pred[]{:T(512)S(6)} %eq.3), kind=kLoop, calls=%fused_computation.9 | loop fusion | flops 6912 | bytes 3585 | tf_op jit(solution)/shard_map/transpose | solution.py:221
  10.7 2.8 %collective-permute-done.1 = bf16[8,4224]{1,0:T(8,128)(2,1)S(1)} collective-permute-done((bf16[8,4224]{1,0:T(8,128)(2,1)S(1)}, bf16[8,4224]{1,0:T(8,128)(2,1)S(1)}, u32[]{:S(2)}, u32[]{:S(2)}) %collective-permute-start.1) | collective-permute-done | bytes 67616 | tf_op jit(solution)/shard_map/ppermute | solution.py:15
  13.7 1.6 %collective-permute-start.13 = (bf16[416,128]{1,0:T(8,128)(2,1)S(1)}, bf16[416,128]{1,0:T(8,128)(2,1)S(1)}, u32[]{:S(2)}, u32[]{:S(2)}) collective-permute-start(bf16[416,128]{1,0:T(8,128)(2,1)S(1)} %get-tuple-element.16), channel_id=1, source_target_pairs={{0,1},{1,0},{2,3},{3,2},{4,5},{5,4},{6,7},{7,6},{8,9},{9,8},{10,11... | collective-permute-start | bytes 319496 | tf_op jit(solution)/shard_map/ppermute | solution.py:15
  15.2 1.5 %collective-permute-start.14 = (bf16[416,128]{1,0:T(8,128)(2,1)S(1)}, bf16[416,128]{1,0:T(8,128)(2,1)S(1)}, u32[]{:S(2)}, u32[]{:S(2)}) collective-permute-start(bf16[416,128]{1,0:T(8,128)(2,1)S(1)} %get-tuple-element.17), channel_id=1, source_target_pairs={{0,2},{1,3},{2,0},{3,1},{4,6},{5,7},{6,4},{7,5},{8,10},{9,11},{10,... | collective-permute-start | bytes 319496 | tf_op jit(solution)/shard_map/ppermute | solution.py:15
  16.7 0.5 %collective-permute-start.15 = (bf16[416,128]{1,0:T(8,128)(2,1)S(1)}, bf16[416,128]{1,0:T(8,128)(2,1)S(1)}, u32[]{:S(2)}, u32[]{:S(2)}) collective-permute-start(bf16[416,128]{1,0:T(8,128)(2,1)S(1)} %get-tuple-element.15), channel_id=1, source_target_pairs={{0,3},{1,2},{2,1},{3,0},{4,7},{5,6},{6,5},{7,4},{8,11},{9,10},{10,... | collective-permute-start | bytes 319496 | tf_op jit(solution)/shard_map/ppermute | solution.py:15
  17.2 1.9 %collective-permute-done.13.refs_7_ = bf16[416,128]{1,0:T(8,128)(2,1)S(1)} collective-permute-done((bf16[416,128]{1,0:T(8,128)(2,1)S(1)}, bf16[416,128]{1,0:T(8,128)(2,1)S(1)}, u32[]{:S(2)}, u32[]{:S(2)}) %collective-permute-start.13) | collective-permute-done | bytes 106528 | tf_op jit(solution)/shard_map/ppermute | solution.py:15
  19.1 3.5 %collective-permute-done.14.refs_8_ = bf16[416,128]{1,0:T(8,128)(2,1)S(1)} collective-permute-done((bf16[416,128]{1,0:T(8,128)(2,1)S(1)}, bf16[416,128]{1,0:T(8,128)(2,1)S(1)}, u32[]{:S(2)}, u32[]{:S(2)}) %collective-permute-start.14) | collective-permute-done | bytes 106528 | tf_op jit(solution)/shard_map/ppermute | solution.py:15
  22.6 1.5 %collective-permute-start.2 = (bf16[16,4224]{1,0:T(8,128)(2,1)S(1)}, bf16[16,4224]{1,0:T(8,128)(2,1)S(1)}, u32[]{:S(2)}, u32[]{:S(2)}) collective-permute-start(bf16[16,4224]{1,0:T(8,128)(2,1)S(1)} %constant_dynamic-update-slice_fusion.refs_2_), channel_id=1, source_target_pairs={{0,3},{1,2},{2,1},{3,0},{4,7},{5,6},{6,5},{7,4},{8,11},{9,10},{10,... | collective-permute-start | bytes 405512 | tf_op jit(solution)/shard_map/ppermute | solution.py:15
  24.1 0.1 collective-permute-start.3
  24.2 2.0 %collective-permute-start.4 = (bf16[16,4224]{1,0:T(8,128)(2,1)S(1)}, bf16[16,4224]{1,0:T(8,128)(2,1)S(1)}, u32[]{:S(2)}, u32[]{:S(2)}) collective-permute-start(bf16[16,4224]{1,0:T(8,128)(2,1)S(1)} %constant_dynamic-update-slice_fusion.refs_2_), channel_id=1, source_target_pairs={{0,1},{1,0},{2,3},{3,2},{4,5},{5,4},{6,7},{7,6},{8,9},{9,8},{10,11... | collective-permute-start | bytes 405512 | tf_op jit(solution)/shard_map/ppermute | solution.py:15
  26.2 2.5 %collective-permute-done.2.refs_0_ = bf16[16,4224]{1,0:T(8,128)(2,1)S(1)} collective-permute-done((bf16[16,4224]{1,0:T(8,128)(2,1)S(1)}, bf16[16,4224]{1,0:T(8,128)(2,1)S(1)}, u32[]{:S(2)}, u32[]{:S(2)}) %collective-permute-start.2) | collective-permute-done | bytes 135200 | tf_op jit(solution)/shard_map/ppermute | solution.py:15
  28.6 2.8 %collective-permute-done.3.refs_1_ = bf16[16,4224]{1,0:T(8,128)(2,1)S(1)} collective-permute-done((bf16[16,4224]{1,0:T(8,128)(2,1)S(1)}, bf16[16,4224]{1,0:T(8,128)(2,1)S(1)}, u32[]{:S(2)}, u32[]{:S(2)}) %collective-permute-start.3) | collective-permute-done | bytes 135200 | tf_op jit(solution)/shard_map/ppermute | solution.py:15
  31.5 0.4 %collective-permute-start.7 = (bf16[16,4224]{1,0:T(8,128)(2,1)S(1)}, bf16[16,4224]{1,0:T(8,128)(2,1)S(1)}, u32[]{:S(2)}, u32[]{:S(2)}) collective-permute-start(bf16[16,4224]{1,0:T(8,128)(2,1)S(1)} %collective-permute-done.4.refs_2_), channel_id=1, source_target_pairs={{0,4},{4,0},{1,5},{5,1},{2,6},{6,2},{3,7},{7,3},{8,12},{12,8},{9,1... | collective-permute-start | bytes 405512 | tf_op jit(solution)/shard_map/ppermute | solution.py:15
  31.9 1.5 %shard_map.82 = (f32[1536,128]{1,0:T(8,128)S(1)}, bf16[2048,192]{1,0:T(8,128)(2,1)S(1)}, bf16[4096,256]{1,0:T(8,128)(2,1)S(1)}, bf16[2,2048,128]{2,1,0:T(8,128)(2,1)S(1)}, bf16[1536,512]{1,0:T(8,128)(2,1)S(1)}) custom-call(bf16[32,4224]{1,0:T(8,128)(2,1)S(1)} %fusion.1.refs_0_, bf16[32,4224]{1,0:T(8,128)(2,1)S(1)} %collective-permute-done.8.refs_1_, ...), custom_call_target="tpu_custom_call" | custom-call | tf_op jit(solution)/shard_map/pallas_call | solution.py:246
  33.4 5.3 %shard_map.83 = f32[2,128,512]{2,1,0:T(8,128)} custom-call(bf16[16,4224]{1,0:T(8,128)(2,1)S(1)} %collective-permute-done.2.refs_0_, bf16[16,4224]{1,0:T(8,128)(2,1)S(1)} %collective-permute-done.3.refs_1_, bf16[16,4224]{1,0:T(8,128)(2,1)S(1)} %collective-permute-done.4.refs_2_, bf16[16,4224]{1,0:T(8,128)(2,1)S(1)} %collective-permute-done.5.refs_3_, ...), custom_call_target="tpu_custom_call" | custom-call | tf_op jit(solution)/shard_map/pallas_call | solution.py:254
  (30 shorter events, 0.4 us)
Async XLA Ops:
  0.7 32.7 %copy-start = (bf16[2,128,512]{2,1,0:T(8,128)(2,1)S(1)}, bf16[2,128,512]{2,1,0:T(8,128)(2,1)}, u32[]{:S(2)}) copy-start(bf16[2,128,512]{2,1,0:T(8,128)(2,1)} %refs_11_.1) | copy-start | bytes 786436
  0.7 32.7 %copy-start.1 = (f32[2]{0:T(128)S(1)}, f32[2]{0:T(128)}, u32[]{:S(2)}) copy-start(f32[2]{0:T(128)} %refs_12_.1) | copy-start | bytes 28
  2.5 8.2 %collective-permute-start = (bf16[8,4224]{1,0:T(8,128)(2,1)S(1)}, bf16[8,4224]{1,0:T(8,128)(2,1)S(1)}, u32[]{:S(2)}, u32[]{:S(2)}) collective-permute-start(bf16[8,4224]{1,0:T(8,128)(2,1)S(1)} %constant_dynamic-slice_fusion), channel_id=1, source_target_pairs={{0,24},{8,16},{16,8},{24,0},{1,25},{9,17},{17,9},{25,1},{2,26},{10... | collective-permute-start | bytes 202760 | tf_op jit(solution)/shard_map/ppermute | solution.py:15
  7.7 5.9 %collective-permute-start.1 = (bf16[8,4224]{1,0:T(8,128)(2,1)S(1)}, bf16[8,4224]{1,0:T(8,128)(2,1)S(1)}, u32[]{:S(2)}, u32[]{:S(2)}) collective-permute-start(bf16[8,4224]{1,0:T(8,128)(2,1)S(1)} %constant_dynamic-slice_fusion), channel_id=1, source_target_pairs={{0,16},{8,24},{16,0},{24,8},{1,17},{9,25},{17,1},{25,9},{2,18},{10... | collective-permute-start | bytes 202760 | tf_op jit(solution)/shard_map/ppermute | solution.py:15
  7.7 16.4 %collective-permute-start.8 = (bf16[32,4224]{1,0:T(8,128)(2,1)S(1)}, bf16[32,4224]{1,0:T(8,128)(2,1)S(1)}, u32[]{:S(2)}, u32[]{:S(2)}) collective-permute-start(bf16[32,4224]{1,0:T(8,128)(2,1)S(1)} %fusion.1.refs_0_), channel_id=1, source_target_pairs={{0,8},{8,0},{16,24},{24,16},{1,9},{9,1},{17,25},{25,17},{2,10},{10... | collective-permute-start | bytes 811016 | tf_op jit(solution)/shard_map/ppermute | solution.py:15
  8.3 1.4 %collective-permute-start.12 = (bf16[8,4,2,8]{3,2,1,0:T(2,128)(2,1)}, bf16[8,4,2,8]{3,2,1,0:T(2,128)(2,1)S(1)}, u32[]{:S(2)}, u32[]{:S(2)}) collective-permute-start(bf16[8,4,2,8]{3,2,1,0:T(2,128)(2,1)} %param.13), channel_id=1, source_target_pairs={{0,4},{4,0},{1,5},{5,1},{2,6},{6,2},{3,7},{7,3},{8,12},{12,8},{9,1... | collective-permute-start | bytes 3080 | tf_op jit(solution)/shard_map/ppermute | solution.py:15
  13.5 10.7 %collective-permute-start.11 = (bf16[16,4224]{1,0:T(8,128)(2,1)S(1)}, bf16[16,4224]{1,0:T(8,128)(2,1)S(1)}, u32[]{:S(2)}, u32[]{:S(2)}) collective-permute-start(bf16[16,4224]{1,0:T(8,128)(2,1)S(1)} %constant_dynamic-update-slice_fusion.refs_2_), channel_id=1, source_target_pairs={{0,4},{4,0},{1,5},{5,1},{2,6},{6,2},{3,7},{7,3},{8,12},{12,8},{9,1... | collective-permute-start | bytes 405512 | tf_op jit(solution)/shard_map/ppermute | solution.py:15
  13.7 5.4 %collective-permute-start.13 = (bf16[416,128]{1,0:T(8,128)(2,1)S(1)}, bf16[416,128]{1,0:T(8,128)(2,1)S(1)}, u32[]{:S(2)}, u32[]{:S(2)}) collective-permute-start(bf16[416,128]{1,0:T(8,128)(2,1)S(1)} %get-tuple-element.16), channel_id=1, source_target_pairs={{0,1},{1,0},{2,3},{3,2},{4,5},{5,4},{6,7},{7,6},{8,9},{9,8},{10,11... | collective-permute-start | bytes 319496 | tf_op jit(solution)/shard_map/ppermute | solution.py:15
  15.2 7.4 %collective-permute-start.14 = (bf16[416,128]{1,0:T(8,128)(2,1)S(1)}, bf16[416,128]{1,0:T(8,128)(2,1)S(1)}, u32[]{:S(2)}, u32[]{:S(2)}) collective-permute-start(bf16[416,128]{1,0:T(8,128)(2,1)S(1)} %get-tuple-element.17), channel_id=1, source_target_pairs={{0,2},{1,3},{2,0},{3,1},{4,6},{5,7},{6,4},{7,5},{8,10},{9,11},{10,... | collective-permute-start | bytes 319496 | tf_op jit(solution)/shard_map/ppermute | solution.py:15
  16.7 7.3 %collective-permute-start.15 = (bf16[416,128]{1,0:T(8,128)(2,1)S(1)}, bf16[416,128]{1,0:T(8,128)(2,1)S(1)}, u32[]{:S(2)}, u32[]{:S(2)}) collective-permute-start(bf16[416,128]{1,0:T(8,128)(2,1)S(1)} %get-tuple-element.15), channel_id=1, source_target_pairs={{0,3},{1,2},{2,1},{3,0},{4,7},{5,6},{6,5},{7,4},{8,11},{9,10},{10,... | collective-permute-start | bytes 319496 | tf_op jit(solution)/shard_map/ppermute | solution.py:15
  19.1 12.8 %collective-permute-start.9 = (bf16[32,4224]{1,0:T(8,128)(2,1)S(1)}, bf16[32,4224]{1,0:T(8,128)(2,1)S(1)}, u32[]{:S(2)}, u32[]{:S(2)}) collective-permute-start(bf16[32,4224]{1,0:T(8,128)(2,1)S(1)} %fusion.1.refs_0_), channel_id=1, source_target_pairs={{0,4},{4,0},{1,5},{5,1},{2,6},{6,2},{3,7},{7,3},{8,12},{12,8},{9,1... | collective-permute-start | bytes 811016 | tf_op jit(solution)/shard_map/ppermute | solution.py:15
  22.6 6.0 %collective-permute-start.2 = (bf16[16,4224]{1,0:T(8,128)(2,1)S(1)}, bf16[16,4224]{1,0:T(8,128)(2,1)S(1)}, u32[]{:S(2)}, u32[]{:S(2)}) collective-permute-start(bf16[16,4224]{1,0:T(8,128)(2,1)S(1)} %constant_dynamic-update-slice_fusion.refs_2_), channel_id=1, source_target_pairs={{0,3},{1,2},{2,1},{3,0},{4,7},{5,6},{6,5},{7,4},{8,11},{9,10},{10,... | collective-permute-start | bytes 405512 | tf_op jit(solution)/shard_map/ppermute | solution.py:15
  24.1 7.8 %collective-permute-start.10 = (bf16[32,4224]{1,0:T(8,128)(2,1)S(1)}, bf16[32,4224]{1,0:T(8,128)(2,1)S(1)}, u32[]{:S(2)}, u32[]{:S(2)}) collective-permute-start(bf16[32,4224]{1,0:T(8,128)(2,1)S(1)} %collective-permute-done.8.refs_1_), channel_id=1, source_target_pairs={{0,4},{4,0},{1,5},{5,1},{2,6},{6,2},{3,7},{7,3},{8,12},{12,8},{9,1... | collective-permute-start | bytes 811016 | tf_op jit(solution)/shard_map/ppermute | solution.py:15
  24.1 7.3 %collective-permute-start.3 = (bf16[16,4224]{1,0:T(8,128)(2,1)S(1)}, bf16[16,4224]{1,0:T(8,128)(2,1)S(1)}, u32[]{:S(2)}, u32[]{:S(2)}) collective-permute-start(bf16[16,4224]{1,0:T(8,128)(2,1)S(1)} %constant_dynamic-update-slice_fusion.refs_2_), channel_id=1, source_target_pairs={{0,2},{1,3},{2,0},{3,1},{4,6},{5,7},{6,4},{7,5},{8,10},{9,11},{10,... | collective-permute-start | bytes 405512 | tf_op jit(solution)/shard_map/ppermute | solution.py:15
  24.2 7.3 %collective-permute-start.4 = (bf16[16,4224]{1,0:T(8,128)(2,1)S(1)}, bf16[16,4224]{1,0:T(8,128)(2,1)S(1)}, u32[]{:S(2)}, u32[]{:S(2)}) collective-permute-start(bf16[16,4224]{1,0:T(8,128)(2,1)S(1)} %constant_dynamic-update-slice_fusion.refs_2_), channel_id=1, source_target_pairs={{0,1},{1,0},{2,3},{3,2},{4,5},{5,4},{6,7},{7,6},{8,9},{9,8},{10,11... | collective-permute-start | bytes 405512 | tf_op jit(solution)/shard_map/ppermute | solution.py:15
  28.6 4.8 %collective-permute-start.5 = (bf16[16,4224]{1,0:T(8,128)(2,1)S(1)}, bf16[16,4224]{1,0:T(8,128)(2,1)S(1)}, u32[]{:S(2)}, u32[]{:S(2)}) collective-permute-start(bf16[16,4224]{1,0:T(8,128)(2,1)S(1)} %collective-permute-done.2.refs_0_), channel_id=1, source_target_pairs={{0,4},{4,0},{1,5},{5,1},{2,6},{6,2},{3,7},{7,3},{8,12},{12,8},{9,1... | collective-permute-start | bytes 405512 | tf_op jit(solution)/shard_map/ppermute | solution.py:15
  31.4 2.0 %collective-permute-start.6 = (bf16[16,4224]{1,0:T(8,128)(2,1)S(1)}, bf16[16,4224]{1,0:T(8,128)(2,1)S(1)}, u32[]{:S(2)}, u32[]{:S(2)}) collective-permute-start(bf16[16,4224]{1,0:T(8,128)(2,1)S(1)} %collective-permute-done.3.refs_1_), channel_id=1, source_target_pairs={{0,4},{4,0},{1,5},{5,1},{2,6},{6,2},{3,7},{7,3},{8,12},{12,8},{9,1... | collective-permute-start | bytes 405512 | tf_op jit(solution)/shard_map/ppermute | solution.py:15
  31.5 1.9 %collective-permute-start.7 = (bf16[16,4224]{1,0:T(8,128)(2,1)S(1)}, bf16[16,4224]{1,0:T(8,128)(2,1)S(1)}, u32[]{:S(2)}, u32[]{:S(2)}) collective-permute-start(bf16[16,4224]{1,0:T(8,128)(2,1)S(1)} %collective-permute-done.4.refs_2_), channel_id=1, source_target_pairs={{0,4},{4,0},{1,5},{5,1},{2,6},{6,2},{3,7},{7,3},{8,12},{12,8},{9,1... | collective-permute-start | bytes 405512 | tf_op jit(solution)/shard_map/ppermute | solution.py:15

commit v2 on v1

--- a/solution.py
+++ b/solution.py
@@ -6,6 +6,7 @@
 from jax.experimental.pallas import tpu as pltpu
 from jax.sharding import PartitionSpec as P
 
+
 LANES = 128
 VMEM_BYTES = 28 * 1024 * 1024
 
@@ -22,6 +23,40 @@
 def visit_codes(tags, visits, group_blocks):
     tags = tags.astype(jnp.float32)
     return tags[:, :visits] * group_blocks + tags[:, visits : 2 * visits]
+
+
+def pack_kernel(patch_ref, dest_ref, block_ref, row_ref, col_ref, weight_ref, *refs):
+    own_ref, row_out, col_out, weight_out, tag_buf, sems = refs
+    width = patch_ref.shape[1]
+    patch_count = patch_ref.shape[0]
+    visits = dest_ref.shape[0]
+    pairs = (
+        (dest_ref, tag_buf.at[0]),
+        (block_ref, tag_buf.at[1]),
+        (patch_ref, own_ref.at[:, :width]),
+        (row_ref, row_out),
+        (col_ref, col_out),
+        (weight_ref, weight_out),
+    )
+    copies = [pltpu.make_async_copy(src, dst, sems.at[i]) for i, (src, dst) in enumerate(pairs)]
+    for copy in copies:
+        copy.start()
+    copies[0].wait()
+    copies[1].wait()
+    tags = jnp.concatenate([tag_buf[0], tag_buf[1]], axis=0).astype(jnp.float32)
+    tags = jnp.concatenate([tags, jnp.zeros((2 * visits, LANES - patch_count), jnp.float32)], axis=1)
+    tags = jnp.concatenate([tags, jnp.zeros((LANES - 2 * visits, LANES), jnp.float32)], axis=0)
+    own_ref[:, width:] = tags.T[:patch_count].astype(jnp.bfloat16)
+    for copy in copies[2:]:
+        copy.wait()
+
+
+def parcel_kernel(row_ref, col_ref, maps_ref):
+    kinds_local, _, rows = row_ref.shape
+    for k in range(kinds_local):
+        both = jnp.concatenate([row_ref[k].astype(jnp.float32), col_ref[k].astype(jnp.float32)], axis=0)
+        both = jnp.concatenate([both, jnp.zeros((LANES, LANES - rows), jnp.float32)], axis=1)
+        maps_ref[k * rows : (k + 1) * rows, :] = both.T[:rows].astype(jnp.bfloat16)
 
 
 def picks(tags, dims, places):
@@ -59,11 +94,9 @@
 
 
 def early_kernel(dims, width, block, kinds_local, *refs):
-    chunk_count = 6
-    chunks = refs[:chunk_count]
-    parcels = refs[chunk_count:-5]
+    chunks, parcels, (table_ref, other_ref) = refs[:6], refs[6:-7], refs[-7:-5]
     sums_ref, rows_ref, main_ref, edge_ref, wide_ref = refs[-5:]
-    visits, group_blocks, per_exp, col_grid, band_grid, strips, exp_local, rows_axis = dims
+    _, group_blocks, per_exp, col_grid, band_grid, strips, exp_local, _ = dims
     blocks = exp_local * strips * col_grid
     summed_into(sums_ref, chunks, None, dims, width, blocks)
     band = lax.axis_index("row")
@@ -114,26 +147,32 @@
                 edge_ref[1, k * LANES : k * LANES + block, :] = jnp.zeros((block, LANES), jnp.bfloat16)
             at = k * 4 * block + b * block
             main_ref[at : at + block, :] = kept.astype(jnp.bfloat16)
-    src = lax.broadcasted_iota(jnp.int32, (LANES, col_grid * block), 0)
-    dst = lax.broadcasted_iota(jnp.int32, (LANES, col_grid * block), 1)
-    spread = jnp.where(src == dst // block, 1.0, 0.0).astype(jnp.bfloat16)
-    for p, parcel in enumerate(parcels):
-        table = parcel[kinds_local * out_rows :, :]
-        lines = jnp.dot(table, spread, preferred_element_type=jnp.float32)
-        for x in range(exp_local):
-            for s in range(strips):
-                for kl in range(kinds_local):
-                    line = (x * (strips + 1) + s) * kinds_local + kl
-                    wide = jnp.broadcast_to(lines[line : line + 1], (16, col_grid * block))
-                    at = ((x * kinds + p * kinds_local + kl) * strips + s) * 16
-                    wide_ref[at : at + 16, :] = wide.astype(jnp.bfloat16)
+    pair = (table_ref[...], other_ref[...])
+    table = jnp.concatenate(
+        [jnp.where(band == 0, pair[0], pair[1]), jnp.where(band == 0, pair[1], pair[0])], axis=1
+    )
+    src = lax.broadcasted_iota(jnp.int32, (table.shape[1], col_grid * block), 0)
+    dst = lax.broadcasted_iota(jnp.int32, (table.shape[1], col_grid * block), 1)
+    ahead = src - dst // block
+    first_exp = lax.axis_index("basis") * exp_local
+    exp_group = group_blocks // per_exp
+    for x in range(exp_local):
+        for s in range(strips):
+            block_row = band * (band_grid - 1) + s
+            line = (block_row // band_grid * exp_group + first_exp + x) * band_grid + block_row % band_grid
+            spread = jnp.where(ahead == line * col_grid, 1.0, 0.0).astype(jnp.bfloat16)
+            lines = jnp.dot(table, spread, preferred_element_type=jnp.float32)
+            for k in range(kinds):
+                wide = jnp.broadcast_to(lines[k : k + 1], (16, col_grid * block))
+                at = ((x * kinds + k) * strips + s) * 16
+                wide_ref[at : at + 16, :] = wide.astype(jnp.bfloat16)
 
 
 def late_kernel(dims, width, block, kinds, *refs):
     chunks = refs[:6]
     (before_ref, rows_ref, main_ref, edge_ref, wide_ref, obs_ref, inv_ref, out_ref) = refs[6:14]
     sums_ref, image_ref, mid_ref, side_ref = refs[14:]
-    visits, group_blocks, per_exp, col_grid, band_grid, strips, exp_local, rows_axis = dims
+    _, _, _, col_grid, band_grid, strips, exp_local, _ = dims
     blocks = exp_local * strips * col_grid
     summed_into(sums_ref, chunks, before_ref, dims, width, blocks)
     half = block // 2
@@ -198,44 +237,68 @@
     per_exp = band_grid * col_grid
     group_blocks = exp_group * per_exp
     kinds = kinds_local * n_basis
-    basis, band = lax.axis_index("basis"), lax.axis_index("row")
+    basis = lax.axis_index("basis")
     dims = (visits, group_blocks, per_exp, col_grid, band_grid, strips, exp_local, n_row)
     blocks = exp_local * strips * col_grid
 
-    tags = jnp.concatenate([visit_dest, visit_block], axis=1).astype(jnp.bfloat16)
-    tags = jnp.pad(tags, ((0, 0), (0, LANES - 2 * visits)))
-    own = jnp.concatenate([scene_patches, tags], axis=1)
+    f32, bf16 = jnp.float32, jnp.bfloat16
+    params = pltpu.CompilerParams(vmem_limit_bytes=VMEM_BYTES)
+    packed = (
+        scene_patches,
+        visit_dest.T,
+        visit_block.T,
+        jnp.swapaxes(row_maps, 1, 2),
+        jnp.swapaxes(col_maps, 1, 2),
+        psf_weights,
+    )
+    own, row_now, col_now, weights_now = pl.pallas_call(
+        pack_kernel,
+        out_shape=[
+            jax.ShapeDtypeStruct((patch_count, width + LANES), bf16),
+            jax.ShapeDtypeStruct((kinds_local, block, out_width), bf16),
+            jax.ShapeDtypeStruct((kinds_local, block, out_width), bf16),
+            jax.ShapeDtypeStruct(psf_weights.shape, bf16),
+        ],
+        in_specs=[pl.BlockSpec(memory_space=pltpu.HBM)] * 6,
+        out_specs=in_vmem(4),
+        scratch_shapes=[pltpu.VMEM((2, visits, patch_count), jnp.int32), pltpu.SemaphoreType.DMA((6,))],
+        compiler_params=params,
+    )(*(pltpu.with_memory_space_constraint(v, pltpu.HBM) for v in packed))
     part = patch_count // n_basis
     own_part = lax.dynamic_slice_in_dim(own, basis * part, part, 0)
-
-    far = [swapped(own_part, "exp", s) for s in range(n_exp - 1, 1, -1)]
+    far = []
+    for s in range(n_exp - 1, 1, -1):
+        far.append(swapped(own_part, "exp", s))
     near = swapped(own, "exp", 1)
+    maps = pl.pallas_call(
+        parcel_kernel,
+        out_shape=jax.ShapeDtypeStruct((kinds_local * out_width, LANES), bf16),
+        in_specs=in_vmem(2),
+        out_specs=in_vmem(1)[0],
+        compiler_params=params,
+    )(row_now, col_now)
+    table = jnp.swapaxes(weights_now, 0, 1).reshape(kinds_local, -1)
+    table = jnp.pad(table, ((0, 16 - kinds_local), (0, 0)))
+    maps = jnp.concatenate([maps, table], axis=0)
+    parcels = [maps]
+    for s in range(1, n_basis):
+        parcels.append(swapped(maps, "basis", s))
     own_other = swapped(own, "row", 1)
-
-    weights_other = swapped(psf_weights, "row", 1)
-    weights = jnp.where(
-        band == 0,
-        jnp.concatenate([psf_weights, weights_other[:, :, :1]], axis=2),
-        jnp.concatenate([weights_other[:, :, band_grid - 1 :], psf_weights], axis=2),
-    )
-    weights = jnp.pad(jnp.swapaxes(weights, 1, 2), ((0, 0), (0, 1), (0, 0), (0, LANES - col_grid)))
-    weights = weights.reshape(n_basis, -1, LANES)
-    maps = jnp.concatenate([row_maps, col_maps], axis=2).reshape(-1, LANES)
-    parcels = []
-    for s in range(n_basis):
-        table = lax.dynamic_index_in_dim(weights, basis ^ s, 0, keepdims=False)
-        parcel = jnp.concatenate([maps, table], axis=0)
-        parcels.append(swapped(parcel, "basis", s) if s else parcel)
-
     far = jnp.concatenate(far, axis=0)
-    spread = [swapped(far, "basis", s) for s in range(n_basis - 1, 0, -1)]
+    spread = []
+    for s in range(n_basis - 1, 0, -1):
+        spread.append(swapped(far, "basis", s))
     near_other = swapped(near, "row", 1)
     far_other = swapped(far, "row", 1)
-    spread_other = [swapped(v, "row", 1) for v in spread]
-
-    f32, bf16 = jnp.float32, jnp.bfloat16
-    params = pltpu.CompilerParams(vmem_limit_bytes=VMEM_BYTES)
-    early = [own, near, far, own_other, near_other, far_other] + parcels
+    table = jnp.concatenate(
+        [p[kinds_local * out_width : kinds_local * out_width + kinds_local] for p in parcels], axis=0
+    )
+    table_other = swapped(table, "row", 1)
+    spread_other = []
+    for s, v in zip(range(n_basis - 1, 0, -1), spread):
+        spread_other.append(swapped(v, "row", 1))
+
+    early = [own, near, far, own_other, near_other, far_other] + parcels + [table, table_other]
     shapes = [
         jax.ShapeDtypeStruct((width // LANES * blocks, LANES), f32),
         jax.ShapeDtypeStruct((kinds * band_rows, strips * block), bf16),
@@ -243,14 +306,15 @@
         jax.ShapeDtypeStruct((2, kinds * LANES, LANES), bf16),
         jax.ShapeDtypeStruct((exp_local * kinds * strips * 16, tile_cols), bf16),
     ]
-    tables = pl.pallas_call(
+    early_call = pl.pallas_call(
         functools.partial(early_kernel, dims, width, block, kinds_local),
         out_shape=shapes,
         in_specs=in_vmem(len(early)),
         out_specs=in_vmem(len(shapes)),
         compiler_params=params,
-    )(*early)
-    late = spread + spread_other + list(tables) + [observed]
+    )
+    prepared = early_call(*early)
+    late = spread + spread_other + list(prepared) + [observed]
     return pl.pallas_call(
         functools.partial(late_kernel, dims, width, block, kinds),
         out_shape=jax.ShapeDtypeStruct(observed.shape, f32),
@@ -321,7 +385,7 @@
     patch_count, visit_count = visit_dest.shape
     capacity = max(2, 2 * patch_count * visit_count // group_size)
     exp_local, band_rows, tile_cols = observed.shape
-    exp_group, kind_count, block_grid, col_grid = psf_weights.shape
+    _, _, block_grid, col_grid = psf_weights.shape
     block_size = row_maps.shape[2]
     spill_rows = (row_maps.shape[1] - block_size) // 2
     per_exposure = block_grid * col_grid
@@ -375,31 +439,35 @@
 def gathers(mesh, patch_count, visits):
     n_exp, n_row, n_basis = mesh.shape["exp"], mesh.shape["row"], mesh.shape["basis"]
     capacity = max(2, 2 * patch_count * visits // (n_exp * n_row))
-    powers = all(n & (n - 1) == 0 for n in (n_exp, n_basis)) and n_exp > 2
+    powers = all(n & (n - 1) == 0 for n in (n_exp, n_basis)) and n_exp > 2 and n_basis > 2
     return capacity >= patch_count and powers and n_row == 2 and patch_count % (8 * n_basis) == 0
 
 
-def per_device(mesh, *arrays):
-    patch_count, visits = arrays[1].shape
-    if gathers(mesh, patch_count, visits):
-        return gathered_device(*arrays)
-    return exchanged_device(*arrays)
+def in_layer(*arrays):
+    return gathered_device(*arrays)
 
 
 def solution(mesh):
-    return jax.shard_map(
-        functools.partial(per_device, mesh),
-        mesh=mesh,
-        in_specs=(
-            P(("exp", "row"), None),
-            P(("exp", "row"), None),
-            P(("exp", "row"), None),
-            P("basis", None, None),
-            P("basis", None, None),
-            P("exp", "basis", "row", None),
-            P(("exp", "basis")),
-            P(("exp", "basis"), "row", None),
-        ),
-        out_specs=P(("exp", "basis"), "row", None),
-        check_vma=False,
-    )
+    def step(*arrays):
+        patch_total, visits = arrays[1].shape
+        patch_count = patch_total // (mesh.shape["exp"] * mesh.shape["row"])
+        gather = gathers(mesh, patch_count, visits)
+        sharded = jax.shard_map(
+            in_layer if gather else exchanged_device,
+            mesh=mesh,
+            in_specs=(
+                P(("exp", "row"), None),
+                P(("exp", "row"), None),
+                P(("exp", "row"), None),
+                P("basis", None, None),
+                P("basis", None, None),
+                P("exp", "basis", "row", None),
+                P(("exp", "basis")),
+                P(("exp", "basis"), "row", None),
+            ),
+            out_specs=P(("exp", "basis"), "row", None),
+            check_vma=False,
+        )
+        return sharded(*arrays)
+
+    return step

time: 39 us -> 33.6 us (0.86)
  waiting for transfers between devices: 13.8 us -> 9.37 us
  other arithmetic: 4.24 us -> 0.02 us
  starting transfers between devices: 13.5 us -> 15.8 us
  Pallas kernels: 6.79 us -> 8.03 us
    ppermute x16, waiting for transfers between devices: 13.8 us -> 9.37 us  [swapped(): return lax.ppermute(value, axis, [(i, i ^ by) for i in range(length)])]
    ppermute x16, starting transfers between devices: 13.5 us -> 15.8 us  [swapped(): return lax.ppermute(value, axis, [(i, i ^ by) for i in range(length)])]
    concatenate x4 -> x2, other arithmetic: 1.94 us -> 0.02 us  [the longest x1 0.01 us: gathered_device(): jnp.concatenate([p[kinds_local * out_width:kinds_local * out_width + kind...]
    pallas_call x1 -> x3, Pallas kernels: 1.46 us -> 2.99 us  [the longest x1 1.81 us: gathered_device(): prepared = early_call(*early)]
    another operation x2 -> x0, other arithmetic: 1.41 us -> none
    transpose x1 -> x0, other arithmetic: 0.89 us -> none  [gathered_device(): jnp.swapaxes(weights, 1, 2)]
  transfers between devices with their start and end apart: 16 -> 16, of which waited for: 6 -> 3; matrix products, arithmetic and copies ran while one was open for 5% -> 0% of each run, Pallas kernels for 4% -> 6%
where the time goes in v2:
time: 33.6 us; the launch traced here: 33.5 us
  starting transfers between devices  15.8 us (47%)
  waiting for transfers between devices  9.37 us (28%)
  Pallas kernels  8.03 us (24%)
    ppermute x16, starting transfers between devices, swapped(): return lax.ppermute(value, axis, [(i, i ^ by) for i in range(length)])  15.8 us
    ppermute x16, waiting for transfers between devices, swapped(): return lax.ppermute(value, axis, [(i, i ^ by) for i in range(length)])  9.37 us
    pallas_call x1, Pallas kernels, gathered_device(): pl.pallas_call(functools.partial(late_kernel, dims, width, block, kinds),...  5.04 us
    pallas_call x1, Pallas kernels, gathered_device(): prepared = early_call(*early)  1.81 us
    pallas_call x1, Pallas kernels, gathered_device(): pl.pallas_call(pack_kernel, out_shape=[jax.ShapeDtypeStruct((patch_count,...  1.08 us
  transfers between devices with their start and end apart: 16, of which 3 were waited for; matrix products, arithmetic and copies ran while one was open for 0% of the time, Pallas kernels for 6%

profile of v2, /device:TPU:0, one launch (start us, length us, event | category | flops | bytes accessed | tf_op | source)
XLA Modules:
  0.0 33.5 jit_solution(3323213631884481062)
XLA Ops:
  0.0 1.1 %shard_map.82 = (bf16[32,4224]{1,0:T(8,128)(2,1)S(1)}, bf16[4,64,96]{2,1,0:T(8,128)(2,1)S(1)}, bf16[4,64,96]{2,1,0:T(8,128)(2,1)S(1)}, bf16[8,4,2,8]{3,2,1,0:T(2,128)(2,1)S(1)}) custom-call(bf16[32,4096]{1,0:T(8,128)(2,1)} %patch_ref.1, s32[4,32]{1,0:T(4,128)} %bitcast.8, s32[4,32]{1,0:T(4,128)} %bitcast.9, bf16[4,64,96]{2,1,0:T(8,128)(2,1)} %bitcast.6, ...), custom_call_target="tpu_custom_call" | custom-call | tf_op jit(solution)/shard_map/pallas_call | solution.py:254
  1.1 5.1 %collective-permute-start = (bf16[8,4224]{1,0:T(8,128)(2,1)S(1)}, bf16[8,4224]{1,0:T(8,128)(2,1)S(1)}, u32[]{:S(2)}, u32[]{:S(2)}) collective-permute-start(bf16[8,4224]{1,0:T(8,128)(2,1)S(1)} %constant_dynamic-slice_fusion), channel_id=1, source_target_pairs={{0,24},{8,16},{16,8},{24,0},{1,25},{9,17},{17,9},{25,1},{2,26},{10... | collective-permute-start | bytes 202760 | tf_op jit(solution)/shard_map/ppermute | solution.py:16
  6.3 0.1 reshape.3
  6.4 0.1 shard_map.83
  6.5 1.6 %collective-permute-start.12 = (bf16[400,128]{1,0:T(8,128)(2,1)S(1)}, bf16[400,128]{1,0:T(8,128)(2,1)S(1)}, u32[]{:S(2)}, u32[]{:S(2)}) collective-permute-start(bf16[400,128]{1,0:T(8,128)(2,1)S(1)} %fusion.1.refs_6_), channel_id=1, source_target_pairs={{0,1},{1,0},{2,3},{3,2},{4,5},{5,4},{6,7},{7,6},{8,9},{9,8},{10,11... | collective-permute-start | bytes 307208 | tf_op jit(solution)/shard_map/ppermute | solution.py:16
  8.1 1.5 %collective-permute-start.13 = (bf16[400,128]{1,0:T(8,128)(2,1)S(1)}, bf16[400,128]{1,0:T(8,128)(2,1)S(1)}, u32[]{:S(2)}, u32[]{:S(2)}) collective-permute-start(bf16[400,128]{1,0:T(8,128)(2,1)S(1)} %fusion.1.refs_6_), channel_id=1, source_target_pairs={{0,2},{1,3},{2,0},{3,1},{4,6},{5,7},{6,4},{7,5},{8,10},{9,11},{10,... | collective-permute-start | bytes 307208 | tf_op jit(solution)/shard_map/ppermute | solution.py:16
  9.6 0.5 %collective-permute-start.14 = (bf16[400,128]{1,0:T(8,128)(2,1)S(1)}, bf16[400,128]{1,0:T(8,128)(2,1)S(1)}, u32[]{:S(2)}, u32[]{:S(2)}) collective-permute-start(bf16[400,128]{1,0:T(8,128)(2,1)S(1)} %fusion.1.refs_6_), channel_id=1, source_target_pairs={{0,3},{1,2},{2,1},{3,0},{4,7},{5,6},{6,5},{7,4},{8,11},{9,10},{10,... | collective-permute-start | bytes 307208 | tf_op jit(solution)/shard_map/ppermute | solution.py:16
  10.1 0.0 collective-permute-start.1
  10.1 0.0 collective-permute-done
  10.1 0.6 %collective-permute-start.8 = (bf16[32,4224]{1,0:T(8,128)(2,1)S(1)}, bf16[32,4224]{1,0:T(8,128)(2,1)S(1)}, u32[]{:S(2)}, u32[]{:S(2)}) collective-permute-start(bf16[32,4224]{1,0:T(8,128)(2,1)S(1)} %get-tuple-element.14.refs_0_), channel_id=1, source_target_pairs={{0,8},{8,0},{16,24},{24,16},{1,9},{9,1},{17,25},{25,17},{2,10},{10... | collective-permute-start | bytes 811016 | tf_op jit(solution)/shard_map/ppermute | solution.py:16
  10.6 4.9 %collective-permute-done.1 = bf16[8,4224]{1,0:T(8,128)(2,1)S(1)} collective-permute-done((bf16[8,4224]{1,0:T(8,128)(2,1)S(1)}, bf16[8,4224]{1,0:T(8,128)(2,1)S(1)}, u32[]{:S(2)}, u32[]{:S(2)}) %collective-permute-start.1) | collective-permute-done | bytes 67616 | tf_op jit(solution)/shard_map/ppermute | solution.py:16
  15.6 0.1 collective-permute-start.11
  15.7 0.5 %collective-permute-start.15 = (bf16[16,128]{1,0:T(8,128)(2,1)S(1)}, bf16[16,128]{1,0:T(8,128)(2,1)S(1)}, u32[]{:S(2)}, u32[]{:S(2)}) collective-permute-start(bf16[16,128]{1,0:T(8,128)(2,1)S(1)} %pad_maximum_fusion.refs_10_), channel_id=1, source_target_pairs={{0,4},{4,0},{1,5},{5,1},{2,6},{6,2},{3,7},{7,3},{8,12},{12,8},{9,1... | collective-permute-start | bytes 12296 | tf_op jit(solution)/shard_map/ppermute | solution.py:16
  16.3 0.1 collective-permute-start.9
  16.3 2.4 %collective-permute-start.2 = (bf16[16,4224]{1,0:T(8,128)(2,1)S(1)}, bf16[16,4224]{1,0:T(8,128)(2,1)S(1)}, u32[]{:S(2)}, u32[]{:S(2)}) collective-permute-start(bf16[16,4224]{1,0:T(8,128)(2,1)S(1)} %constant_dynamic-update-slice_fusion.refs_2_), channel_id=1, source_target_pairs={{0,3},{1,2},{2,1},{3,0},{4,7},{5,6},{6,5},{7,4},{8,11},{9,10},{10,... | collective-permute-start | bytes 405512 | tf_op jit(solution)/shard_map/ppermute | solution.py:16
  18.8 0.2 collective-permute-start.10
  19.0 1.2 %collective-permute-start.3 = (bf16[16,4224]{1,0:T(8,128)(2,1)S(1)}, bf16[16,4224]{1,0:T(8,128)(2,1)S(1)}, u32[]{:S(2)}, u32[]{:S(2)}) collective-permute-start(bf16[16,4224]{1,0:T(8,128)(2,1)S(1)} %constant_dynamic-update-slice_fusion.refs_2_), channel_id=1, source_target_pairs={{0,2},{1,3},{2,0},{3,1},{4,6},{5,7},{6,4},{7,5},{8,10},{9,11},{10,... | collective-permute-start | bytes 405512 | tf_op jit(solution)/shard_map/ppermute | solution.py:16
  20.1 1.5 %collective-permute-start.4 = (bf16[16,4224]{1,0:T(8,128)(2,1)S(1)}, bf16[16,4224]{1,0:T(8,128)(2,1)S(1)}, u32[]{:S(2)}, u32[]{:S(2)}) collective-permute-start(bf16[16,4224]{1,0:T(8,128)(2,1)S(1)} %constant_dynamic-update-slice_fusion.refs_2_), channel_id=1, source_target_pairs={{0,1},{1,0},{2,3},{3,2},{4,5},{5,4},{6,7},{7,6},{8,9},{9,8},{10,11... | collective-permute-start | bytes 405512 | tf_op jit(solution)/shard_map/ppermute | solution.py:16
  21.6 1.6 %collective-permute-done.2.refs_0_ = bf16[16,4224]{1,0:T(8,128)(2,1)S(1)} collective-permute-done((bf16[16,4224]{1,0:T(8,128)(2,1)S(1)}, bf16[16,4224]{1,0:T(8,128)(2,1)S(1)}, u32[]{:S(2)}, u32[]{:S(2)}) %collective-permute-start.2) | collective-permute-done | bytes 135200 | tf_op jit(solution)/shard_map/ppermute | solution.py:16
  23.3 2.8 %collective-permute-done.3.refs_1_ = bf16[16,4224]{1,0:T(8,128)(2,1)S(1)} collective-permute-done((bf16[16,4224]{1,0:T(8,128)(2,1)S(1)}, bf16[16,4224]{1,0:T(8,128)(2,1)S(1)}, u32[]{:S(2)}, u32[]{:S(2)}) %collective-permute-start.3) | collective-permute-done | bytes 135200 | tf_op jit(solution)/shard_map/ppermute | solution.py:16
  26.1 0.1 collective-permute-start.6
  26.1 0.5 %collective-permute-start.7 = (bf16[16,4224]{1,0:T(8,128)(2,1)S(1)}, bf16[16,4224]{1,0:T(8,128)(2,1)S(1)}, u32[]{:S(2)}, u32[]{:S(2)}) collective-permute-start(bf16[16,4224]{1,0:T(8,128)(2,1)S(1)} %collective-permute-done.4.refs_2_), channel_id=1, source_target_pairs={{0,4},{4,0},{1,5},{5,1},{2,6},{6,2},{3,7},{7,3},{8,12},{12,8},{9,1... | collective-permute-start | bytes 405512 | tf_op jit(solution)/shard_map/ppermute | solution.py:16
  26.6 1.8 %shard_map.84 = (f32[1536,128]{1,0:T(8,128)S(1)}, bf16[2048,192]{1,0:T(8,128)(2,1)S(1)}, bf16[4096,256]{1,0:T(8,128)(2,1)S(1)}, bf16[2,2048,128]{2,1,0:T(8,128)(2,1)S(1)}, bf16[1536,512]{1,0:T(8,128)(2,1)S(1)}) custom-call(bf16[32,4224]{1,0:T(8,128)(2,1)S(1)} %get-tuple-element.14.refs_0_, bf16[32,4224]{1,0:T(8,128)(2,1)S(1)} %collective-permute-done.8.refs_1_, ...), custom_call_target="tpu_custom_call" | custom-call | tf_op jit(solution)/shard_map/pallas_call | solution.py:316
  28.5 5.0 %shard_map.85 = f32[2,128,512]{2,1,0:T(8,128)} custom-call(bf16[16,4224]{1,0:T(8,128)(2,1)S(1)} %collective-permute-done.2.refs_0_, bf16[16,4224]{1,0:T(8,128)(2,1)S(1)} %collective-permute-done.3.refs_1_, bf16[16,4224]{1,0:T(8,128)(2,1)S(1)} %collective-permute-done.4.refs_2_, bf16[16,4224]{1,0:T(8,128)(2,1)S(1)} %collective-permute-done.5.refs_3_, ...), custom_call_target="tpu_custom_call" | custom-call | tf_op jit(solution)/shard_map/pallas_call | solution.py:318
  (26 shorter events, 0.1 us)
Async XLA Ops:
  0.0 28.4 %copy-start.1 = (f32[2]{0:T(128)S(1)}, f32[2]{0:T(128)}, u32[]{:S(2)}) copy-start(f32[2]{0:T(128)} %refs_12_.1) | copy-start | bytes 28
  0.0 28.4 %copy-start = (bf16[2,128,512]{2,1,0:T(8,128)(2,1)S(1)}, bf16[2,128,512]{2,1,0:T(8,128)(2,1)}, u32[]{:S(2)}) copy-start(bf16[2,128,512]{2,1,0:T(8,128)(2,1)} %refs_11_.1) | copy-start | bytes 786436
  1.1 8.9 %collective-permute-start = (bf16[8,4224]{1,0:T(8,128)(2,1)S(1)}, bf16[8,4224]{1,0:T(8,128)(2,1)S(1)}, u32[]{:S(2)}, u32[]{:S(2)}) collective-permute-start(bf16[8,4224]{1,0:T(8,128)(2,1)S(1)} %constant_dynamic-slice_fusion), channel_id=1, source_target_pairs={{0,24},{8,16},{16,8},{24,0},{1,25},{9,17},{17,9},{25,1},{2,26},{10... | collective-permute-start | bytes 202760 | tf_op jit(solution)/shard_map/ppermute | solution.py:16
  6.5 9.1 %collective-permute-start.12 = (bf16[400,128]{1,0:T(8,128)(2,1)S(1)}, bf16[400,128]{1,0:T(8,128)(2,1)S(1)}, u32[]{:S(2)}, u32[]{:S(2)}) collective-permute-start(bf16[400,128]{1,0:T(8,128)(2,1)S(1)} %fusion.1.refs_6_), channel_id=1, source_target_pairs={{0,1},{1,0},{2,3},{3,2},{4,5},{5,4},{6,7},{7,6},{8,9},{9,8},{10,11... | collective-permute-start | bytes 307208 | tf_op jit(solution)/shard_map/ppermute | solution.py:16
  8.1 7.6 %collective-permute-start.13 = (bf16[400,128]{1,0:T(8,128)(2,1)S(1)}, bf16[400,128]{1,0:T(8,128)(2,1)S(1)}, u32[]{:S(2)}, u32[]{:S(2)}) collective-permute-start(bf16[400,128]{1,0:T(8,128)(2,1)S(1)} %fusion.1.refs_6_), channel_id=1, source_target_pairs={{0,2},{1,3},{2,0},{3,1},{4,6},{5,7},{6,4},{7,5},{8,10},{9,11},{10,... | collective-permute-start | bytes 307208 | tf_op jit(solution)/shard_map/ppermute | solution.py:16
  9.6 6.1 %collective-permute-start.14 = (bf16[400,128]{1,0:T(8,128)(2,1)S(1)}, bf16[400,128]{1,0:T(8,128)(2,1)S(1)}, u32[]{:S(2)}, u32[]{:S(2)}) collective-permute-start(bf16[400,128]{1,0:T(8,128)(2,1)S(1)} %fusion.1.refs_6_), channel_id=1, source_target_pairs={{0,3},{1,2},{2,1},{3,0},{4,7},{5,6},{6,5},{7,4},{8,11},{9,10},{10,... | collective-permute-start | bytes 307208 | tf_op jit(solution)/shard_map/ppermute | solution.py:16
  10.1 5.5 %collective-permute-start.1 = (bf16[8,4224]{1,0:T(8,128)(2,1)S(1)}, bf16[8,4224]{1,0:T(8,128)(2,1)S(1)}, u32[]{:S(2)}, u32[]{:S(2)}) collective-permute-start(bf16[8,4224]{1,0:T(8,128)(2,1)S(1)} %constant_dynamic-slice_fusion), channel_id=1, source_target_pairs={{0,16},{8,24},{16,0},{24,8},{1,17},{9,25},{17,1},{25,9},{2,18},{10... | collective-permute-start | bytes 202760 | tf_op jit(solution)/shard_map/ppermute | solution.py:16
  10.1 8.7 %collective-permute-start.8 = (bf16[32,4224]{1,0:T(8,128)(2,1)S(1)}, bf16[32,4224]{1,0:T(8,128)(2,1)S(1)}, u32[]{:S(2)}, u32[]{:S(2)}) collective-permute-start(bf16[32,4224]{1,0:T(8,128)(2,1)S(1)} %get-tuple-element.14.refs_0_), channel_id=1, source_target_pairs={{0,8},{8,0},{16,24},{24,16},{1,9},{9,1},{17,25},{25,17},{2,10},{10... | collective-permute-start | bytes 811016 | tf_op jit(solution)/shard_map/ppermute | solution.py:16
  15.6 4.6 %collective-permute-start.11 = (bf16[16,4224]{1,0:T(8,128)(2,1)S(1)}, bf16[16,4224]{1,0:T(8,128)(2,1)S(1)}, u32[]{:S(2)}, u32[]{:S(2)}) collective-permute-start(bf16[16,4224]{1,0:T(8,128)(2,1)S(1)} %constant_dynamic-update-slice_fusion.refs_2_), channel_id=1, source_target_pairs={{0,4},{4,0},{1,5},{5,1},{2,6},{6,2},{3,7},{7,3},{8,12},{12,8},{9,1... | collective-permute-start | bytes 405512 | tf_op jit(solution)/shard_map/ppermute | solution.py:16
  15.7 3.2 %collective-permute-start.15 = (bf16[16,128]{1,0:T(8,128)(2,1)S(1)}, bf16[16,128]{1,0:T(8,128)(2,1)S(1)}, u32[]{:S(2)}, u32[]{:S(2)}) collective-permute-start(bf16[16,128]{1,0:T(8,128)(2,1)S(1)} %pad_maximum_fusion.refs_10_), channel_id=1, source_target_pairs={{0,4},{4,0},{1,5},{5,1},{2,6},{6,2},{3,7},{7,3},{8,12},{12,8},{9,1... | collective-permute-start | bytes 12296 | tf_op jit(solution)/shard_map/ppermute | solution.py:16
  16.3 10.3 %collective-permute-start.9 = (bf16[32,4224]{1,0:T(8,128)(2,1)S(1)}, bf16[32,4224]{1,0:T(8,128)(2,1)S(1)}, u32[]{:S(2)}, u32[]{:S(2)}) collective-permute-start(bf16[32,4224]{1,0:T(8,128)(2,1)S(1)} %get-tuple-element.14.refs_0_), channel_id=1, source_target_pairs={{0,4},{4,0},{1,5},{5,1},{2,6},{6,2},{3,7},{7,3},{8,12},{12,8},{9,1... | collective-permute-start | bytes 811016 | tf_op jit(solution)/shard_map/ppermute | solution.py:16
  16.3 6.9 %collective-permute-start.2 = (bf16[16,4224]{1,0:T(8,128)(2,1)S(1)}, bf16[16,4224]{1,0:T(8,128)(2,1)S(1)}, u32[]{:S(2)}, u32[]{:S(2)}) collective-permute-start(bf16[16,4224]{1,0:T(8,128)(2,1)S(1)} %constant_dynamic-update-slice_fusion.refs_2_), channel_id=1, source_target_pairs={{0,3},{1,2},{2,1},{3,0},{4,7},{5,6},{6,5},{7,4},{8,11},{9,10},{10,... | collective-permute-start | bytes 405512 | tf_op jit(solution)/shard_map/ppermute | solution.py:16
  18.8 7.8 %collective-permute-start.10 = (bf16[32,4224]{1,0:T(8,128)(2,1)S(1)}, bf16[32,4224]{1,0:T(8,128)(2,1)S(1)}, u32[]{:S(2)}, u32[]{:S(2)}) collective-permute-start(bf16[32,4224]{1,0:T(8,128)(2,1)S(1)} %collective-permute-done.8.refs_1_), channel_id=1, source_target_pairs={{0,4},{4,0},{1,5},{5,1},{2,6},{6,2},{3,7},{7,3},{8,12},{12,8},{9,1... | collective-permute-start | bytes 811016 | tf_op jit(solution)/shard_map/ppermute | solution.py:16
  19.0 7.1 %collective-permute-start.3 = (bf16[16,4224]{1,0:T(8,128)(2,1)S(1)}, bf16[16,4224]{1,0:T(8,128)(2,1)S(1)}, u32[]{:S(2)}, u32[]{:S(2)}) collective-permute-start(bf16[16,4224]{1,0:T(8,128)(2,1)S(1)} %constant_dynamic-update-slice_fusion.refs_2_), channel_id=1, source_target_pairs={{0,2},{1,3},{2,0},{3,1},{4,6},{5,7},{6,4},{7,5},{8,10},{9,11},{10,... | collective-permute-start | bytes 405512 | tf_op jit(solution)/shard_map/ppermute | solution.py:16
  20.1 6.0 %collective-permute-start.4 = (bf16[16,4224]{1,0:T(8,128)(2,1)S(1)}, bf16[16,4224]{1,0:T(8,128)(2,1)S(1)}, u32[]{:S(2)}, u32[]{:S(2)}) collective-permute-start(bf16[16,4224]{1,0:T(8,128)(2,1)S(1)} %constant_dynamic-update-slice_fusion.refs_2_), channel_id=1, source_target_pairs={{0,1},{1,0},{2,3},{3,2},{4,5},{5,4},{6,7},{7,6},{8,9},{9,8},{10,11... | collective-permute-start | bytes 405512 | tf_op jit(solution)/shard_map/ppermute | solution.py:16
  23.3 5.1 %collective-permute-start.5 = (bf16[16,4224]{1,0:T(8,128)(2,1)S(1)}, bf16[16,4224]{1,0:T(8,128)(2,1)S(1)}, u32[]{:S(2)}, u32[]{:S(2)}) collective-permute-start(bf16[16,4224]{1,0:T(8,128)(2,1)S(1)} %collective-permute-done.2.refs_0_), channel_id=1, source_target_pairs={{0,4},{4,0},{1,5},{5,1},{2,6},{6,2},{3,7},{7,3},{8,12},{12,8},{9,1... | collective-permute-start | bytes 405512 | tf_op jit(solution)/shard_map/ppermute | solution.py:16
  26.1 2.4 %collective-permute-start.6 = (bf16[16,4224]{1,0:T(8,128)(2,1)S(1)}, bf16[16,4224]{1,0:T(8,128)(2,1)S(1)}, u32[]{:S(2)}, u32[]{:S(2)}) collective-permute-start(bf16[16,4224]{1,0:T(8,128)(2,1)S(1)} %collective-permute-done.3.refs_1_), channel_id=1, source_target_pairs={{0,4},{4,0},{1,5},{5,1},{2,6},{6,2},{3,7},{7,3},{8,12},{12,8},{9,1... | collective-permute-start | bytes 405512 | tf_op jit(solution)/shard_map/ppermute | solution.py:16
  26.1 2.3 %collective-permute-start.7 = (bf16[16,4224]{1,0:T(8,128)(2,1)S(1)}, bf16[16,4224]{1,0:T(8,128)(2,1)S(1)}, u32[]{:S(2)}, u32[]{:S(2)}) collective-permute-start(bf16[16,4224]{1,0:T(8,128)(2,1)S(1)} %collective-permute-done.4.refs_2_), channel_id=1, source_target_pairs={{0,4},{4,0},{1,5},{5,1},{2,6},{6,2},{3,7},{7,3},{8,12},{12,8},{9,1... | collective-permute-start | bytes 405512 | tf_op jit(solution)/shard_map/ppermute | solution.py:16

commit v3 on v2

--- a/solution.py
+++ b/solution.py
@@ -8,6 +8,7 @@
 
 
 LANES = 128
+TAGS_AT = 64
 VMEM_BYTES = 28 * 1024 * 1024
 
 
@@ -18,11 +19,6 @@
 
 def in_vmem(count):
     return [pl.BlockSpec(memory_space=pltpu.VMEM)] * count
-
-
-def visit_codes(tags, visits, group_blocks):
-    tags = tags.astype(jnp.float32)
-    return tags[:, :visits] * group_blocks + tags[:, visits : 2 * visits]
 
 
 def pack_kernel(patch_ref, dest_ref, block_ref, row_ref, col_ref, weight_ref, *refs):
@@ -46,23 +42,41 @@
     tags = jnp.concatenate([tag_buf[0], tag_buf[1]], axis=0).astype(jnp.float32)
     tags = jnp.concatenate([tags, jnp.zeros((2 * visits, LANES - patch_count), jnp.float32)], axis=1)
     tags = jnp.concatenate([tags, jnp.zeros((LANES - 2 * visits, LANES), jnp.float32)], axis=0)
-    own_ref[:, width:] = tags.T[:patch_count].astype(jnp.bfloat16)
+    tags = tags.T[:patch_count]
+    part = patch_count // lax.axis_size("basis")
+    pieces = [tags[at : at + part] for at in range(0, patch_count, part)]
+    every = pieces[0]
+    for i, piece in enumerate(pieces[1:], 1):
+        every = every + pltpu.roll(piece, 2 * visits * i, 1)
+    tags = jnp.concatenate([every + pltpu.roll(piece, TAGS_AT, 1) for piece in pieces], axis=0)
+    own_ref[:, width:] = tags.astype(jnp.bfloat16)
     for copy in copies[2:]:
         copy.wait()
 
 
 def parcel_kernel(row_ref, col_ref, maps_ref):
     kinds_local, _, rows = row_ref.shape
-    for k in range(kinds_local):
-        both = jnp.concatenate([row_ref[k].astype(jnp.float32), col_ref[k].astype(jnp.float32)], axis=0)
+    share = kinds_local // lax.axis_size("row")
+    first = lax.axis_index("row") * share
+    for i in range(share):
+        both = [ref[first + i].astype(jnp.float32) for ref in (row_ref, col_ref)]
+        both = jnp.concatenate(both, axis=0)
         both = jnp.concatenate([both, jnp.zeros((LANES, LANES - rows), jnp.float32)], axis=1)
-        maps_ref[k * rows : (k + 1) * rows, :] = both.T[:rows].astype(jnp.bfloat16)
-
-
-def picks(tags, dims, places):
+        maps_ref[i * rows : (i + 1) * rows, :] = both.T[:rows].astype(jnp.bfloat16)
+
+
+def stack_kernel(*refs):
+    *parts, out_ref = refs
+    at = 0
+    for part in parts:
+        out_ref[at : at + part.shape[0], :] = part[...]
+        at += part.shape[0]
+
+
+def picks(tags, dims):
     visits, group_blocks, per_exp, col_grid, band_grid, strips, exp_local, rows_axis = dims
-    group, band, basis = places
-    codes = visit_codes(tags, visits, group_blocks)
+    group, band, basis = lax.axis_index("exp"), lax.axis_index("row"), lax.axis_index("basis")
+    codes = tags[:, :visits] * group_blocks + tags[:, visits : 2 * visits]
     lane = lax.broadcasted_iota(jnp.int32, (1, LANES), 1)
     exp_at = lane // (strips * col_grid)
     strip = lane // col_grid % strips
@@ -73,14 +87,22 @@
     hit = jnp.zeros((tags.shape[0], LANES), jnp.float32)
     for v in range(visits):
         hit = hit + jnp.where(codes[:, v : v + 1] == want, 1.0, 0.0)
-    blocks = exp_local * strips * col_grid
-    return hit.T[:blocks].astype(jnp.bfloat16)
-
-
-def summed_into(out_ref, chunk_refs, before_ref, dims, width, blocks):
-    places = (lax.axis_index("exp"), lax.axis_index("row"), lax.axis_index("basis"))
-    tags = jnp.concatenate([ref[:, width:] for ref in chunk_refs], axis=0)
-    pick = picks(tags, dims, places)
+    return hit.T[: exp_local * strips * col_grid].astype(jnp.bfloat16)
+
+
+def tags_of(ref, width, lane):
+    return pltpu.roll(ref[:, width:].astype(jnp.float32), (LANES - lane) % LANES, 1)
+
+
+def pick_kernel(dims, width, sources, near_ref, near_other_ref, far_ref, far_other_ref, pick_ref):
+    tags = [tags_of(ref, width, TAGS_AT) for ref in (near_ref, near_other_ref)]
+    basis = lax.axis_index("basis")
+    for ref in (far_ref, far_other_ref):
+        tags += [tags_of(ref, width, (basis ^ s) * 2 * dims[0]) for s in range(sources - 1, 0, -1)]
+    pick_ref[...] = picks(jnp.concatenate(tags, axis=0), dims)
+
+
+def summed_into(out_ref, pick, chunk_refs, before_ref, width, blocks):
     step = 4 * LANES
     for start in range(0, width, step):
         rows = jnp.concatenate([ref[:, start : start + step] for ref in chunk_refs], axis=0)
@@ -93,15 +115,17 @@
             out_ref[at : at + blocks, :] = piece
 
 
-def early_kernel(dims, width, block, kinds_local, *refs):
-    chunks, parcels, (table_ref, other_ref) = refs[:6], refs[6:-7], refs[-7:-5]
+def early_kernel(dims, width, block, kinds, sources, *refs):
+    chunks, stacks = refs[:4], refs[4:6]
     sums_ref, rows_ref, main_ref, edge_ref, wide_ref = refs[-5:]
     _, group_blocks, per_exp, col_grid, band_grid, strips, exp_local, _ = dims
     blocks = exp_local * strips * col_grid
-    summed_into(sums_ref, chunks, None, dims, width, blocks)
+    tags = jnp.concatenate([tags_of(ref, width, TAGS_AT) for ref in chunks], axis=0)
+    summed_into(sums_ref, picks(tags, dims), chunks, None, width, blocks)
     band = lax.axis_index("row")
     out_rows = 96
-    kinds = kinds_local * len(parcels)
+    share = kinds // (2 * sources)
+    tall = stacks[0].shape[0] // sources
     src = lax.broadcasted_iota(jnp.int32, (LANES, 2 * LANES), 0)
     dst = lax.broadcasted_iota(jnp.int32, (LANES, 2 * LANES), 1)
     half = block // 2
@@ -111,10 +135,10 @@
     lane2 = lax.broadcasted_iota(jnp.int32, (out_rows, 2 * LANES), 1)
     spill = (out_rows - block) // 2
     lane_c = lax.broadcasted_iota(jnp.int32, (block, 2 * LANES), 1)
-    lane_e = lax.broadcasted_iota(jnp.int32, (block, LANES), 1)
+    lane_e = lax.broadcasted_iota(jnp.int32, (spill, LANES), 1)
     for k in range(kinds):
-        parcel = parcels[k // kinds_local]
-        both = parcel[(k % kinds_local) * out_rows : (k % kinds_local + 1) * out_rows, :]
+        at = k // share % sources * tall + k % share * out_rows
+        both = stacks[k // (share * sources)][at : at + out_rows, :]
         moved = jnp.dot(both, perm, preferred_element_type=jnp.float32)
         gap = jnp.zeros((block, 2 * LANES), jnp.float32)
         total = None
@@ -128,6 +152,10 @@
         chosen = jnp.where(band == 0, first, second).astype(jnp.bfloat16)
         rows_ref[k * 2 * block : (k + 1) * 2 * block, :] = chosen
         cols = both.astype(jnp.float32)
+        left = jnp.where(lane_e < block, 0.0, cols[out_rows - spill :])
+        right = jnp.where(lane_e < block, pltpu.roll(cols[:spill], block, 1), 0.0)
+        both_edges = jnp.concatenate([left, right], axis=0)
+        edge_ref[:, k * LANES : (k + 1) * LANES] = both_edges.astype(jnp.bfloat16)
         cols = jnp.concatenate([cols, jnp.zeros((LANES - out_rows, LANES), jnp.float32)], axis=0)
         turned = cols.T[block:, :]
         turned = jnp.concatenate([turned, jnp.zeros_like(turned)], axis=1)
@@ -137,20 +165,23 @@
             kept = placed
             if b == 0:
                 kept = jnp.where(lane_c < 2 * LANES - spill, placed, 0.0)
-                edge = jnp.where(lane_e >= LANES - spill, placed[:, LANES:], 0.0)
-                edge_ref[0, k * LANES : k * LANES + block, :] = edge.astype(jnp.bfloat16)
-                edge_ref[0, k * LANES + block : (k + 1) * LANES, :] = jnp.zeros((block, LANES), jnp.bfloat16)
             if b == 3:
                 kept = jnp.where(lane_c >= spill, placed, 0.0)
-                edge = jnp.where(lane_e < spill, placed[:, :LANES], 0.0)
-                edge_ref[1, k * LANES + block : (k + 1) * LANES, :] = edge.astype(jnp.bfloat16)
-                edge_ref[1, k * LANES : k * LANES + block, :] = jnp.zeros((block, LANES), jnp.bfloat16)
             at = k * 4 * block + b * block
             main_ref[at : at + block, :] = kept.astype(jnp.bfloat16)
-    pair = (table_ref[...], other_ref[...])
-    table = jnp.concatenate(
-        [jnp.where(band == 0, pair[0], pair[1]), jnp.where(band == 0, pair[1], pair[0])], axis=1
-    )
+    deep = tall - share * out_rows
+    row = lax.broadcasted_iota(jnp.int32, (kinds, sources * deep), 0)
+    col = lax.broadcasted_iota(jnp.int32, (kinds, sources * deep), 1)
+    core = jnp.where(row < share * sources, band, 1 - band)
+    wanted = row // share % sources * deep + core * share + row % share
+    find = jnp.where(col == wanted, 1.0, 0.0).astype(jnp.bfloat16)
+    pair = []
+    for stack in stacks:
+        lines = [stack[(s + 1) * tall - deep : (s + 1) * tall, :] for s in range(sources)]
+        lines = jnp.concatenate(lines, axis=0)
+        pair.append(jnp.dot(find, lines, preferred_element_type=jnp.float32))
+    table = [jnp.where(band == b, pair[0], pair[1]).astype(jnp.bfloat16) for b in range(2)]
+    table = jnp.concatenate(table, axis=1)
     src = lax.broadcasted_iota(jnp.int32, (table.shape[1], col_grid * block), 0)
     dst = lax.broadcasted_iota(jnp.int32, (table.shape[1], col_grid * block), 1)
     ahead = src - dst // block
@@ -169,56 +200,70 @@
 
 
 def late_kernel(dims, width, block, kinds, *refs):
-    chunks = refs[:6]
-    (before_ref, rows_ref, main_ref, edge_ref, wide_ref, obs_ref, inv_ref, out_ref) = refs[6:14]
-    sums_ref, image_ref, mid_ref, side_ref = refs[14:]
+    chunks = refs[:-13]
+    (pick_ref, before_ref, rows_ref, main_ref, edge_ref, wide_ref, obs_ref, inv_ref, out_ref) = refs[-13:-4]
+    sums_ref, image_ref, mid_ref, side_ref = refs[-4:]
     _, _, _, col_grid, band_grid, strips, exp_local, _ = dims
     blocks = exp_local * strips * col_grid
-    summed_into(sums_ref, chunks, before_ref, dims, width, blocks)
+    summed_into(sums_ref, pick_ref[...], chunks, before_ref, width, blocks)
     half = block // 2
     low = lax.broadcasted_iota(jnp.int32, (half, LANES), 1) < block
     tall = strips * block
-    wide_cols = col_grid * block
+    window = 4 * block
     band_rows = band_grid * block
+    low_band = lax.broadcasted_iota(jnp.int32, (band_rows, LANES), 1) < block
+
+    def laid_out(x, s, m):
+        n = (x * strips + s) * col_grid + 2 * m
+        a = sums_ref[pl.ds(n, half, stride=blocks), :]
+        b = sums_ref[pl.ds(n + 1, half, stride=blocks), :]
+        even = jnp.where(low, a, pltpu.roll(b, block, 1))
+        odd = jnp.where(low, pltpu.roll(a, block, 1), b)
+        at = s * block
+        cols = slice(m * LANES, (m + 1) * LANES)
+        image_ref[x, at : at + half, cols] = even.astype(jnp.bfloat16)
+        image_ref[x, at + half : at + block, cols] = odd.astype(jnp.bfloat16)
+
+    places = [[(x, s, m) for s in range(strips) for m in range(col_grid // 2)] for x in range(exp_local)]
+    for place in places[0]:
+        laid_out(*place)
     for x in range(exp_local):
-        for s in range(strips):
-            for m in range(col_grid // 2):
-                n = (x * strips + s) * col_grid + 2 * m
-                a = sums_ref[pl.ds(n, half, stride=blocks), :]
-                b = sums_ref[pl.ds(n + 1, half, stride=blocks), :]
-                even = jnp.where(low, a, pltpu.roll(b, block, 1))
-                odd = jnp.where(low, pltpu.roll(a, block, 1), b)
-                at = s * block
-                cols = slice(m * LANES, (m + 1) * LANES)
-                image_ref[x, at : at + half, cols] = even.astype(jnp.bfloat16)
-                image_ref[x, at + half : at + block, cols] = odd.astype(jnp.bfloat16)
-    window = 4 * block
-    for x in range(exp_local):
+        ahead = places[x + 1] if x + 1 < exp_local else []
         for k in range(kinds):
-            image = image_ref[x].reshape(strips, block // 16, 16, wide_cols)
             at = (x * kinds + k) * strips * 16
-            wide = wide_ref[at : at + strips * 16, :].reshape(strips, 1, 16, wide_cols)
-            scaled = (image * wide).reshape(tall, wide_cols)
             rows = rows_ref[k * band_rows : (k + 1) * band_rows, :]
-            mid = jnp.dot(rows, scaled, preferred_element_type=jnp.float32).astype(jnp.bfloat16)
+            mids = []
             for w in range(2):
+                cols = slice(w * window, (w + 1) * window)
+                image = image_ref[x, :, cols].reshape(strips, block // 16, 16, window)
+                wide = wide_ref[at : at + strips * 16, cols].reshape(strips, 1, 16, window)
+                scaled = (image * wide).reshape(tall, window)
+                mid = jnp.dot(rows, scaled, preferred_element_type=jnp.float32)
                 top = (w * exp_local + x) * band_rows
-                mid_ref[top : top + band_rows, k * window : (k + 1) * window] = mid[:, w * window : (w + 1) * window]
-            at = x * band_rows
-            cols = slice(k * LANES, (k + 1) * LANES)
-            side_ref[0, at : at + band_rows, cols] = mid[:, window : window + LANES]
-            side_ref[1, at : at + band_rows, cols] = mid[:, window - LANES : window]
+                mid_ref[top : top + band_rows, k * window : (k + 1) * window] = mid.astype(jnp.bfloat16)
+                mids.append(mid[:, :LANES] if w else mid[:, window - LANES :])
+            side = jnp.where(low_band, mids[1], mids[0])
+            side_ref[x * band_rows : (x + 1) * band_rows, k * LANES : (k + 1) * LANES] = side.astype(jnp.bfloat16)
+            for place in ahead[k :: kinds]:
+                laid_out(*place)
     tall2 = exp_local * band_rows
+    spill = edge_ref.shape[0] // 2
+    side = lax.dot_general(
+        edge_ref[...], side_ref[...], (((1,), (1,)), ((), ())), preferred_element_type=jnp.float32
+    )
+    gap = jnp.zeros((LANES - 2 * spill, tall2), jnp.float32)
+    side = jnp.concatenate([side[:spill], gap, side[spill:]], axis=0).T
+    low_all = lax.broadcasted_iota(jnp.int32, (tall2, LANES), 1) < block
     for w in range(2):
         main = jnp.dot(mid_ref[w * tall2 : (w + 1) * tall2, :], main_ref[...], preferred_element_type=jnp.float32)
-        side = jnp.dot(side_ref[w], edge_ref[w], preferred_element_type=jnp.float32)
+        edge = jnp.where(low_all, side, 0.0) if w else jnp.where(low_all, 0.0, side)
         for x in range(exp_local):
             rows = slice(x * band_rows, (x + 1) * band_rows)
             noise = jnp.sqrt(jnp.full((1, LANES), inv_ref[x], jnp.float32))
             for t in range(2):
                 model = main[rows, t * LANES : (t + 1) * LANES]
                 if t == 1 - w:
-                    model = model + side[rows]
+                    model = model + edge[rows]
                 cols = slice(w * window + t * LANES, w * window + (t + 1) * LANES)
                 out_ref[x, :, cols] = noise * (obs_ref[x, :, cols].astype(jnp.float32) - model)
 
@@ -240,6 +285,7 @@
     basis = lax.axis_index("basis")
     dims = (visits, group_blocks, per_exp, col_grid, band_grid, strips, exp_local, n_row)
     blocks = exp_local * strips * col_grid
+    spill = (out_width - block) // 2
 
     f32, bf16 = jnp.float32, jnp.bfloat16
     params = pltpu.CompilerParams(vmem_limit_bytes=VMEM_BYTES)
@@ -269,10 +315,9 @@
     far = []
     for s in range(n_exp - 1, 1, -1):
         far.append(swapped(own_part, "exp", s))
-    near = swapped(own, "exp", 1)
     maps = pl.pallas_call(
         parcel_kernel,
-        out_shape=jax.ShapeDtypeStruct((kinds_local * out_width, LANES), bf16),
+        out_shape=jax.ShapeDtypeStruct((kinds_local // n_row * out_width, LANES), bf16),
         in_specs=in_vmem(2),
         out_specs=in_vmem(1)[0],
         compiler_params=params,
@@ -283,38 +328,51 @@
     parcels = [maps]
     for s in range(1, n_basis):
         parcels.append(swapped(maps, "basis", s))
-    own_other = swapped(own, "row", 1)
+    near = swapped(own, "exp", 1)
     far = jnp.concatenate(far, axis=0)
     spread = []
     for s in range(n_basis - 1, 0, -1):
         spread.append(swapped(far, "basis", s))
+    own_other = swapped(own, "row", 1)
+    far_other = swapped(far, "row", 1)
+    stack = pl.pallas_call(
+        stack_kernel,
+        out_shape=jax.ShapeDtypeStruct((n_basis * maps.shape[0], LANES), bf16),
+        in_specs=in_vmem(n_basis),
+        out_specs=in_vmem(1)[0],
+        compiler_params=params,
+    )(*parcels)
+    stack_other = swapped(stack, "row", 1)
     near_other = swapped(near, "row", 1)
-    far_other = swapped(far, "row", 1)
-    table = jnp.concatenate(
-        [p[kinds_local * out_width : kinds_local * out_width + kinds_local] for p in parcels], axis=0
-    )
-    table_other = swapped(table, "row", 1)
     spread_other = []
     for s, v in zip(range(n_basis - 1, 0, -1), spread):
         spread_other.append(swapped(v, "row", 1))
 
-    early = [own, near, far, own_other, near_other, far_other] + parcels + [table, table_other]
+    early = [own, far, own_other, far_other, stack, stack_other]
     shapes = [
         jax.ShapeDtypeStruct((width // LANES * blocks, LANES), f32),
         jax.ShapeDtypeStruct((kinds * band_rows, strips * block), bf16),
         jax.ShapeDtypeStruct((kinds * 4 * block, 4 * block), bf16),
-        jax.ShapeDtypeStruct((2, kinds * LANES, LANES), bf16),
+        jax.ShapeDtypeStruct((2 * spill, kinds * LANES), bf16),
         jax.ShapeDtypeStruct((exp_local * kinds * strips * 16, tile_cols), bf16),
     ]
     early_call = pl.pallas_call(
-        functools.partial(early_kernel, dims, width, block, kinds_local),
+        functools.partial(early_kernel, dims, width, block, kinds, n_basis),
         out_shape=shapes,
         in_specs=in_vmem(len(early)),
         out_specs=in_vmem(len(shapes)),
         compiler_params=params,
     )
     prepared = early_call(*early)
-    late = spread + spread_other + list(prepared) + [observed]
+    late_count = 2 * (patch_count + (n_basis - 1) * far.shape[0])
+    pick = pl.pallas_call(
+        functools.partial(pick_kernel, dims, width, n_basis),
+        out_shape=jax.ShapeDtypeStruct((blocks, late_count), bf16),
+        in_specs=in_vmem(4),
+        out_specs=in_vmem(1)[0],
+        compiler_params=params,
+    )(near, near_other, far, far_other)
+    late = [near, near_other] + spread + spread_other + [pick] + list(prepared) + [observed]
     return pl.pallas_call(
         functools.partial(late_kernel, dims, width, block, kinds),
         out_shape=jax.ShapeDtypeStruct(observed.shape, f32),
@@ -324,7 +382,7 @@
             pltpu.VMEM((width // LANES * blocks, LANES), f32),
             pltpu.VMEM((exp_local, strips * block, tile_cols), bf16),
             pltpu.VMEM((2 * exp_local * band_rows, kinds * 4 * block), bf16),
-            pltpu.VMEM((2, exp_local * band_rows, kinds * LANES), bf16),
+            pltpu.VMEM((exp_local * band_rows, kinds * LANES), bf16),
         ],
         compiler_params=params,
     )(*late, inv_variance)

time: 33.6 us -> 37 us (1.10)
  waiting for transfers between devices: 9.37 us -> 13 us
    ppermute x16, waiting for transfers between devices: 9.37 us -> 13 us  [swapped(): return lax.ppermute(value, axis, [(i, i ^ by) for i in range(length)])]
  transfers between devices with their start and end apart: 16 -> 16, of which waited for: 3 -> 4; matrix products, arithmetic and copies ran while one was open for 0% -> 0% of each run, Pallas kernels for 6% -> 6%
where the time goes in v3:
time: 37 us; the launch traced here: 36.8 us
  starting transfers between devices  15.6 us (42%)
  waiting for transfers between devices  13 us (35%)
  Pallas kernels  7.92 us (21%)
    ppermute x16, starting transfers between devices, swapped(): return lax.ppermute(value, axis, [(i, i ^ by) for i in range(length)])  15.6 us
    ppermute x16, waiting for transfers between devices, swapped(): return lax.ppermute(value, axis, [(i, i ^ by) for i in range(length)])  13 us
    pallas_call x1, Pallas kernels, gathered_device(): pl.pallas_call(functools.partial(late_kernel, dims, width, block, kinds),...  4.78 us
    pallas_call x1, Pallas kernels, gathered_device(): prepared = early_call(*early)  1.59 us
    pallas_call x1, Pallas kernels, gathered_device(): pl.pallas_call(pack_kernel, out_shape=[jax.ShapeDtypeStruct((patch_count,...  1.08 us
  transfers between devices with their start and end apart: 16, of which 4 were waited for; matrix products, arithmetic and copies ran while one was open for 0% of the time, Pallas kernels for 6%

profile of v3, /device:TPU:0, one launch (start us, length us, event | category | flops | bytes accessed | tf_op | source)
XLA Modules:
  0.0 36.8 jit_solution(112867673679720457)
XLA Ops:
  0.0 1.1 %shard_map.82 = (bf16[32,4224]{1,0:T(8,128)(2,1)S(1)}, bf16[4,64,96]{2,1,0:T(8,128)(2,1)S(1)}, bf16[4,64,96]{2,1,0:T(8,128)(2,1)S(1)}, bf16[8,4,2,8]{3,2,1,0:T(2,128)(2,1)S(1)}) custom-call(bf16[32,4096]{1,0:T(8,128)(2,1)} %patch_ref.1, s32[4,32]{1,0:T(4,128)} %bitcast.8, s32[4,32]{1,0:T(4,128)} %bitcast.9, bf16[4,64,96]{2,1,0:T(8,128)(2,1)} %bitcast.6, ...), custom_call_target="tpu_custom_call" | custom-call | tf_op jit(solution)/shard_map/pallas_call | solution.py:300
  1.1 5.1 %collective-permute-start.2 = (bf16[8,4224]{1,0:T(8,128)(2,1)S(1)}, bf16[8,4224]{1,0:T(8,128)(2,1)S(1)}, u32[]{:S(2)}, u32[]{:S(2)}) collective-permute-start(bf16[8,4224]{1,0:T(8,128)(2,1)S(1)} %constant_dynamic-slice_fusion), channel_id=1, source_target_pairs={{0,24},{8,16},{16,8},{24,0},{1,25},{9,17},{17,9},{25,1},{2,26},{10... | collective-permute-start | bytes 202760 | tf_op jit(solution)/shard_map/ppermute | solution.py:17
  6.3 0.0 collective-permute-start.3
  6.3 0.6 %collective-permute-start = (bf16[32,4224]{1,0:T(8,128)(2,1)S(1)}, bf16[32,4224]{1,0:T(8,128)(2,1)S(1)}, u32[]{:S(2)}, u32[]{:S(2)}) collective-permute-start(bf16[32,4224]{1,0:T(8,128)(2,1)S(1)} %get-tuple-element.14.refs_0_), channel_id=1, source_target_pairs={{0,8},{8,0},{16,24},{24,16},{1,9},{9,1},{17,25},{25,17},{2,10},{10... | collective-permute-start | bytes 811016 | tf_op jit(solution)/shard_map/ppermute | solution.py:17
  6.9 0.1 reshape.3
  7.0 0.1 shard_map.84
  7.1 1.7 %collective-permute-start.12 = (bf16[208,128]{1,0:T(8,128)(2,1)S(1)}, bf16[208,128]{1,0:T(8,128)(2,1)S(1)}, u32[]{:S(2)}, u32[]{:S(2)}) collective-permute-start(bf16[208,128]{1,0:T(8,128)(2,1)S(1)} %fusion.1.refs_0_), channel_id=1, source_target_pairs={{0,1},{1,0},{2,3},{3,2},{4,5},{5,4},{6,7},{7,6},{8,9},{9,8},{10,11... | collective-permute-start | bytes 159752 | tf_op jit(solution)/shard_map/ppermute | solution.py:17
  8.9 3.3 %collective-permute-done.3 = bf16[8,4224]{1,0:T(8,128)(2,1)S(1)} collective-permute-done((bf16[8,4224]{1,0:T(8,128)(2,1)S(1)}, bf16[8,4224]{1,0:T(8,128)(2,1)S(1)}, u32[]{:S(2)}, u32[]{:S(2)}) %collective-permute-start.3) | collective-permute-done | bytes 67616 | tf_op jit(solution)/shard_map/ppermute | solution.py:17
  12.1 0.1 collective-permute-start.10
  12.2 2.5 %collective-permute-start.4 = (bf16[16,4224]{1,0:T(8,128)(2,1)S(1)}, bf16[16,4224]{1,0:T(8,128)(2,1)S(1)}, u32[]{:S(2)}, u32[]{:S(2)}) collective-permute-start(bf16[16,4224]{1,0:T(8,128)(2,1)S(1)} %constant_dynamic-update-slice_fusion.far_ref.refs_1_), channel_id=1, source_target_pairs={{0,3},{1,2},{2,1},{3,0},{4,7},{5,6},{6,5},{7,4},{8,11},{9,10},{10,... | collective-permute-start | bytes 405512 | tf_op jit(solution)/shard_map/ppermute | solution.py:17
  14.7 0.5 %collective-permute-start.13 = (bf16[208,128]{1,0:T(8,128)(2,1)S(1)}, bf16[208,128]{1,0:T(8,128)(2,1)S(1)}, u32[]{:S(2)}, u32[]{:S(2)}) collective-permute-start(bf16[208,128]{1,0:T(8,128)(2,1)S(1)} %fusion.1.refs_0_), channel_id=1, source_target_pairs={{0,2},{1,3},{2,0},{3,1},{4,6},{5,7},{6,4},{7,5},{8,10},{9,11},{10,... | collective-permute-start | bytes 159752 | tf_op jit(solution)/shard_map/ppermute | solution.py:17
  15.2 1.5 %collective-permute-start.14 = (bf16[208,128]{1,0:T(8,128)(2,1)S(1)}, bf16[208,128]{1,0:T(8,128)(2,1)S(1)}, u32[]{:S(2)}, u32[]{:S(2)}) collective-permute-start(bf16[208,128]{1,0:T(8,128)(2,1)S(1)} %fusion.1.refs_0_), channel_id=1, source_target_pairs={{0,3},{1,2},{2,1},{3,0},{4,7},{5,6},{6,5},{7,4},{8,11},{9,10},{10,... | collective-permute-start | bytes 159752 | tf_op jit(solution)/shard_map/ppermute | solution.py:17
  16.7 4.7 %collective-permute-done.13.refs_2_ = bf16[208,128]{1,0:T(8,128)(2,1)S(1)} collective-permute-done((bf16[208,128]{1,0:T(8,128)(2,1)S(1)}, bf16[208,128]{1,0:T(8,128)(2,1)S(1)}, u32[]{:S(2)}, u32[]{:S(2)}) %collective-permute-start.13) | collective-permute-done | bytes 53280 | tf_op jit(solution)/shard_map/ppermute | solution.py:17
  21.4 0.1 collective-permute-start.15
  21.5 0.5 %collective-permute-start.11 = (bf16[32,4224]{1,0:T(8,128)(2,1)S(1)}, bf16[32,4224]{1,0:T(8,128)(2,1)S(1)}, u32[]{:S(2)}, u32[]{:S(2)}) collective-permute-start(bf16[32,4224]{1,0:T(8,128)(2,1)S(1)} %get-tuple-element.14.refs_0_), channel_id=1, source_target_pairs={{0,4},{4,0},{1,5},{5,1},{2,6},{6,2},{3,7},{7,3},{8,12},{12,8},{9,1... | collective-permute-start | bytes 811016 | tf_op jit(solution)/shard_map/ppermute | solution.py:17
  22.0 1.5 %collective-permute-start.5 = (bf16[16,4224]{1,0:T(8,128)(2,1)S(1)}, bf16[16,4224]{1,0:T(8,128)(2,1)S(1)}, u32[]{:S(2)}, u32[]{:S(2)}) collective-permute-start(bf16[16,4224]{1,0:T(8,128)(2,1)S(1)} %constant_dynamic-update-slice_fusion.far_ref.refs_1_), channel_id=1, source_target_pairs={{0,2},{1,3},{2,0},{3,1},{4,6},{5,7},{6,4},{7,5},{8,10},{9,11},{10,... | collective-permute-start | bytes 405512 | tf_op jit(solution)/shard_map/ppermute | solution.py:17
  23.5 1.0 %collective-permute-start.6 = (bf16[16,4224]{1,0:T(8,128)(2,1)S(1)}, bf16[16,4224]{1,0:T(8,128)(2,1)S(1)}, u32[]{:S(2)}, u32[]{:S(2)}) collective-permute-start(bf16[16,4224]{1,0:T(8,128)(2,1)S(1)} %constant_dynamic-update-slice_fusion.far_ref.refs_1_), channel_id=1, source_target_pairs={{0,1},{1,0},{2,3},{3,2},{4,5},{5,4},{6,7},{7,6},{8,9},{9,8},{10,11... | collective-permute-start | bytes 405512 | tf_op jit(solution)/shard_map/ppermute | solution.py:17
  24.5 3.1 %collective-permute-done.5.refs_3_ = bf16[16,4224]{1,0:T(8,128)(2,1)S(1)} collective-permute-done((bf16[16,4224]{1,0:T(8,128)(2,1)S(1)}, bf16[16,4224]{1,0:T(8,128)(2,1)S(1)}, u32[]{:S(2)}, u32[]{:S(2)}) %collective-permute-start.5) | collective-permute-done | bytes 135200 | tf_op jit(solution)/shard_map/ppermute | solution.py:17
  27.5 2.0 %collective-permute-done.6.refs_4_ = bf16[16,4224]{1,0:T(8,128)(2,1)S(1)} collective-permute-done((bf16[16,4224]{1,0:T(8,128)(2,1)S(1)}, bf16[16,4224]{1,0:T(8,128)(2,1)S(1)}, u32[]{:S(2)}, u32[]{:S(2)}) %collective-permute-start.6) | collective-permute-done | bytes 135200 | tf_op jit(solution)/shard_map/ppermute | solution.py:17
  29.5 0.5 %collective-permute-start.9 = (bf16[16,4224]{1,0:T(8,128)(2,1)S(1)}, bf16[16,4224]{1,0:T(8,128)(2,1)S(1)}, u32[]{:S(2)}, u32[]{:S(2)}) collective-permute-start(bf16[16,4224]{1,0:T(8,128)(2,1)S(1)} %collective-permute-done.6.refs_4_), channel_id=1, source_target_pairs={{0,4},{4,0},{1,5},{5,1},{2,6},{6,2},{3,7},{7,3},{8,12},{12,8},{9,1... | collective-permute-start | bytes 405512 | tf_op jit(solution)/shard_map/ppermute | solution.py:17
  30.0 1.6 %shard_map.86 = (f32[1536,128]{1,0:T(8,128)S(1)}, bf16[2048,192]{1,0:T(8,128)(2,1)S(1)}, bf16[4096,256]{1,0:T(8,128)(2,1)S(1)}, bf16[32,2048]{1,0:T(8,128)(2,1)S(1)}, bf16[1536,512]{1,0:T(8,128)(2,1)S(1)}) custom-call(bf16[32,4224]{1,0:T(8,128)(2,1)S(1)} %get-tuple-element.14.refs_0_, bf16[16,4224]{1,0:T(8,128)(2,1)S(1)} %constant_dynamic-update-slice_fusion.far_ref.refs_1_, ...), custom_call_target="tpu_custom_call" | custom-call | tf_op jit(solution)/shard_map/pallas_call | solution.py:366
  31.6 0.4 shard_map.83.refs_8_
  32.0 0.0 collective-permute-done.7.refs_5_
  32.0 4.8 %shard_map.87 = f32[2,128,512]{2,1,0:T(8,128)} custom-call(bf16[32,4224]{1,0:T(8,128)(2,1)S(1)} %collective-permute-done.near_ref.refs_0_, bf16[32,4224]{1,0:T(8,128)(2,1)S(1)} %collective-permute-done.1.near_other_ref.refs_1_, bf16[16,4224]{1,0:T(8,128)(2,1)S(1)} %collective-permute-done.4.refs_2_, bf16[16,4224]{1,0:T(8,128)(2,1)S(1)} %collective-permute-done.5.refs_3_, ...), custom_call_target="tpu_custom_call" | custom-call | tf_op jit(solution)/shard_map/pallas_call | solution.py:376
  (24 shorter events, 0.1 us)
Async XLA Ops:
  0.0 32.0 %copy-start.1 = (f32[2]{0:T(128)S(1)}, f32[2]{0:T(128)}, u32[]{:S(2)}) copy-start(f32[2]{0:T(128)} %refs_15_.1) | copy-start | bytes 28
  0.0 32.0 %copy-start = (bf16[2,128,512]{2,1,0:T(8,128)(2,1)S(1)}, bf16[2,128,512]{2,1,0:T(8,128)(2,1)}, u32[]{:S(2)}) copy-start(bf16[2,128,512]{2,1,0:T(8,128)(2,1)} %refs_14_.1) | copy-start | bytes 786436
  1.1 7.7 %collective-permute-start.2 = (bf16[8,4224]{1,0:T(8,128)(2,1)S(1)}, bf16[8,4224]{1,0:T(8,128)(2,1)S(1)}, u32[]{:S(2)}, u32[]{:S(2)}) collective-permute-start(bf16[8,4224]{1,0:T(8,128)(2,1)S(1)} %constant_dynamic-slice_fusion), channel_id=1, source_target_pairs={{0,24},{8,16},{16,8},{24,0},{1,25},{9,17},{17,9},{25,1},{2,26},{10... | collective-permute-start | bytes 202760 | tf_op jit(solution)/shard_map/ppermute | solution.py:17
  6.3 5.9 %collective-permute-start.3 = (bf16[8,4224]{1,0:T(8,128)(2,1)S(1)}, bf16[8,4224]{1,0:T(8,128)(2,1)S(1)}, u32[]{:S(2)}, u32[]{:S(2)}) collective-permute-start(bf16[8,4224]{1,0:T(8,128)(2,1)S(1)} %constant_dynamic-slice_fusion), channel_id=1, source_target_pairs={{0,16},{8,24},{16,0},{24,8},{1,17},{9,25},{17,1},{25,9},{2,18},{10... | collective-permute-start | bytes 202760 | tf_op jit(solution)/shard_map/ppermute | solution.py:17
  6.3 17.2 %collective-permute-start = (bf16[32,4224]{1,0:T(8,128)(2,1)S(1)}, bf16[32,4224]{1,0:T(8,128)(2,1)S(1)}, u32[]{:S(2)}, u32[]{:S(2)}) collective-permute-start(bf16[32,4224]{1,0:T(8,128)(2,1)S(1)} %get-tuple-element.14.refs_0_), channel_id=1, source_target_pairs={{0,8},{8,0},{16,24},{24,16},{1,9},{9,1},{17,25},{25,17},{2,10},{10... | collective-permute-start | bytes 811016 | tf_op jit(solution)/shard_map/ppermute | solution.py:17
  7.1 8.1 %collective-permute-start.12 = (bf16[208,128]{1,0:T(8,128)(2,1)S(1)}, bf16[208,128]{1,0:T(8,128)(2,1)S(1)}, u32[]{:S(2)}, u32[]{:S(2)}) collective-permute-start(bf16[208,128]{1,0:T(8,128)(2,1)S(1)} %fusion.1.refs_0_), channel_id=1, source_target_pairs={{0,1},{1,0},{2,3},{3,2},{4,5},{5,4},{6,7},{7,6},{8,9},{9,8},{10,11... | collective-permute-start | bytes 159752 | tf_op jit(solution)/shard_map/ppermute | solution.py:17
  12.1 9.8 %collective-permute-start.10 = (bf16[16,4224]{1,0:T(8,128)(2,1)S(1)}, bf16[16,4224]{1,0:T(8,128)(2,1)S(1)}, u32[]{:S(2)}, u32[]{:S(2)}) collective-permute-start(bf16[16,4224]{1,0:T(8,128)(2,1)S(1)} %constant_dynamic-update-slice_fusion.far_ref.refs_1_), channel_id=1, source_target_pairs={{0,4},{4,0},{1,5},{5,1},{2,6},{6,2},{3,7},{7,3},{8,12},{12,8},{9,1... | collective-permute-start | bytes 405512 | tf_op jit(solution)/shard_map/ppermute | solution.py:17
  12.2 11.3 %collective-permute-start.4 = (bf16[16,4224]{1,0:T(8,128)(2,1)S(1)}, bf16[16,4224]{1,0:T(8,128)(2,1)S(1)}, u32[]{:S(2)}, u32[]{:S(2)}) collective-permute-start(bf16[16,4224]{1,0:T(8,128)(2,1)S(1)} %constant_dynamic-update-slice_fusion.far_ref.refs_1_), channel_id=1, source_target_pairs={{0,3},{1,2},{2,1},{3,0},{4,7},{5,6},{6,5},{7,4},{8,11},{9,10},{10,... | collective-permute-start | bytes 405512 | tf_op jit(solution)/shard_map/ppermute | solution.py:17
  14.7 6.7 %collective-permute-start.13 = (bf16[208,128]{1,0:T(8,128)(2,1)S(1)}, bf16[208,128]{1,0:T(8,128)(2,1)S(1)}, u32[]{:S(2)}, u32[]{:S(2)}) collective-permute-start(bf16[208,128]{1,0:T(8,128)(2,1)S(1)} %fusion.1.refs_0_), channel_id=1, source_target_pairs={{0,2},{1,3},{2,0},{3,1},{4,6},{5,7},{6,4},{7,5},{8,10},{9,11},{10,... | collective-permute-start | bytes 159752 | tf_op jit(solution)/shard_map/ppermute | solution.py:17
  15.2 6.2 %collective-permute-start.14 = (bf16[208,128]{1,0:T(8,128)(2,1)S(1)}, bf16[208,128]{1,0:T(8,128)(2,1)S(1)}, u32[]{:S(2)}, u32[]{:S(2)}) collective-permute-start(bf16[208,128]{1,0:T(8,128)(2,1)S(1)} %fusion.1.refs_0_), channel_id=1, source_target_pairs={{0,3},{1,2},{2,1},{3,0},{4,7},{5,6},{6,5},{7,4},{8,11},{9,10},{10,... | collective-permute-start | bytes 159752 | tf_op jit(solution)/shard_map/ppermute | solution.py:17
  21.4 8.1 %collective-permute-start.15 = (bf16[832,128]{1,0:T(8,128)(2,1)S(1)}, bf16[832,128]{1,0:T(8,128)(2,1)S(1)}, u32[]{:S(2)}, u32[]{:S(2)}) collective-permute-start(bf16[832,128]{1,0:T(8,128)(2,1)S(1)} %shard_map.85.refs_4_), channel_id=1, source_target_pairs={{0,4},{4,0},{1,5},{5,1},{2,6},{6,2},{3,7},{7,3},{8,12},{12,8},{9,1... | collective-permute-start | bytes 638984 | tf_op jit(solution)/shard_map/ppermute | solution.py:17
  21.5 8.5 %collective-permute-start.11 = (bf16[32,4224]{1,0:T(8,128)(2,1)S(1)}, bf16[32,4224]{1,0:T(8,128)(2,1)S(1)}, u32[]{:S(2)}, u32[]{:S(2)}) collective-permute-start(bf16[32,4224]{1,0:T(8,128)(2,1)S(1)} %get-tuple-element.14.refs_0_), channel_id=1, source_target_pairs={{0,4},{4,0},{1,5},{5,1},{2,6},{6,2},{3,7},{7,3},{8,12},{12,8},{9,1... | collective-permute-start | bytes 811016 | tf_op jit(solution)/shard_map/ppermute | solution.py:17
  22.0 5.6 %collective-permute-start.5 = (bf16[16,4224]{1,0:T(8,128)(2,1)S(1)}, bf16[16,4224]{1,0:T(8,128)(2,1)S(1)}, u32[]{:S(2)}, u32[]{:S(2)}) collective-permute-start(bf16[16,4224]{1,0:T(8,128)(2,1)S(1)} %constant_dynamic-update-slice_fusion.far_ref.refs_1_), channel_id=1, source_target_pairs={{0,2},{1,3},{2,0},{3,1},{4,6},{5,7},{6,4},{7,5},{8,10},{9,11},{10,... | collective-permute-start | bytes 405512 | tf_op jit(solution)/shard_map/ppermute | solution.py:17
  23.5 8.1 %collective-permute-start.1 = (bf16[32,4224]{1,0:T(8,128)(2,1)S(1)}, bf16[32,4224]{1,0:T(8,128)(2,1)S(1)}, u32[]{:S(2)}, u32[]{:S(2)}) collective-permute-start(bf16[32,4224]{1,0:T(8,128)(2,1)S(1)} %collective-permute-done.near_ref.refs_0_), channel_id=1, source_target_pairs={{0,4},{4,0},{1,5},{5,1},{2,6},{6,2},{3,7},{7,3},{8,12},{12,8},{9,1... | collective-permute-start | bytes 811016 | tf_op jit(solution)/shard_map/ppermute | solution.py:17
  23.5 6.0 %collective-permute-start.6 = (bf16[16,4224]{1,0:T(8,128)(2,1)S(1)}, bf16[16,4224]{1,0:T(8,128)(2,1)S(1)}, u32[]{:S(2)}, u32[]{:S(2)}) collective-permute-start(bf16[16,4224]{1,0:T(8,128)(2,1)S(1)} %constant_dynamic-update-slice_fusion.far_ref.refs_1_), channel_id=1, source_target_pairs={{0,1},{1,0},{2,3},{3,2},{4,5},{5,4},{6,7},{7,6},{8,9},{9,8},{10,11... | collective-permute-start | bytes 405512 | tf_op jit(solution)/shard_map/ppermute | solution.py:17
  27.5 4.5 %collective-permute-start.7 = (bf16[16,4224]{1,0:T(8,128)(2,1)S(1)}, bf16[16,4224]{1,0:T(8,128)(2,1)S(1)}, u32[]{:S(2)}, u32[]{:S(2)}) collective-permute-start(bf16[16,4224]{1,0:T(8,128)(2,1)S(1)} %collective-permute-done.4.refs_2_), channel_id=1, source_target_pairs={{0,4},{4,0},{1,5},{5,1},{2,6},{6,2},{3,7},{7,3},{8,12},{12,8},{9,1... | collective-permute-start | bytes 405512 | tf_op jit(solution)/shard_map/ppermute | solution.py:17
  29.5 2.5 %collective-permute-start.8 = (bf16[16,4224]{1,0:T(8,128)(2,1)S(1)}, bf16[16,4224]{1,0:T(8,128)(2,1)S(1)}, u32[]{:S(2)}, u32[]{:S(2)}) collective-permute-start(bf16[16,4224]{1,0:T(8,128)(2,1)S(1)} %collective-permute-done.5.refs_3_), channel_id=1, source_target_pairs={{0,4},{4,0},{1,5},{5,1},{2,6},{6,2},{3,7},{7,3},{8,12},{12,8},{9,1... | collective-permute-start | bytes 405512 | tf_op jit(solution)/shard_map/ppermute | solution.py:17
  29.5 2.5 %collective-permute-start.9 = (bf16[16,4224]{1,0:T(8,128)(2,1)S(1)}, bf16[16,4224]{1,0:T(8,128)(2,1)S(1)}, u32[]{:S(2)}, u32[]{:S(2)}) collective-permute-start(bf16[16,4224]{1,0:T(8,128)(2,1)S(1)} %collective-permute-done.6.refs_4_), channel_id=1, source_target_pairs={{0,4},{4,0},{1,5},{5,1},{2,6},{6,2},{3,7},{7,3},{8,12},{12,8},{9,1... | collective-permute-start | bytes 405512 | tf_op jit(solution)/shard_map/ppermute | solution.py:17

commit v4 on v3

--- a/solution.py
+++ b/solution.py
@@ -9,6 +9,7 @@
 
 LANES = 128
 TAGS_AT = 64
+ROW_PAD = 4
 VMEM_BYTES = 28 * 1024 * 1024
 
 
@@ -102,7 +103,7 @@
     pick_ref[...] = picks(jnp.concatenate(tags, axis=0), dims)
 
 
-def summed_into(out_ref, pick, chunk_refs, before_ref, width, blocks):
+def summed_into(out_ref, pick, chunk_refs, before_ref, width, blocks, pitch):
     step = 4 * LANES
     for start in range(0, width, step):
         rows = jnp.concatenate([ref[:, start : start + step] for ref in chunk_refs], axis=0)
@@ -112,6 +113,7 @@
             piece = part[:, t * LANES : (t + 1) * LANES]
             if before_ref is not None:
                 piece = piece + before_ref[at : at + blocks, :]
+            at = (start // LANES + t) * pitch
             out_ref[at : at + blocks, :] = piece
 
 
@@ -121,7 +123,7 @@
     _, group_blocks, per_exp, col_grid, band_grid, strips, exp_local, _ = dims
     blocks = exp_local * strips * col_grid
     tags = jnp.concatenate([tags_of(ref, width, TAGS_AT) for ref in chunks], axis=0)
-    summed_into(sums_ref, picks(tags, dims), chunks, None, width, blocks)
+    summed_into(sums_ref, picks(tags, dims), chunks, None, width, blocks, blocks)
     band = lax.axis_index("row")
     out_rows = 96
     share = kinds // (2 * sources)
@@ -205,7 +207,8 @@
     sums_ref, image_ref, mid_ref, side_ref = refs[-4:]
     _, _, _, col_grid, band_grid, strips, exp_local, _ = dims
     blocks = exp_local * strips * col_grid
-    summed_into(sums_ref, pick_ref[...], chunks, before_ref, width, blocks)
+    pitch = sums_ref.shape[0] // (width // LANES)
+    summed_into(sums_ref, pick_ref[...], chunks, before_ref, width, blocks, pitch)
     half = block // 2
     low = lax.broadcasted_iota(jnp.int32, (half, LANES), 1) < block
     tall = strips * block
@@ -215,8 +218,8 @@
 
     def laid_out(x, s, m):
         n = (x * strips + s) * col_grid + 2 * m
-        a = sums_ref[pl.ds(n, half, stride=blocks), :]
-        b = sums_ref[pl.ds(n + 1, half, stride=blocks), :]
+        a = sums_ref[pl.ds(n, half, stride=pitch), :]
+        b = sums_ref[pl.ds(n + 1, half, stride=pitch), :]
         even = jnp.where(low, a, pltpu.roll(b, block, 1))
         odd = jnp.where(low, pltpu.roll(a, block, 1), b)
         at = s * block
@@ -254,8 +257,9 @@
     gap = jnp.zeros((LANES - 2 * spill, tall2), jnp.float32)
     side = jnp.concatenate([side[:spill], gap, side[spill:]], axis=0).T
     low_all = lax.broadcasted_iota(jnp.int32, (tall2, LANES), 1) < block
+    mains = jnp.dot(mid_ref[...], main_ref[...], preferred_element_type=jnp.float32)
     for w in range(2):
-        main = jnp.dot(mid_ref[w * tall2 : (w + 1) * tall2, :], main_ref[...], preferred_element_type=jnp.float32)
+        main = mains[w * tall2 : (w + 1) * tall2]
         edge = jnp.where(low_all, side, 0.0) if w else jnp.where(low_all, 0.0, side)
         for x in range(exp_local):
             rows = slice(x * band_rows, (x + 1) * band_rows)
@@ -313,7 +317,7 @@
     part = patch_count // n_basis
     own_part = lax.dynamic_slice_in_dim(own, basis * part, part, 0)
     far = []
-    for s in range(n_exp - 1, 1, -1):
+    for s in range(2, n_exp):
         far.append(swapped(own_part, "exp", s))
     maps = pl.pallas_call(
         parcel_kernel,
@@ -329,10 +333,11 @@
     for s in range(1, n_basis):
         parcels.append(swapped(maps, "basis", s))
     near = swapped(own, "exp", 1)
+    bare = jnp.concatenate([v[:, :width] for v in far], axis=0)
     far = jnp.concatenate(far, axis=0)
     spread = []
     for s in range(n_basis - 1, 0, -1):
-        spread.append(swapped(far, "basis", s))
+        spread.append(swapped(bare, "basis", s))
     own_other = swapped(own, "row", 1)
     far_other = swapped(far, "row", 1)
     stack = pl.pallas_call(
@@ -379,7 +384,7 @@
         in_specs=in_vmem(len(late)) + [pl.BlockSpec(memory_space=pltpu.SMEM)],
         out_specs=pl.BlockSpec(memory_space=pltpu.VMEM),
         scratch_shapes=[
-            pltpu.VMEM((width // LANES * blocks, LANES), f32),
+            pltpu.VMEM((width // LANES * (blocks + ROW_PAD), LANES), f32),
             pltpu.VMEM((exp_local, strips * block, tile_cols), bf16),
             pltpu.VMEM((2 * exp_local * band_rows, kinds * 4 * block), bf16),
             pltpu.VMEM((exp_local * band_rows, kinds * LANES), bf16),

time: 37 us -> 36.5 us (0.986)
  starting transfers between devices: 15.6 us -> 13.2 us
  waiting for transfers between devices: 13 us -> 14.9 us
    ppermute x16, starting transfers between devices: 15.6 us -> 13.2 us  [swapped(): return lax.ppermute(value, axis, [(i, i ^ by) for i in range(length)])]
    ppermute x16, waiting for transfers between devices: 13 us -> 14.9 us  [swapped(): return lax.ppermute(value, axis, [(i, i ^ by) for i in range(length)])]
  transfers between devices with their start and end apart: 16 -> 16, of which waited for: 4 -> 7; matrix products, arithmetic and copies ran while one was open for 0% -> 0% of each run, Pallas kernels for 6% -> 6%
where the time goes in v4:
time: 36.5 us; the launch traced here: 36.3 us
  waiting for transfers between devices  14.9 us (41%)
  starting transfers between devices  13.2 us (36%)
  Pallas kernels  7.81 us (21%)
    ppermute x16, waiting for transfers between devices, swapped(): return lax.ppermute(value, axis, [(i, i ^ by) for i in range(length)])  14.9 us
    ppermute x16, starting transfers between devices, swapped(): return lax.ppermute(value, axis, [(i, i ^ by) for i in range(length)])  13.2 us
    pallas_call x1, Pallas kernels, gathered_device(): pl.pallas_call(functools.partial(late_kernel, dims, width, block, kinds),...  4.68 us
    pallas_call x1, Pallas kernels, gathered_device(): prepared = early_call(*early)  1.59 us
    pallas_call x1, Pallas kernels, gathered_device(): pl.pallas_call(pack_kernel, out_shape=[jax.ShapeDtypeStruct((patch_count,...  1.08 us
  transfers between devices with their start and end apart: 16, of which 7 were waited for; matrix products, arithmetic and copies ran while one was open for 0% of the time, Pallas kernels for 6%

profile of v4, /device:TPU:0, one launch (start us, length us, event | category | flops | bytes accessed | tf_op | source)
XLA Modules:
  0.0 36.3 jit_solution(15835246831569958723)
XLA Ops:
  0.0 1.1 %shard_map.82 = (bf16[32,4224]{1,0:T(8,128)(2,1)S(1)}, bf16[4,64,96]{2,1,0:T(8,128)(2,1)S(1)}, bf16[4,64,96]{2,1,0:T(8,128)(2,1)S(1)}, bf16[8,4,2,8]{3,2,1,0:T(2,128)(2,1)S(1)}) custom-call(bf16[32,4096]{1,0:T(8,128)(2,1)} %patch_ref.1, s32[4,32]{1,0:T(4,128)} %bitcast.8, s32[4,32]{1,0:T(4,128)} %bitcast.9, bf16[4,64,96]{2,1,0:T(8,128)(2,1)} %bitcast.6, ...), custom_call_target="tpu_custom_call" | custom-call | tf_op jit(solution)/shard_map/pallas_call | solution.py:304
  1.1 4.1 %collective-permute-start.2 = (bf16[8,4224]{1,0:T(8,128)(2,1)S(1)}, bf16[8,4224]{1,0:T(8,128)(2,1)S(1)}, u32[]{:S(2)}, u32[]{:S(2)}) collective-permute-start(bf16[8,4224]{1,0:T(8,128)(2,1)S(1)} %constant_dynamic-slice_fusion), channel_id=1, source_target_pairs={{0,16},{8,24},{16,0},{24,8},{1,17},{9,25},{17,1},{25,9},{2,18},{10... | collective-permute-start | bytes 202760 | tf_op jit(solution)/shard_map/ppermute | solution.py:18
  5.2 1.3 %collective-permute-start.3 = (bf16[8,4224]{1,0:T(8,128)(2,1)S(1)}, bf16[8,4224]{1,0:T(8,128)(2,1)S(1)}, u32[]{:S(2)}, u32[]{:S(2)}) collective-permute-start(bf16[8,4224]{1,0:T(8,128)(2,1)S(1)} %constant_dynamic-slice_fusion), channel_id=1, source_target_pairs={{0,24},{8,16},{16,8},{24,0},{1,25},{9,17},{17,9},{25,1},{2,26},{10... | collective-permute-start | bytes 202760 | tf_op jit(solution)/shard_map/ppermute | solution.py:18
  6.6 0.1 reshape.3
  6.7 0.1 shard_map.84
  6.8 1.6 %collective-permute-start.12 = (bf16[208,128]{1,0:T(8,128)(2,1)S(1)}, bf16[208,128]{1,0:T(8,128)(2,1)S(1)}, u32[]{:S(2)}, u32[]{:S(2)}) collective-permute-start(bf16[208,128]{1,0:T(8,128)(2,1)S(1)} %fusion.1.refs_0_), channel_id=1, source_target_pairs={{0,1},{1,0},{2,3},{3,2},{4,5},{5,4},{6,7},{7,6},{8,9},{9,8},{10,11... | collective-permute-start | bytes 159752 | tf_op jit(solution)/shard_map/ppermute | solution.py:18
  8.4 1.5 %collective-permute-start.13 = (bf16[208,128]{1,0:T(8,128)(2,1)S(1)}, bf16[208,128]{1,0:T(8,128)(2,1)S(1)}, u32[]{:S(2)}, u32[]{:S(2)}) collective-permute-start(bf16[208,128]{1,0:T(8,128)(2,1)S(1)} %fusion.1.refs_0_), channel_id=1, source_target_pairs={{0,2},{1,3},{2,0},{3,1},{4,6},{5,7},{6,4},{7,5},{8,10},{9,11},{10,... | collective-permute-start | bytes 159752 | tf_op jit(solution)/shard_map/ppermute | solution.py:18
  9.9 0.5 %collective-permute-start.14 = (bf16[208,128]{1,0:T(8,128)(2,1)S(1)}, bf16[208,128]{1,0:T(8,128)(2,1)S(1)}, u32[]{:S(2)}, u32[]{:S(2)}) collective-permute-start(bf16[208,128]{1,0:T(8,128)(2,1)S(1)} %fusion.1.refs_0_), channel_id=1, source_target_pairs={{0,3},{1,2},{2,1},{3,0},{4,7},{5,6},{6,5},{7,4},{8,11},{9,10},{10,... | collective-permute-start | bytes 159752 | tf_op jit(solution)/shard_map/ppermute | solution.py:18
  10.4 0.6 %collective-permute-done.12.refs_1_ = bf16[208,128]{1,0:T(8,128)(2,1)S(1)} collective-permute-done((bf16[208,128]{1,0:T(8,128)(2,1)S(1)}, bf16[208,128]{1,0:T(8,128)(2,1)S(1)}, u32[]{:S(2)}, u32[]{:S(2)}) %collective-permute-start.12) | collective-permute-done | bytes 53280 | tf_op jit(solution)/shard_map/ppermute | solution.py:18
  11.0 2.1 %collective-permute-done.13.refs_2_ = bf16[208,128]{1,0:T(8,128)(2,1)S(1)} collective-permute-done((bf16[208,128]{1,0:T(8,128)(2,1)S(1)}, bf16[208,128]{1,0:T(8,128)(2,1)S(1)}, u32[]{:S(2)}, u32[]{:S(2)}) %collective-permute-start.13) | collective-permute-done | bytes 53280 | tf_op jit(solution)/shard_map/ppermute | solution.py:18
  13.1 0.2 collective-permute-start
  13.3 1.6 %collective-permute-done.14.refs_3_ = bf16[208,128]{1,0:T(8,128)(2,1)S(1)} collective-permute-done((bf16[208,128]{1,0:T(8,128)(2,1)S(1)}, bf16[208,128]{1,0:T(8,128)(2,1)S(1)}, u32[]{:S(2)}, u32[]{:S(2)}) %collective-permute-start.14) | collective-permute-done | bytes 53280 | tf_op jit(solution)/shard_map/ppermute | solution.py:18
  15.0 0.1 collective-permute-start.15
  15.1 0.5 %collective-permute-start.4 = (bf16[16,4096]{1,0:T(8,128)(2,1)S(1)}, bf16[16,4096]{1,0:T(8,128)(2,1)S(1)}, u32[]{:S(2)}, u32[]{:S(2)}) collective-permute-start(bf16[16,4096]{1,0:T(8,128)(2,1)S(1)} %pad_maximum_fusion), channel_id=1, source_target_pairs={{0,3},{1,2},{2,1},{3,0},{4,7},{5,6},{6,5},{7,4},{8,11},{9,10},{10,... | collective-permute-start | bytes 393224 | tf_op jit(solution)/shard_map/ppermute | solution.py:18
  15.7 1.5 %collective-permute-start.5 = (bf16[16,4096]{1,0:T(8,128)(2,1)S(1)}, bf16[16,4096]{1,0:T(8,128)(2,1)S(1)}, u32[]{:S(2)}, u32[]{:S(2)}) collective-permute-start(bf16[16,4096]{1,0:T(8,128)(2,1)S(1)} %pad_maximum_fusion), channel_id=1, source_target_pairs={{0,2},{1,3},{2,0},{3,1},{4,6},{5,7},{6,4},{7,5},{8,10},{9,11},{10,... | collective-permute-start | bytes 393224 | tf_op jit(solution)/shard_map/ppermute | solution.py:18
  17.2 2.8 %collective-permute-done.near_ref.refs_0_ = bf16[32,4224]{1,0:T(8,128)(2,1)S(1)} collective-permute-done((bf16[32,4224]{1,0:T(8,128)(2,1)S(1)}, bf16[32,4224]{1,0:T(8,128)(2,1)S(1)}, u32[]{:S(2)}, u32[]{:S(2)}) %collective-permute-start) | collective-permute-done | bytes 270368 | tf_op jit(solution)/shard_map/ppermute | solution.py:18
  19.9 2.1 %collective-permute-done.4.refs_2_ = bf16[16,4096]{1,0:T(8,128)(2,1)S(1)} collective-permute-done((bf16[16,4096]{1,0:T(8,128)(2,1)S(1)}, bf16[16,4096]{1,0:T(8,128)(2,1)S(1)}, u32[]{:S(2)}, u32[]{:S(2)}) %collective-permute-start.4) | collective-permute-done | bytes 131104 | tf_op jit(solution)/shard_map/ppermute | solution.py:18
  22.1 2.0 %collective-permute-done.5.refs_3_ = bf16[16,4096]{1,0:T(8,128)(2,1)S(1)} collective-permute-done((bf16[16,4096]{1,0:T(8,128)(2,1)S(1)}, bf16[16,4096]{1,0:T(8,128)(2,1)S(1)}, u32[]{:S(2)}, u32[]{:S(2)}) %collective-permute-start.5) | collective-permute-done | bytes 131104 | tf_op jit(solution)/shard_map/ppermute | solution.py:18
  24.1 1.2 %collective-permute-start.6 = (bf16[16,4096]{1,0:T(8,128)(2,1)S(1)}, bf16[16,4096]{1,0:T(8,128)(2,1)S(1)}, u32[]{:S(2)}, u32[]{:S(2)}) collective-permute-start(bf16[16,4096]{1,0:T(8,128)(2,1)S(1)} %pad_maximum_fusion), channel_id=1, source_target_pairs={{0,1},{1,0},{2,3},{3,2},{4,5},{5,4},{6,7},{7,6},{8,9},{9,8},{10,11... | collective-permute-start | bytes 393224 | tf_op jit(solution)/shard_map/ppermute | solution.py:18
  25.3 3.7 %collective-permute-done.6.refs_4_ = bf16[16,4096]{1,0:T(8,128)(2,1)S(1)} collective-permute-done((bf16[16,4096]{1,0:T(8,128)(2,1)S(1)}, bf16[16,4096]{1,0:T(8,128)(2,1)S(1)}, u32[]{:S(2)}, u32[]{:S(2)}) %collective-permute-start.6) | collective-permute-done | bytes 131104 | tf_op jit(solution)/shard_map/ppermute | solution.py:18
  29.0 0.5 %collective-permute-start.8 = (bf16[16,4096]{1,0:T(8,128)(2,1)S(1)}, bf16[16,4096]{1,0:T(8,128)(2,1)S(1)}, u32[]{:S(2)}, u32[]{:S(2)}) collective-permute-start(bf16[16,4096]{1,0:T(8,128)(2,1)S(1)} %collective-permute-done.5.refs_3_), channel_id=1, source_target_pairs={{0,4},{4,0},{1,5},{5,1},{2,6},{6,2},{3,7},{7,3},{8,12},{12,8},{9,1... | collective-permute-start | bytes 393224 | tf_op jit(solution)/shard_map/ppermute | solution.py:18
  29.6 1.6 %shard_map.86 = (f32[1536,128]{1,0:T(8,128)S(1)}, bf16[2048,192]{1,0:T(8,128)(2,1)S(1)}, bf16[4096,256]{1,0:T(8,128)(2,1)S(1)}, bf16[32,2048]{1,0:T(8,128)(2,1)S(1)}, bf16[1536,512]{1,0:T(8,128)(2,1)S(1)}) custom-call(bf16[32,4224]{1,0:T(8,128)(2,1)S(1)} %get-tuple-element.14.refs_0_, bf16[16,4224]{1,0:T(8,128)(2,1)S(1)} %constant_dynamic-update-slice_fusion.far_ref.refs_1_, ...), custom_call_target="tpu_custom_call" | custom-call | tf_op jit(solution)/shard_map/pallas_call | solution.py:371
  31.2 0.4 shard_map.83.refs_8_
  31.7 4.7 %shard_map.87 = f32[2,128,512]{2,1,0:T(8,128)} custom-call(bf16[32,4224]{1,0:T(8,128)(2,1)S(1)} %collective-permute-done.near_ref.refs_0_, bf16[32,4224]{1,0:T(8,128)(2,1)S(1)} %collective-permute-done.1.near_other_ref.refs_1_, bf16[16,4096]{1,0:T(8,128)(2,1)S(1)} %collective-permute-done.4.refs_2_, bf16[16,4096]{1,0:T(8,128)(2,1)S(1)} %collective-permute-done.5.refs_3_, ...), custom_call_target="tpu_custom_call" | custom-call | tf_op jit(solution)/shard_map/pallas_call | solution.py:381
  (27 shorter events, 0.2 us)
Async XLA Ops:
  0.0 31.6 %copy-start = (bf16[2,128,512]{2,1,0:T(8,128)(2,1)S(1)}, bf16[2,128,512]{2,1,0:T(8,128)(2,1)}, u32[]{:S(2)}) copy-start(bf16[2,128,512]{2,1,0:T(8,128)(2,1)} %refs_14_.1) | copy-start | bytes 786436
  0.0 31.6 %copy-start.1 = (f32[2]{0:T(128)S(1)}, f32[2]{0:T(128)}, u32[]{:S(2)}) copy-start(f32[2]{0:T(128)} %refs_15_.1) | copy-start | bytes 28
  1.1 13.9 %collective-permute-start.2 = (bf16[8,4224]{1,0:T(8,128)(2,1)S(1)}, bf16[8,4224]{1,0:T(8,128)(2,1)S(1)}, u32[]{:S(2)}, u32[]{:S(2)}) collective-permute-start(bf16[8,4224]{1,0:T(8,128)(2,1)S(1)} %constant_dynamic-slice_fusion), channel_id=1, source_target_pairs={{0,16},{8,24},{16,0},{24,8},{1,17},{9,25},{17,1},{25,9},{2,18},{10... | collective-permute-start | bytes 202760 | tf_op jit(solution)/shard_map/ppermute | solution.py:18
  5.2 9.8 %collective-permute-start.3 = (bf16[8,4224]{1,0:T(8,128)(2,1)S(1)}, bf16[8,4224]{1,0:T(8,128)(2,1)S(1)}, u32[]{:S(2)}, u32[]{:S(2)}) collective-permute-start(bf16[8,4224]{1,0:T(8,128)(2,1)S(1)} %constant_dynamic-slice_fusion), channel_id=1, source_target_pairs={{0,24},{8,16},{16,8},{24,0},{1,25},{9,17},{17,9},{25,1},{2,26},{10... | collective-permute-start | bytes 202760 | tf_op jit(solution)/shard_map/ppermute | solution.py:18
  6.8 4.2 %collective-permute-start.12 = (bf16[208,128]{1,0:T(8,128)(2,1)S(1)}, bf16[208,128]{1,0:T(8,128)(2,1)S(1)}, u32[]{:S(2)}, u32[]{:S(2)}) collective-permute-start(bf16[208,128]{1,0:T(8,128)(2,1)S(1)} %fusion.1.refs_0_), channel_id=1, source_target_pairs={{0,1},{1,0},{2,3},{3,2},{4,5},{5,4},{6,7},{7,6},{8,9},{9,8},{10,11... | collective-permute-start | bytes 159752 | tf_op jit(solution)/shard_map/ppermute | solution.py:18
  8.4 4.7 %collective-permute-start.13 = (bf16[208,128]{1,0:T(8,128)(2,1)S(1)}, bf16[208,128]{1,0:T(8,128)(2,1)S(1)}, u32[]{:S(2)}, u32[]{:S(2)}) collective-permute-start(bf16[208,128]{1,0:T(8,128)(2,1)S(1)} %fusion.1.refs_0_), channel_id=1, source_target_pairs={{0,2},{1,3},{2,0},{3,1},{4,6},{5,7},{6,4},{7,5},{8,10},{9,11},{10,... | collective-permute-start | bytes 159752 | tf_op jit(solution)/shard_map/ppermute | solution.py:18
  9.9 5.0 %collective-permute-start.14 = (bf16[208,128]{1,0:T(8,128)(2,1)S(1)}, bf16[208,128]{1,0:T(8,128)(2,1)S(1)}, u32[]{:S(2)}, u32[]{:S(2)}) collective-permute-start(bf16[208,128]{1,0:T(8,128)(2,1)S(1)} %fusion.1.refs_0_), channel_id=1, source_target_pairs={{0,3},{1,2},{2,1},{3,0},{4,7},{5,6},{6,5},{7,4},{8,11},{9,10},{10,... | collective-permute-start | bytes 159752 | tf_op jit(solution)/shard_map/ppermute | solution.py:18
  11.0 18.6 %collective-permute-start.11 = (bf16[32,4224]{1,0:T(8,128)(2,1)S(1)}, bf16[32,4224]{1,0:T(8,128)(2,1)S(1)}, u32[]{:S(2)}, u32[]{:S(2)}) collective-permute-start(bf16[32,4224]{1,0:T(8,128)(2,1)S(1)} %get-tuple-element.14.refs_0_), channel_id=1, source_target_pairs={{0,4},{4,0},{1,5},{5,1},{2,6},{6,2},{3,7},{7,3},{8,12},{12,8},{9,1... | collective-permute-start | bytes 811016 | tf_op jit(solution)/shard_map/ppermute | solution.py:18
  13.1 6.8 %collective-permute-start = (bf16[32,4224]{1,0:T(8,128)(2,1)S(1)}, bf16[32,4224]{1,0:T(8,128)(2,1)S(1)}, u32[]{:S(2)}, u32[]{:S(2)}) collective-permute-start(bf16[32,4224]{1,0:T(8,128)(2,1)S(1)} %get-tuple-element.14.refs_0_), channel_id=1, source_target_pairs={{0,8},{8,0},{16,24},{24,16},{1,9},{9,1},{17,25},{25,17},{2,10},{10... | collective-permute-start | bytes 811016 | tf_op jit(solution)/shard_map/ppermute | solution.py:18
  15.0 14.6 %collective-permute-start.15 = (bf16[832,128]{1,0:T(8,128)(2,1)S(1)}, bf16[832,128]{1,0:T(8,128)(2,1)S(1)}, u32[]{:S(2)}, u32[]{:S(2)}) collective-permute-start(bf16[832,128]{1,0:T(8,128)(2,1)S(1)} %shard_map.85.refs_4_), channel_id=1, source_target_pairs={{0,4},{4,0},{1,5},{5,1},{2,6},{6,2},{3,7},{7,3},{8,12},{12,8},{9,1... | collective-permute-start | bytes 638984 | tf_op jit(solution)/shard_map/ppermute | solution.py:18
  15.1 7.0 %collective-permute-start.4 = (bf16[16,4096]{1,0:T(8,128)(2,1)S(1)}, bf16[16,4096]{1,0:T(8,128)(2,1)S(1)}, u32[]{:S(2)}, u32[]{:S(2)}) collective-permute-start(bf16[16,4096]{1,0:T(8,128)(2,1)S(1)} %pad_maximum_fusion), channel_id=1, source_target_pairs={{0,3},{1,2},{2,1},{3,0},{4,7},{5,6},{6,5},{7,4},{8,11},{9,10},{10,... | collective-permute-start | bytes 393224 | tf_op jit(solution)/shard_map/ppermute | solution.py:18
  15.7 8.4 %collective-permute-start.5 = (bf16[16,4096]{1,0:T(8,128)(2,1)S(1)}, bf16[16,4096]{1,0:T(8,128)(2,1)S(1)}, u32[]{:S(2)}, u32[]{:S(2)}) collective-permute-start(bf16[16,4096]{1,0:T(8,128)(2,1)S(1)} %pad_maximum_fusion), channel_id=1, source_target_pairs={{0,2},{1,3},{2,0},{3,1},{4,6},{5,7},{6,4},{7,5},{8,10},{9,11},{10,... | collective-permute-start | bytes 393224 | tf_op jit(solution)/shard_map/ppermute | solution.py:18
  19.9 11.3 %collective-permute-start.1 = (bf16[32,4224]{1,0:T(8,128)(2,1)S(1)}, bf16[32,4224]{1,0:T(8,128)(2,1)S(1)}, u32[]{:S(2)}, u32[]{:S(2)}) collective-permute-start(bf16[32,4224]{1,0:T(8,128)(2,1)S(1)} %collective-permute-done.near_ref.refs_0_), channel_id=1, source_target_pairs={{0,4},{4,0},{1,5},{5,1},{2,6},{6,2},{3,7},{7,3},{8,12},{12,8},{9,1... | collective-permute-start | bytes 811016 | tf_op jit(solution)/shard_map/ppermute | solution.py:18
  22.1 7.0 %collective-permute-start.10 = (bf16[16,4224]{1,0:T(8,128)(2,1)S(1)}, bf16[16,4224]{1,0:T(8,128)(2,1)S(1)}, u32[]{:S(2)}, u32[]{:S(2)}) collective-permute-start(bf16[16,4224]{1,0:T(8,128)(2,1)S(1)} %constant_dynamic-update-slice_fusion.far_ref.refs_1_), channel_id=1, source_target_pairs={{0,4},{4,0},{1,5},{5,1},{2,6},{6,2},{3,7},{7,3},{8,12},{12,8},{9,1... | collective-permute-start | bytes 405512 | tf_op jit(solution)/shard_map/ppermute | solution.py:18
  24.1 5.0 %collective-permute-start.6 = (bf16[16,4096]{1,0:T(8,128)(2,1)S(1)}, bf16[16,4096]{1,0:T(8,128)(2,1)S(1)}, u32[]{:S(2)}, u32[]{:S(2)}) collective-permute-start(bf16[16,4096]{1,0:T(8,128)(2,1)S(1)} %pad_maximum_fusion), channel_id=1, source_target_pairs={{0,1},{1,0},{2,3},{3,2},{4,5},{5,4},{6,7},{7,6},{8,9},{9,8},{10,11... | collective-permute-start | bytes 393224 | tf_op jit(solution)/shard_map/ppermute | solution.py:18
  29.0 2.6 %collective-permute-start.7 = (bf16[16,4096]{1,0:T(8,128)(2,1)S(1)}, bf16[16,4096]{1,0:T(8,128)(2,1)S(1)}, u32[]{:S(2)}, u32[]{:S(2)}) collective-permute-start(bf16[16,4096]{1,0:T(8,128)(2,1)S(1)} %collective-permute-done.4.refs_2_), channel_id=1, source_target_pairs={{0,4},{4,0},{1,5},{5,1},{2,6},{6,2},{3,7},{7,3},{8,12},{12,8},{9,1... | collective-permute-start | bytes 393224 | tf_op jit(solution)/shard_map/ppermute | solution.py:18
  29.0 2.6 %collective-permute-start.8 = (bf16[16,4096]{1,0:T(8,128)(2,1)S(1)}, bf16[16,4096]{1,0:T(8,128)(2,1)S(1)}, u32[]{:S(2)}, u32[]{:S(2)}) collective-permute-start(bf16[16,4096]{1,0:T(8,128)(2,1)S(1)} %collective-permute-done.5.refs_3_), channel_id=1, source_target_pairs={{0,4},{4,0},{1,5},{5,1},{2,6},{6,2},{3,7},{7,3},{8,12},{12,8},{9,1... | collective-permute-start | bytes 393224 | tf_op jit(solution)/shard_map/ppermute | solution.py:18
  29.6 2.1 %collective-permute-start.9 = (bf16[16,4096]{1,0:T(8,128)(2,1)S(1)}, bf16[16,4096]{1,0:T(8,128)(2,1)S(1)}, u32[]{:S(2)}, u32[]{:S(2)}) collective-permute-start(bf16[16,4096]{1,0:T(8,128)(2,1)S(1)} %collective-permute-done.6.refs_4_), channel_id=1, source_target_pairs={{0,4},{4,0},{1,5},{5,1},{2,6},{6,2},{3,7},{7,3},{8,12},{12,8},{9,1... | collective-permute-start | bytes 393224 | tf_op jit(solution)/shard_map/ppermute | solution.py:18

commit v5 on v4

--- a/solution.py
+++ b/solution.py
@@ -202,9 +202,9 @@
 
 
 def late_kernel(dims, width, block, kinds, *refs):
-    chunks = refs[:-13]
-    (pick_ref, before_ref, rows_ref, main_ref, edge_ref, wide_ref, obs_ref, inv_ref, out_ref) = refs[-13:-4]
-    sums_ref, image_ref, mid_ref, side_ref = refs[-4:]
+    chunks = refs[:-15]
+    (pick_ref, before_ref, rows_ref, main_ref, edge_ref, wide_ref, obs_ref, inv_ref, out_ref) = refs[-15:-6]
+    sums_ref, image_ref, mid_ref, side_ref, out_buf, out_sems = refs[-6:]
     _, _, _, col_grid, band_grid, strips, exp_local, _ = dims
     blocks = exp_local * strips * col_grid
     pitch = sums_ref.shape[0] // (width // LANES)
@@ -256,6 +256,7 @@
     )
     gap = jnp.zeros((LANES - 2 * spill, tall2), jnp.float32)
     side = jnp.concatenate([side[:spill], gap, side[spill:]], axis=0).T
+    copies = []
     low_all = lax.broadcasted_iota(jnp.int32, (tall2, LANES), 1) < block
     mains = jnp.dot(mid_ref[...], main_ref[...], preferred_element_type=jnp.float32)
     for w in range(2):
@@ -269,7 +270,13 @@
                 if t == 1 - w:
                     model = model + edge[rows]
                 cols = slice(w * window + t * LANES, w * window + (t + 1) * LANES)
-                out_ref[x, :, cols] = noise * (obs_ref[x, :, cols].astype(jnp.float32) - model)
+                out_buf[x, :, cols] = noise * (obs_ref[x, :, cols].astype(jnp.float32) - model)
+            cols = slice(w * window, (w + 1) * window)
+            copy = pltpu.make_async_copy(out_buf.at[x, :, cols], out_ref.at[x, :, cols], out_sems.at[w, x])
+            copy.start()
+            copies.append(copy)
+    for copy in copies:
+        copy.wait()
 
 
 def gathered_device(
@@ -382,12 +389,14 @@
         functools.partial(late_kernel, dims, width, block, kinds),
         out_shape=jax.ShapeDtypeStruct(observed.shape, f32),
         in_specs=in_vmem(len(late)) + [pl.BlockSpec(memory_space=pltpu.SMEM)],
-        out_specs=pl.BlockSpec(memory_space=pltpu.VMEM),
+        out_specs=pl.BlockSpec(memory_space=pltpu.HBM),
         scratch_shapes=[
             pltpu.VMEM((width // LANES * (blocks + ROW_PAD), LANES), f32),
             pltpu.VMEM((exp_local, strips * block, tile_cols), bf16),
             pltpu.VMEM((2 * exp_local * band_rows, kinds * 4 * block), bf16),
             pltpu.VMEM((exp_local * band_rows, kinds * LANES), bf16),
+            pltpu.VMEM(observed.shape, f32),
+            pltpu.SemaphoreType.DMA((2, exp_local)),
         ],
         compiler_params=params,
     )(*late, inv_variance)

time: 36.5 us -> 36.4 us (level)
  no operation moved by 1% of the time
where the time goes in v5:
time: 36.4 us; the launch traced here: 36.3 us
  waiting for transfers between devices  14.9 us (41%)
  starting transfers between devices  13.2 us (36%)
  Pallas kernels  7.74 us (21%)
    ppermute x16, waiting for transfers between devices, swapped(): return lax.ppermute(value, axis, [(i, i ^ by) for i in range(length)])  14.9 us
    ppermute x16, starting transfers between devices, swapped(): return lax.ppermute(value, axis, [(i, i ^ by) for i in range(length)])  13.2 us
    pallas_call x1, Pallas kernels, gathered_device(): pl.pallas_call(functools.partial(late_kernel, dims, width, block, kinds),...  4.6 us
    pallas_call x1, Pallas kernels, gathered_device(): prepared = early_call(*early)  1.59 us
    pallas_call x1, Pallas kernels, gathered_device(): pl.pallas_call(pack_kernel, out_shape=[jax.ShapeDtypeStruct((patch_count,...  1.08 us
  transfers between devices with their start and end apart: 16, of which 7 were waited for; matrix products, arithmetic and copies ran while one was open for 0% of the time, Pallas kernels for 6%

profile of v5, /device:TPU:0, one launch (start us, length us, event | category | flops | bytes accessed | tf_op | source)
XLA Modules:
  0.0 36.3 jit_solution(13370448647662958223)
XLA Ops:
  0.0 1.1 %shard_map.82 = (bf16[32,4224]{1,0:T(8,128)(2,1)S(1)}, bf16[4,64,96]{2,1,0:T(8,128)(2,1)S(1)}, bf16[4,64,96]{2,1,0:T(8,128)(2,1)S(1)}, bf16[8,4,2,8]{3,2,1,0:T(2,128)(2,1)S(1)}) custom-call(bf16[32,4096]{1,0:T(8,128)(2,1)} %patch_ref.1, s32[4,32]{1,0:T(4,128)} %bitcast.8, s32[4,32]{1,0:T(4,128)} %bitcast.9, bf16[4,64,96]{2,1,0:T(8,128)(2,1)} %bitcast.6, ...), custom_call_target="tpu_custom_call" | custom-call | tf_op jit(solution)/shard_map/pallas_call | solution.py:311
  1.1 4.1 %collective-permute-start.2 = (bf16[8,4224]{1,0:T(8,128)(2,1)S(1)}, bf16[8,4224]{1,0:T(8,128)(2,1)S(1)}, u32[]{:S(2)}, u32[]{:S(2)}) collective-permute-start(bf16[8,4224]{1,0:T(8,128)(2,1)S(1)} %constant_dynamic-slice_fusion), channel_id=1, source_target_pairs={{0,16},{8,24},{16,0},{24,8},{1,17},{9,25},{17,1},{25,9},{2,18},{10... | collective-permute-start | bytes 202760 | tf_op jit(solution)/shard_map/ppermute | solution.py:18
  5.2 1.3 %collective-permute-start.3 = (bf16[8,4224]{1,0:T(8,128)(2,1)S(1)}, bf16[8,4224]{1,0:T(8,128)(2,1)S(1)}, u32[]{:S(2)}, u32[]{:S(2)}) collective-permute-start(bf16[8,4224]{1,0:T(8,128)(2,1)S(1)} %constant_dynamic-slice_fusion), channel_id=1, source_target_pairs={{0,24},{8,16},{16,8},{24,0},{1,25},{9,17},{17,9},{25,1},{2,26},{10... | collective-permute-start | bytes 202760 | tf_op jit(solution)/shard_map/ppermute | solution.py:18
  6.6 0.1 reshape.3
  6.7 0.1 shard_map.84
  6.8 1.6 %collective-permute-start.12 = (bf16[208,128]{1,0:T(8,128)(2,1)S(1)}, bf16[208,128]{1,0:T(8,128)(2,1)S(1)}, u32[]{:S(2)}, u32[]{:S(2)}) collective-permute-start(bf16[208,128]{1,0:T(8,128)(2,1)S(1)} %fusion.1.refs_0_), channel_id=1, source_target_pairs={{0,1},{1,0},{2,3},{3,2},{4,5},{5,4},{6,7},{7,6},{8,9},{9,8},{10,11... | collective-permute-start | bytes 159752 | tf_op jit(solution)/shard_map/ppermute | solution.py:18
  8.4 1.5 %collective-permute-start.13 = (bf16[208,128]{1,0:T(8,128)(2,1)S(1)}, bf16[208,128]{1,0:T(8,128)(2,1)S(1)}, u32[]{:S(2)}, u32[]{:S(2)}) collective-permute-start(bf16[208,128]{1,0:T(8,128)(2,1)S(1)} %fusion.1.refs_0_), channel_id=1, source_target_pairs={{0,2},{1,3},{2,0},{3,1},{4,6},{5,7},{6,4},{7,5},{8,10},{9,11},{10,... | collective-permute-start | bytes 159752 | tf_op jit(solution)/shard_map/ppermute | solution.py:18
  9.9 0.5 %collective-permute-start.14 = (bf16[208,128]{1,0:T(8,128)(2,1)S(1)}, bf16[208,128]{1,0:T(8,128)(2,1)S(1)}, u32[]{:S(2)}, u32[]{:S(2)}) collective-permute-start(bf16[208,128]{1,0:T(8,128)(2,1)S(1)} %fusion.1.refs_0_), channel_id=1, source_target_pairs={{0,3},{1,2},{2,1},{3,0},{4,7},{5,6},{6,5},{7,4},{8,11},{9,10},{10,... | collective-permute-start | bytes 159752 | tf_op jit(solution)/shard_map/ppermute | solution.py:18
  10.4 0.6 %collective-permute-done.12.refs_1_ = bf16[208,128]{1,0:T(8,128)(2,1)S(1)} collective-permute-done((bf16[208,128]{1,0:T(8,128)(2,1)S(1)}, bf16[208,128]{1,0:T(8,128)(2,1)S(1)}, u32[]{:S(2)}, u32[]{:S(2)}) %collective-permute-start.12) | collective-permute-done | bytes 53280 | tf_op jit(solution)/shard_map/ppermute | solution.py:18
  11.0 2.1 %collective-permute-done.13.refs_2_ = bf16[208,128]{1,0:T(8,128)(2,1)S(1)} collective-permute-done((bf16[208,128]{1,0:T(8,128)(2,1)S(1)}, bf16[208,128]{1,0:T(8,128)(2,1)S(1)}, u32[]{:S(2)}, u32[]{:S(2)}) %collective-permute-start.13) | collective-permute-done | bytes 53280 | tf_op jit(solution)/shard_map/ppermute | solution.py:18
  13.1 0.2 collective-permute-start
  13.3 1.6 %collective-permute-done.14.refs_3_ = bf16[208,128]{1,0:T(8,128)(2,1)S(1)} collective-permute-done((bf16[208,128]{1,0:T(8,128)(2,1)S(1)}, bf16[208,128]{1,0:T(8,128)(2,1)S(1)}, u32[]{:S(2)}, u32[]{:S(2)}) %collective-permute-start.14) | collective-permute-done | bytes 53280 | tf_op jit(solution)/shard_map/ppermute | solution.py:18
  15.0 0.1 collective-permute-start.15
  15.1 0.5 %collective-permute-start.4 = (bf16[16,4096]{1,0:T(8,128)(2,1)S(1)}, bf16[16,4096]{1,0:T(8,128)(2,1)S(1)}, u32[]{:S(2)}, u32[]{:S(2)}) collective-permute-start(bf16[16,4096]{1,0:T(8,128)(2,1)S(1)} %pad_maximum_fusion), channel_id=1, source_target_pairs={{0,3},{1,2},{2,1},{3,0},{4,7},{5,6},{6,5},{7,4},{8,11},{9,10},{10,... | collective-permute-start | bytes 393224 | tf_op jit(solution)/shard_map/ppermute | solution.py:18
  15.7 1.5 %collective-permute-start.5 = (bf16[16,4096]{1,0:T(8,128)(2,1)S(1)}, bf16[16,4096]{1,0:T(8,128)(2,1)S(1)}, u32[]{:S(2)}, u32[]{:S(2)}) collective-permute-start(bf16[16,4096]{1,0:T(8,128)(2,1)S(1)} %pad_maximum_fusion), channel_id=1, source_target_pairs={{0,2},{1,3},{2,0},{3,1},{4,6},{5,7},{6,4},{7,5},{8,10},{9,11},{10,... | collective-permute-start | bytes 393224 | tf_op jit(solution)/shard_map/ppermute | solution.py:18
  17.2 2.8 %collective-permute-done.near_ref.refs_0_ = bf16[32,4224]{1,0:T(8,128)(2,1)S(1)} collective-permute-done((bf16[32,4224]{1,0:T(8,128)(2,1)S(1)}, bf16[32,4224]{1,0:T(8,128)(2,1)S(1)}, u32[]{:S(2)}, u32[]{:S(2)}) %collective-permute-start) | collective-permute-done | bytes 270368 | tf_op jit(solution)/shard_map/ppermute | solution.py:18
  19.9 2.1 %collective-permute-done.4.refs_2_ = bf16[16,4096]{1,0:T(8,128)(2,1)S(1)} collective-permute-done((bf16[16,4096]{1,0:T(8,128)(2,1)S(1)}, bf16[16,4096]{1,0:T(8,128)(2,1)S(1)}, u32[]{:S(2)}, u32[]{:S(2)}) %collective-permute-start.4) | collective-permute-done | bytes 131104 | tf_op jit(solution)/shard_map/ppermute | solution.py:18
  22.1 2.0 %collective-permute-done.5.refs_3_ = bf16[16,4096]{1,0:T(8,128)(2,1)S(1)} collective-permute-done((bf16[16,4096]{1,0:T(8,128)(2,1)S(1)}, bf16[16,4096]{1,0:T(8,128)(2,1)S(1)}, u32[]{:S(2)}, u32[]{:S(2)}) %collective-permute-start.5) | collective-permute-done | bytes 131104 | tf_op jit(solution)/shard_map/ppermute | solution.py:18
  24.1 1.2 %collective-permute-start.6 = (bf16[16,4096]{1,0:T(8,128)(2,1)S(1)}, bf16[16,4096]{1,0:T(8,128)(2,1)S(1)}, u32[]{:S(2)}, u32[]{:S(2)}) collective-permute-start(bf16[16,4096]{1,0:T(8,128)(2,1)S(1)} %pad_maximum_fusion), channel_id=1, source_target_pairs={{0,1},{1,0},{2,3},{3,2},{4,5},{5,4},{6,7},{7,6},{8,9},{9,8},{10,11... | collective-permute-start | bytes 393224 | tf_op jit(solution)/shard_map/ppermute | solution.py:18
  25.3 3.7 %collective-permute-done.6.refs_4_ = bf16[16,4096]{1,0:T(8,128)(2,1)S(1)} collective-permute-done((bf16[16,4096]{1,0:T(8,128)(2,1)S(1)}, bf16[16,4096]{1,0:T(8,128)(2,1)S(1)}, u32[]{:S(2)}, u32[]{:S(2)}) %collective-permute-start.6) | collective-permute-done | bytes 131104 | tf_op jit(solution)/shard_map/ppermute | solution.py:18
  29.0 0.5 %collective-permute-start.8 = (bf16[16,4096]{1,0:T(8,128)(2,1)S(1)}, bf16[16,4096]{1,0:T(8,128)(2,1)S(1)}, u32[]{:S(2)}, u32[]{:S(2)}) collective-permute-start(bf16[16,4096]{1,0:T(8,128)(2,1)S(1)} %collective-permute-done.5.refs_3_), channel_id=1, source_target_pairs={{0,4},{4,0},{1,5},{5,1},{2,6},{6,2},{3,7},{7,3},{8,12},{12,8},{9,1... | collective-permute-start | bytes 393224 | tf_op jit(solution)/shard_map/ppermute | solution.py:18
  29.6 1.6 %shard_map.86 = (f32[1536,128]{1,0:T(8,128)S(1)}, bf16[2048,192]{1,0:T(8,128)(2,1)S(1)}, bf16[4096,256]{1,0:T(8,128)(2,1)S(1)}, bf16[32,2048]{1,0:T(8,128)(2,1)S(1)}, bf16[1536,512]{1,0:T(8,128)(2,1)S(1)}) custom-call(bf16[32,4224]{1,0:T(8,128)(2,1)S(1)} %get-tuple-element.14.refs_0_, bf16[16,4224]{1,0:T(8,128)(2,1)S(1)} %constant_dynamic-update-slice_fusion.far_ref.refs_1_, ...), custom_call_target="tpu_custom_call" | custom-call | tf_op jit(solution)/shard_map/pallas_call | solution.py:378
  31.2 0.4 shard_map.83.refs_8_
  31.7 4.6 %shard_map.87 = f32[2,128,512]{2,1,0:T(8,128)} custom-call(bf16[32,4224]{1,0:T(8,128)(2,1)S(1)} %collective-permute-done.near_ref.refs_0_, bf16[32,4224]{1,0:T(8,128)(2,1)S(1)} %collective-permute-done.1.near_other_ref.refs_1_, bf16[16,4096]{1,0:T(8,128)(2,1)S(1)} %collective-permute-done.4.refs_2_, bf16[16,4096]{1,0:T(8,128)(2,1)S(1)} %collective-permute-done.5.refs_3_, ...), custom_call_target="tpu_custom_call" | custom-call | tf_op jit(solution)/shard_map/pallas_call | solution.py:388
  (27 shorter events, 0.2 us)
Async XLA Ops:
  0.0 31.6 %copy-start = (bf16[2,128,512]{2,1,0:T(8,128)(2,1)S(1)}, bf16[2,128,512]{2,1,0:T(8,128)(2,1)}, u32[]{:S(2)}) copy-start(bf16[2,128,512]{2,1,0:T(8,128)(2,1)} %refs_14_.1) | copy-start | bytes 786436
  0.0 31.6 %copy-start.1 = (f32[2]{0:T(128)S(1)}, f32[2]{0:T(128)}, u32[]{:S(2)}) copy-start(f32[2]{0:T(128)} %refs_15_.1) | copy-start | bytes 28
  1.1 13.9 %collective-permute-start.2 = (bf16[8,4224]{1,0:T(8,128)(2,1)S(1)}, bf16[8,4224]{1,0:T(8,128)(2,1)S(1)}, u32[]{:S(2)}, u32[]{:S(2)}) collective-permute-start(bf16[8,4224]{1,0:T(8,128)(2,1)S(1)} %constant_dynamic-slice_fusion), channel_id=1, source_target_pairs={{0,16},{8,24},{16,0},{24,8},{1,17},{9,25},{17,1},{25,9},{2,18},{10... | collective-permute-start | bytes 202760 | tf_op jit(solution)/shard_map/ppermute | solution.py:18
  5.2 9.8 %collective-permute-start.3 = (bf16[8,4224]{1,0:T(8,128)(2,1)S(1)}, bf16[8,4224]{1,0:T(8,128)(2,1)S(1)}, u32[]{:S(2)}, u32[]{:S(2)}) collective-permute-start(bf16[8,4224]{1,0:T(8,128)(2,1)S(1)} %constant_dynamic-slice_fusion), channel_id=1, source_target_pairs={{0,24},{8,16},{16,8},{24,0},{1,25},{9,17},{17,9},{25,1},{2,26},{10... | collective-permute-start | bytes 202760 | tf_op jit(solution)/shard_map/ppermute | solution.py:18
  6.8 4.2 %collective-permute-start.12 = (bf16[208,128]{1,0:T(8,128)(2,1)S(1)}, bf16[208,128]{1,0:T(8,128)(2,1)S(1)}, u32[]{:S(2)}, u32[]{:S(2)}) collective-permute-start(bf16[208,128]{1,0:T(8,128)(2,1)S(1)} %fusion.1.refs_0_), channel_id=1, source_target_pairs={{0,1},{1,0},{2,3},{3,2},{4,5},{5,4},{6,7},{7,6},{8,9},{9,8},{10,11... | collective-permute-start | bytes 159752 | tf_op jit(solution)/shard_map/ppermute | solution.py:18
  8.4 4.7 %collective-permute-start.13 = (bf16[208,128]{1,0:T(8,128)(2,1)S(1)}, bf16[208,128]{1,0:T(8,128)(2,1)S(1)}, u32[]{:S(2)}, u32[]{:S(2)}) collective-permute-start(bf16[208,128]{1,0:T(8,128)(2,1)S(1)} %fusion.1.refs_0_), channel_id=1, source_target_pairs={{0,2},{1,3},{2,0},{3,1},{4,6},{5,7},{6,4},{7,5},{8,10},{9,11},{10,... | collective-permute-start | bytes 159752 | tf_op jit(solution)/shard_map/ppermute | solution.py:18
  9.9 5.0 %collective-permute-start.14 = (bf16[208,128]{1,0:T(8,128)(2,1)S(1)}, bf16[208,128]{1,0:T(8,128)(2,1)S(1)}, u32[]{:S(2)}, u32[]{:S(2)}) collective-permute-start(bf16[208,128]{1,0:T(8,128)(2,1)S(1)} %fusion.1.refs_0_), channel_id=1, source_target_pairs={{0,3},{1,2},{2,1},{3,0},{4,7},{5,6},{6,5},{7,4},{8,11},{9,10},{10,... | collective-permute-start | bytes 159752 | tf_op jit(solution)/shard_map/ppermute | solution.py:18
  11.0 18.6 %collective-permute-start.11 = (bf16[32,4224]{1,0:T(8,128)(2,1)S(1)}, bf16[32,4224]{1,0:T(8,128)(2,1)S(1)}, u32[]{:S(2)}, u32[]{:S(2)}) collective-permute-start(bf16[32,4224]{1,0:T(8,128)(2,1)S(1)} %get-tuple-element.14.refs_0_), channel_id=1, source_target_pairs={{0,4},{4,0},{1,5},{5,1},{2,6},{6,2},{3,7},{7,3},{8,12},{12,8},{9,1... | collective-permute-start | bytes 811016 | tf_op jit(solution)/shard_map/ppermute | solution.py:18
  13.1 6.8 %collective-permute-start = (bf16[32,4224]{1,0:T(8,128)(2,1)S(1)}, bf16[32,4224]{1,0:T(8,128)(2,1)S(1)}, u32[]{:S(2)}, u32[]{:S(2)}) collective-permute-start(bf16[32,4224]{1,0:T(8,128)(2,1)S(1)} %get-tuple-element.14.refs_0_), channel_id=1, source_target_pairs={{0,8},{8,0},{16,24},{24,16},{1,9},{9,1},{17,25},{25,17},{2,10},{10... | collective-permute-start | bytes 811016 | tf_op jit(solution)/shard_map/ppermute | solution.py:18
  15.0 14.6 %collective-permute-start.15 = (bf16[832,128]{1,0:T(8,128)(2,1)S(1)}, bf16[832,128]{1,0:T(8,128)(2,1)S(1)}, u32[]{:S(2)}, u32[]{:S(2)}) collective-permute-start(bf16[832,128]{1,0:T(8,128)(2,1)S(1)} %shard_map.85.refs_4_), channel_id=1, source_target_pairs={{0,4},{4,0},{1,5},{5,1},{2,6},{6,2},{3,7},{7,3},{8,12},{12,8},{9,1... | collective-permute-start | bytes 638984 | tf_op jit(solution)/shard_map/ppermute | solution.py:18
  15.1 7.0 %collective-permute-start.4 = (bf16[16,4096]{1,0:T(8,128)(2,1)S(1)}, bf16[16,4096]{1,0:T(8,128)(2,1)S(1)}, u32[]{:S(2)}, u32[]{:S(2)}) collective-permute-start(bf16[16,4096]{1,0:T(8,128)(2,1)S(1)} %pad_maximum_fusion), channel_id=1, source_target_pairs={{0,3},{1,2},{2,1},{3,0},{4,7},{5,6},{6,5},{7,4},{8,11},{9,10},{10,... | collective-permute-start | bytes 393224 | tf_op jit(solution)/shard_map/ppermute | solution.py:18
  15.7 8.4 %collective-permute-start.5 = (bf16[16,4096]{1,0:T(8,128)(2,1)S(1)}, bf16[16,4096]{1,0:T(8,128)(2,1)S(1)}, u32[]{:S(2)}, u32[]{:S(2)}) collective-permute-start(bf16[16,4096]{1,0:T(8,128)(2,1)S(1)} %pad_maximum_fusion), channel_id=1, source_target_pairs={{0,2},{1,3},{2,0},{3,1},{4,6},{5,7},{6,4},{7,5},{8,10},{9,11},{10,... | collective-permute-start | bytes 393224 | tf_op jit(solution)/shard_map/ppermute | solution.py:18
  19.9 11.3 %collective-permute-start.1 = (bf16[32,4224]{1,0:T(8,128)(2,1)S(1)}, bf16[32,4224]{1,0:T(8,128)(2,1)S(1)}, u32[]{:S(2)}, u32[]{:S(2)}) collective-permute-start(bf16[32,4224]{1,0:T(8,128)(2,1)S(1)} %collective-permute-done.near_ref.refs_0_), channel_id=1, source_target_pairs={{0,4},{4,0},{1,5},{5,1},{2,6},{6,2},{3,7},{7,3},{8,12},{12,8},{9,1... | collective-permute-start | bytes 811016 | tf_op jit(solution)/shard_map/ppermute | solution.py:18
  22.1 7.0 %collective-permute-start.10 = (bf16[16,4224]{1,0:T(8,128)(2,1)S(1)}, bf16[16,4224]{1,0:T(8,128)(2,1)S(1)}, u32[]{:S(2)}, u32[]{:S(2)}) collective-permute-start(bf16[16,4224]{1,0:T(8,128)(2,1)S(1)} %constant_dynamic-update-slice_fusion.far_ref.refs_1_), channel_id=1, source_target_pairs={{0,4},{4,0},{1,5},{5,1},{2,6},{6,2},{3,7},{7,3},{8,12},{12,8},{9,1... | collective-permute-start | bytes 405512 | tf_op jit(solution)/shard_map/ppermute | solution.py:18
  24.1 5.0 %collective-permute-start.6 = (bf16[16,4096]{1,0:T(8,128)(2,1)S(1)}, bf16[16,4096]{1,0:T(8,128)(2,1)S(1)}, u32[]{:S(2)}, u32[]{:S(2)}) collective-permute-start(bf16[16,4096]{1,0:T(8,128)(2,1)S(1)} %pad_maximum_fusion), channel_id=1, source_target_pairs={{0,1},{1,0},{2,3},{3,2},{4,5},{5,4},{6,7},{7,6},{8,9},{9,8},{10,11... | collective-permute-start | bytes 393224 | tf_op jit(solution)/shard_map/ppermute | solution.py:18
  29.0 2.6 %collective-permute-start.7 = (bf16[16,4096]{1,0:T(8,128)(2,1)S(1)}, bf16[16,4096]{1,0:T(8,128)(2,1)S(1)}, u32[]{:S(2)}, u32[]{:S(2)}) collective-permute-start(bf16[16,4096]{1,0:T(8,128)(2,1)S(1)} %collective-permute-done.4.refs_2_), channel_id=1, source_target_pairs={{0,4},{4,0},{1,5},{5,1},{2,6},{6,2},{3,7},{7,3},{8,12},{12,8},{9,1... | collective-permute-start | bytes 393224 | tf_op jit(solution)/shard_map/ppermute | solution.py:18
  29.0 2.6 %collective-permute-start.8 = (bf16[16,4096]{1,0:T(8,128)(2,1)S(1)}, bf16[16,4096]{1,0:T(8,128)(2,1)S(1)}, u32[]{:S(2)}, u32[]{:S(2)}) collective-permute-start(bf16[16,4096]{1,0:T(8,128)(2,1)S(1)} %collective-permute-done.5.refs_3_), channel_id=1, source_target_pairs={{0,4},{4,0},{1,5},{5,1},{2,6},{6,2},{3,7},{7,3},{8,12},{12,8},{9,1... | collective-permute-start | bytes 393224 | tf_op jit(solution)/shard_map/ppermute | solution.py:18
  29.6 2.1 %collective-permute-start.9 = (bf16[16,4096]{1,0:T(8,128)(2,1)S(1)}, bf16[16,4096]{1,0:T(8,128)(2,1)S(1)}, u32[]{:S(2)}, u32[]{:S(2)}) collective-permute-start(bf16[16,4096]{1,0:T(8,128)(2,1)S(1)} %collective-permute-done.6.refs_4_), channel_id=1, source_target_pairs={{0,4},{4,0},{1,5},{5,1},{2,6},{6,2},{3,7},{7,3},{8,12},{12,8},{9,1... | collective-permute-start | bytes 393224 | tf_op jit(solution)/shard_map/ppermute | solution.py:18
